TPU v7x, 32 devices: a whole 2x2x4 slice. The times are simulated.
32 devices in a mesh: groups: 2 (over y), tm: 4 (over x, core), space: 4 (over z).
Axes of the slice: x: 2, y: 2, z: 4, core: 2. Of those that a mesh axis runs over, the one named last changes fastest.
Arguments:
- features: bfloat16 [8, 32, 128, 256], P(('groups', 'tm'), 'space'), parts along dimension 0, may hold values from -6 to 6
- pair_order: int32 [8], P(('groups', 'tm')), parts along dimension 0, may hold values 0 or 1
- flow_now: bfloat16 [8, 2, 32, 128], P(('groups', 'tm'), None, 'space'), parts along dimension 0, may hold values from -8 to 8
- targets: int32 [8, 2, 32, 128], P(('groups', 'tm'), None, 'space'), parts along dimension 0, may hold values from -4 to 4
- w_volume: bfloat16 [162, 128], replicated, may hold values from -0.5 to 0.5
- b_volume: float32 [128], replicated, may hold values from -3 to 3
- w_code: bfloat16 [3, 3, 128, 128], replicated, may hold values from -0.1875 to 0.1875
- b_code: float32 [128], replicated, may hold values from -3 to 3
- w_flow: bfloat16 [7, 7, 2, 128], replicated, may hold values from -0.625 to 0.625
- b_flow: float32 [128], replicated, may hold values from -3 to 3
- w_joint: bfloat16 [3, 3, 256, 128], replicated, may hold values from -0.125 to 0.125
- b_joint: float32 [128], replicated, may hold values from -3 to 3
- w_head: bfloat16 [128, 2], replicated, may hold values from -0.5 to 0.5
- b_head: float32 [2], replicated, may hold values from -3 to 3
Outputs:
- loss: float32 [2], P('groups'), parts along dimension 0
- flow_error: float32 [8, 2, 32, 128], P(('groups', 'tm'), None, 'space'), parts along dimension 0
- grad_w_volume: float32 [324, 128], P('groups'), parts along dimension 0
- grad_b_volume: float32 [256], P('groups'), parts along dimension 0
- grad_w_code: float32 [6, 3, 128, 128], P('groups'), parts along dimension 0
- grad_b_code: float32 [256], P('groups'), parts along dimension 0
- grad_w_flow: float32 [14, 7, 2, 128], P('groups'), parts along dimension 0
- grad_b_flow: float32 [256], P('groups'), parts along dimension 0
- grad_w_joint: float32 [6, 3, 256, 128], P('groups'), parts along dimension 0
- grad_b_joint: float32 [256], P('groups'), parts along dimension 0
- grad_w_head: float32 [256, 2], P('groups'), parts along dimension 0
- grad_b_head: float32 [4], P('groups'), parts along dimension 0
There are 2 independent parts, one for each index of `groups`. A program takes and returns all parts, laid end to end along the dimension named above; an argument that names none is the same for every part. Nothing has to cross between parts.
All inputs are finite; a program needn't handle non-finite values. No bound on the sum of `pair_order` on one device may be relied on, other than what follows from the above.
Results may differ from a plain program's by a relative error of at most 0.0032.
Values may be sent and summed in bfloat16 or wider, within the bound.
No kernel may reach another device: no remote copies, remote signals or barrier semaphores. Data moves between devices by JAX's collectives and lax.ppermute only.
A program may use at most 64 MiB of HBM per device.

v0:
```python
import jax
import jax.numpy as jnp
from jax import lax
from jax.sharding import PartitionSpec as P

RADIUS = 4


highest_precision = lax.Precision.HIGHEST


def extended_2(array, sides, width):
    for axis, dim in sides:
        devices, length = (lax.axis_size(axis), array.shape[dim])
        up = [(i, (i + 1) % devices) for i in range(devices - 1)]
        down = [(j, i) for i, j in up]
        last = lax.slice_in_dim(array, length - width, length, axis=dim)
        first = lax.slice_in_dim(array, 0, width, axis=dim)
        before = lax.ppermute(last, axis, up)
        after = lax.ppermute(first, axis, down)
        array = jnp.concatenate([before, array, after], axis=dim)
    return array


def shifted(block, axis, distance):
    devices = range(lax.axis_size(axis))
    route = [(i - distance, i) for i in devices if i - distance in devices]
    return lax.ppermute(block, axis, route)


def silu_slope(values):
    sigma = jax.nn.sigmoid(values)
    return sigma * (1.0 + values * (1.0 - sigma))


def correlate(own_tile, other_ext):
    n_rows = own_tile.shape[0]
    n_cols = own_tile.shape[1]
    n_chan = own_tile.shape[2]
    side = 2 * RADIUS + 1
    padded_other = jnp.pad(other_ext, ((0, 0), (RADIUS, RADIUS), (0, 0)))
    bands = []
    for row_off in range(side):
        window = padded_other[row_off : row_off + n_rows]
        scores = jnp.einsum("rxc,ryc->rxy", own_tile, window, preferred_element_type=jnp.float32)
        flat_scores = scores.reshape(n_rows, n_cols * (n_cols + 2 * RADIUS))
        flat_scores = jnp.pad(flat_scores, ((0, 0), (0, n_cols)))
        bands.append(flat_scores.reshape(n_rows, n_cols, n_cols + side)[:, :, :side])
    stacked = jnp.stack(bands, axis=2).reshape(n_rows, n_cols, side * side)
    return (stacked * n_chan ** (-0.5)).astype(jnp.bfloat16)


def column_stack(extended, ksize):
    half_k = ksize // 2
    n_cols = extended.shape[1]
    padded = jnp.pad(extended, ((0, 0), (half_k, half_k), (0, 0)))
    return jnp.concatenate([padded[:, j : j + n_cols] for j in range(ksize)], axis=-1)


def conv_tile(extended, weight):
    ksize = weight.shape[0]
    half_k = ksize // 2
    n_rows = extended.shape[0] - 2 * half_k
    n_cols = extended.shape[1]
    stacked = column_stack(extended, ksize)
    depth = stacked.shape[2]
    summed = jnp.zeros((n_rows * n_cols, weight.shape[3]), jnp.float32)
    for i in range(ksize):
        taken = stacked[i : i + n_rows].reshape(n_rows * n_cols, depth)
        summed = summed + jnp.dot(
            taken, weight[i].reshape(depth, weight.shape[3]), preferred_element_type=jnp.float32
        )
    return summed


def conv_tile_back(extended_slope, weight):
    ksize = weight.shape[0]
    half_k = ksize // 2
    n_rows = extended_slope.shape[0] - 2 * half_k
    n_cols = extended_slope.shape[1]
    stacked = column_stack(extended_slope, ksize)
    depth = stacked.shape[2]
    summed = jnp.zeros((n_rows * n_cols, weight.shape[2]), jnp.float32)
    for row_at in range(ksize):
        i = ksize - 1 - row_at
        taken = stacked[row_at : row_at + n_rows].reshape(n_rows * n_cols, depth)
        w_rows = jnp.concatenate([weight[i, ksize - 1 - col_at] for col_at in range(ksize)], axis=1)
        summed = summed + lax.dot_general(
            taken, w_rows, (((1,), (1,)), ((), ())), preferred_element_type=jnp.float32
        )
    return summed


def conv_tile_grad(extended, slope_flat, ksize):
    half_k = ksize // 2
    n_rows = extended.shape[0] - 2 * half_k
    n_cols = extended.shape[1]
    stacked = column_stack(extended, ksize)
    depth = stacked.shape[2]
    taps = []
    for i in range(ksize):
        taken = stacked[i : i + n_rows].reshape(n_rows * n_cols, depth)
        rows_grad = lax.dot_general(
            taken, slope_flat, (((0,), (0,)), ((), ())), preferred_element_type=jnp.float32
        )
        taps.append(rows_grad.reshape(ksize, extended.shape[2], slope_flat.shape[1]))
    return jnp.stack(taps, axis=0)


def local(
    features,
    pair_order,
    flow_now,
    targets,
    w_volume,
    b_volume,
    w_code,
    b_code,
    w_flow,
    b_flow,
    w_joint,
    b_joint,
    w_head,
    b_head,
):
    own_tile = features[0]
    n_rows = own_tile.shape[0]
    n_cols = own_tile.shape[1]
    n_pix = n_rows * n_cols
    n_code = w_code.shape[3]
    own_ext = extended_2(own_tile, (("space", 0),), RADIUS)
    next_ext = shifted(own_ext, "tm", -1)
    forward = correlate(own_tile, next_ext)
    prior_ext = shifted(own_ext, "tm", 1)
    backward = correlate(own_tile, prior_ext)
    swapped = pair_order[0] == 1
    first_half = jnp.where(swapped, backward, forward)
    second_half = jnp.where(swapped, forward, backward)
    volume = jnp.concatenate([first_half, second_half], axis=-1)
    volume_flat = volume.reshape(n_pix, volume.shape[2])
    code_pre = jnp.dot(volume_flat, w_volume, preferred_element_type=jnp.float32) + b_volume
    code = jax.nn.silu(code_pre).astype(jnp.bfloat16)
    code_ext = extended_2(code.reshape(n_rows, n_cols, n_code), (("space", 0),), 1)
    motion_pre = conv_tile(code_ext, w_code) + b_code
    motion = jax.nn.silu(motion_pre).astype(jnp.bfloat16)
    flow_ext = extended_2(flow_now[0], (("space", 1),), 3)
    padded_flow = jnp.pad(flow_ext, ((0, 0), (0, 0), (3, 3)))
    patch_list = []
    for i in range(7):
        for j in range(7):
            for comp in range(2):
                patch_list.append(padded_flow[comp, i : i + n_rows, j : j + n_cols].reshape(n_pix))
    patches = jnp.stack(patch_list, axis=0)
    flow_weight = w_flow.reshape(98, n_code)
    flow_pre = (
        lax.dot_general(
            patches, flow_weight, (((0,), (0,)), ((), ())), preferred_element_type=jnp.float32
        )
        + b_flow
    )
    flow_code = jax.nn.silu(flow_pre).astype(jnp.bfloat16)
    joint = jnp.concatenate([motion, flow_code], axis=-1)
    joint_ext = extended_2(joint.reshape(n_rows, n_cols, 2 * n_code), (("space", 0),), 1)
    hidden_pre = conv_tile(joint_ext, w_joint) + b_joint
    hidden = jax.nn.silu(hidden_pre).astype(jnp.bfloat16)
    pred = jnp.dot(hidden, w_head, preferred_element_type=jnp.float32) + b_head
    target_flat = targets[0].reshape(2, n_pix).T.astype(jnp.float32)
    error_flat = pred - target_flat
    flow_error = error_flat.T.reshape(1, 2, n_rows, n_cols)
    n_frames = lax.axis_size("tm")
    frame_at = lax.axis_index("tm").astype(jnp.float32)
    frame_weight = jnp.power(jnp.float32(0.25), (n_frames - 1 - frame_at) / (n_frames - 1))
    count = 2.0 * n_frames * n_rows * lax.axis_size("space") * n_cols
    loss_local = jnp.reshape(frame_weight * jnp.sum(error_flat * error_flat) / count, (1,))
    slope_pred = 2.0 * frame_weight * error_flat / count
    grad_w_head = jnp.dot(hidden.astype(jnp.float32).T, slope_pred, precision=highest_precision)
    grad_b_head = jnp.sum(slope_pred, axis=0)
    slope_hidden = (
        jnp.dot(slope_pred, w_head.astype(jnp.float32).T, precision=highest_precision)
        * silu_slope(hidden_pre)
    ).astype(jnp.bfloat16)
    grad_w_joint = conv_tile_grad(joint_ext, slope_hidden, 3)
    grad_b_joint = jnp.sum(slope_hidden.astype(jnp.float32), axis=0)
    slope_ext = extended_2(slope_hidden.reshape(n_rows, n_cols, n_code), (("space", 0),), 1)
    slope_joint = conv_tile_back(slope_ext, w_joint)
    slope_motion = (slope_joint[:, :n_code] * silu_slope(motion_pre)).astype(jnp.bfloat16)
    slope_flow = (slope_joint[:, n_code:] * silu_slope(flow_pre)).astype(jnp.bfloat16)
    grad_w_flow = jnp.dot(patches, slope_flow, preferred_element_type=jnp.float32).reshape(
        7, 7, 2, n_code
    )
    grad_b_flow = jnp.sum(slope_flow.astype(jnp.float32), axis=0)
    grad_w_code = conv_tile_grad(code_ext, slope_motion, 3)
    grad_b_code = jnp.sum(slope_motion.astype(jnp.float32), axis=0)
    motion_ext = extended_2(slope_motion.reshape(n_rows, n_cols, n_code), (("space", 0),), 1)
    slope_code = (conv_tile_back(motion_ext, w_code) * silu_slope(code_pre)).astype(jnp.bfloat16)
    grad_w_volume = lax.dot_general(
        volume_flat, slope_code, (((0,), (0,)), ((), ())), preferred_element_type=jnp.float32
    )
    grad_b_volume = jnp.sum(slope_code.astype(jnp.float32), axis=0)
    (
        loss_local,
        grad_w_volume,
        grad_b_volume,
        grad_w_code,
        grad_b_code,
        grad_w_flow,
        grad_b_flow,
        grad_w_joint,
        grad_b_joint,
        grad_w_head,
        grad_b_head,
    ) = lax.psum(
        (
            loss_local,
            grad_w_volume,
            grad_b_volume,
            grad_w_code,
            grad_b_code,
            grad_w_flow,
            grad_b_flow,
            grad_w_joint,
            grad_b_joint,
            grad_w_head,
            grad_b_head,
        ),
        ("tm", "space"),
    )
    return (
        loss_local,
        flow_error,
        grad_w_volume,
        grad_b_volume,
        grad_w_code,
        grad_b_code,
        grad_w_flow,
        grad_b_flow,
        grad_w_joint,
        grad_b_joint,
        grad_w_head,
        grad_b_head,
    )


def solution(mesh):
    placed = (
        P(("groups", "tm"), "space", None, None),
        P(("groups", "tm")),
        P(("groups", "tm"), None, "space", None),
        P(("groups", "tm"), None, "space", None),
        P(),
        P(),
        P(),
        P(),
        P(),
        P(),
        P(),
        P(),
        P(),
        P(),
    )
    return jax.shard_map(
        local,
        mesh=mesh,
        in_specs=placed,
        out_specs=(
            P("groups"),
            P(("groups", "tm"), None, "space", None),
            P("groups", None),
            P("groups"),
            P("groups", None, None, None),
            P("groups"),
            P("groups", None, None, None),
            P("groups"),
            P("groups", None, None, None),
            P("groups"),
            P("groups", None),
            P("groups"),
        ),
        check_vma=False,
    )
```

profile of v0, /device:TPU:0, one launch (start us, length us, event | category | flops | bytes accessed | tf_op | source)
XLA Modules:
  0.0 301.7 jit_solution(11512304857704696042)
XLA Ops:
  8.4 4.9 %collective-permute-start = (bf16[4,128,256]{2,1,0:T(8,128)(2,1)S(1)}, bf16[4,128,256]{2,1,0:T(8,128)(2,1)S(1)}, u32[]{:S(2)}, u32[]{:S(2)}) collective-permute-start(bf16[4,128,256]{2,1,0:T(8,128)(2,1)S(1)} %get-tuple-element.61), channel_id=1, source_target_pairs={{0,1},{1,2},{2,3},{4,5},{5,6},{6,7},{8,9},{9,10},{10,11},{12,13},{... | collective-permute-start | bytes 786440 | tf_op jit(solution)/shard_map/ppermute | solution.py:19
  15.4 4.5 %collective-permute-start.6 = (bf16[2,3,128]{2,1,0:T(4,128)(2,1)S(1)}, bf16[2,3,128]{2,1,0:T(4,128)(2,1)S(1)}, u32[]{:S(2)}, u32[]{:S(2)}) collective-permute-start(bf16[2,3,128]{2,1,0:T(4,128)(2,1)S(1)} %get-tuple-element.186), channel_id=1, source_target_pairs={{0,1},{1,2},{2,3},{4,5},{5,6},{6,7},{8,9},{9,10},{10,11},{12,13},{... | collective-permute-start | bytes 4616 | tf_op jit(solution)/shard_map/ppermute | solution.py:19
  22.0 2.0 fusion.158
  32.2 4.2 %collective-permute-start.2 = (bf16[16,128,256]{2,1,0:T(8,128)(2,1)}, bf16[16,128,256]{2,1,0:T(8,128)(2,1)}, u32[]{:S(2)}, u32[]{:S(2)}) collective-permute-start(bf16[16,128,256]{2,1,0:T(8,128)(2,1)} %pad_maximum_fusion.2), channel_id=1, source_target_pairs={{0,4},{4,8},{8,12},{1,5},{5,9},{9,13},{2,6},{6,10},{10,14},{3,7},{... | collective-permute-start | bytes 3145736 | tf_op jit(solution)/shard_map/ppermute | solution.py:28
  55.9 1.8 convolution_bitcast_fusion.3
  114.4 4.5 %collective-permute-start.4 = (bf16[1,128,128]{2,1,0:T(8,128)(2,1)S(1)}, bf16[1,128,128]{2,1,0:T(8,128)(2,1)S(1)}, u32[]{:S(2)}, u32[]{:S(2)}) collective-permute-start(bf16[1,128,128]{2,1,0:T(8,128)(2,1)S(1)} %get-tuple-element.85), channel_id=1, source_target_pairs={{0,1},{1,2},{2,3},{4,5},{5,6},{6,7},{8,9},{9,10},{10,11},{12,13},{... | collective-permute-start | bytes 98312 | tf_op jit(solution)/shard_map/ppermute | solution.py:19
  121.3 3.4 %collective-permute-done.5 = bf16[1,128,128]{2,1,0:T(8,128)(2,1)S(1)} collective-permute-done((bf16[1,128,128]{2,1,0:T(8,128)(2,1)S(1)}, bf16[1,128,128]{2,1,0:T(8,128)(2,1)S(1)}, u32[]{:S(2)}, u32[]{:S(2)}) %collective-permute-start.5) | collective-permute-done | bytes 32800 | tf_op jit(solution)/shard_map/ppermute | solution.py:20
  132.0 3.5 %collective-permute-start.8 = (bf16[1,128,256]{2,1,0:T(8,128)(2,1)S(1)}, bf16[1,128,256]{2,1,0:T(8,128)(2,1)S(1)}, u32[]{:S(2)}, u32[]{:S(2)}) collective-permute-start(bf16[1,128,256]{2,1,0:T(8,128)(2,1)S(1)} %get-tuple-element.59), channel_id=1, source_target_pairs={{0,1},{1,2},{2,3},{4,5},{5,6},{6,7},{8,9},{9,10},{10,11},{12,13},{... | collective-permute-start | bytes 196616 | tf_op jit(solution)/shard_map/ppermute | solution.py:19
  135.5 1.5 collective-permute-start.9
  137.4 4.3 %collective-permute-done.9 = bf16[1,128,256]{2,1,0:T(8,128)(2,1)S(1)} collective-permute-done((bf16[1,128,256]{2,1,0:T(8,128)(2,1)S(1)}, bf16[1,128,256]{2,1,0:T(8,128)(2,1)S(1)}, u32[]{:S(2)}, u32[]{:S(2)}) %collective-permute-start.9) | collective-permute-done | bytes 65568 | tf_op jit(solution)/shard_map/ppermute | solution.py:20
  142.2 1.7 fusion.153
  143.9 1.6 copy.98
  145.5 2.4 fusion.165
  148.7 2.3 fusion.166
  151.0 1.7 copy.97
  152.7 2.4 multiply_convert_fusion
  159.1 3.5 %collective-permute-start.10 = (bf16[1,128,128]{2,1,0:T(8,128)(2,1)S(1)}, bf16[1,128,128]{2,1,0:T(8,128)(2,1)S(1)}, u32[]{:S(2)}, u32[]{:S(2)}) collective-permute-start(bf16[1,128,128]{2,1,0:T(8,128)(2,1)S(1)} %get-tuple-element.83), channel_id=1, source_target_pairs={{0,1},{1,2},{2,3},{4,5},{5,6},{6,7},{8,9},{9,10},{10,11},{12,13},{... | collective-permute-start | bytes 98312 | tf_op jit(solution)/shard_map/ppermute | solution.py:19
  165.0 3.4 %collective-permute-done.11 = bf16[1,128,128]{2,1,0:T(8,128)(2,1)S(1)} collective-permute-done((bf16[1,128,128]{2,1,0:T(8,128)(2,1)S(1)}, bf16[1,128,128]{2,1,0:T(8,128)(2,1)S(1)}, u32[]{:S(2)}, u32[]{:S(2)}) %collective-permute-start.11) | collective-permute-done | bytes 32800 | tf_op jit(solution)/shard_map/ppermute | solution.py:20
  174.0 1.9 collective-permute-start.12
  178.1 3.6 %collective-permute-done.13 = bf16[1,128,128]{2,1,0:T(8,128)(2,1)S(1)} collective-permute-done((bf16[1,128,128]{2,1,0:T(8,128)(2,1)S(1)}, bf16[1,128,128]{2,1,0:T(8,128)(2,1)S(1)}, u32[]{:S(2)}, u32[]{:S(2)}) %collective-permute-start.13) | collective-permute-done | bytes 32800 | tf_op jit(solution)/shard_map/ppermute | solution.py:20
  187.7 62.3 %all-reduce.25 = (f32[1]{0:T(128)}, f32[128]{0:T(128)}, f32[128]{0:T(128)}, f32[7,7,2,128]{3,2,1,0:T(2,128)}, f32[128]{0:T(128)}, /*index=5*/f32[128]{0:T(128)}, f32[128,2]{0,1:T(2,128)}, f32[2]{0:T(128)}) all-reduce(f32[1]{0:T(128)} %bitcast.60, ...), channel_id=1, replica_groups=mesh['groups'=2,'tm'=4,'space'=4] {'tm','space'}, use_global_device_ids=true, to_apply=%region_1.2 | all-reduce | flops 13315 | bytes 106520 | tf_op jit(solution)/shard_map/psum | solution.py:212
  250.0 39.9 %all-reduce.29.cloned.1.call-done = (f32[162,128]{1,0:T(8,128)}, f32[3,3,128,128]{3,2,1,0:T(8,128)}, f32[3,3,256,128]{3,2,1,0:T(8,128)}) async-done(((f32[162,128]{1,0:T(8,128)}, f32[3,3,128,128]{3,2,1,0:T(8,128)}, f32[3,3,256,128]{3,2,1,0:T(8,128)}), (f32[162,128]{1,0:T(8,128)}, f32[3,3,128,128]{3,2,1,0:T(8,128)}, f32[3,3,256,128]{3,2,1,0:T(8,128)})) %all-reduce.29.cloned.1.call-update) | async-done | bytes 1852432 | tf_op jit(solution)/shard_map/psum | solution.py:212
  289.9 1.6 copy.329
  291.5 1.9 copy.330
  (405 shorter events, 118.6 us)
Async XLA Ops:
  7.2 105.9 %copy-start = (bf16[162,128]{1,0:T(8,128)(2,1)S(1)}, bf16[162,128]{1,0:T(8,128)(2,1)}, u32[]{:S(2)}) copy-start(bf16[162,128]{1,0:T(8,128)(2,1)} %param.18) | copy-start | bytes 124420
  7.2 16.8 %copy-start.5 = (bf16[3,3,256,128]{3,2,1,0:T(8,128)(2,1)S(1)}, bf16[3,3,256,128]{3,2,1,0:T(8,128)(2,1)}, u32[]{:S(2)}) copy-start(bf16[3,3,256,128]{3,2,1,0:T(8,128)(2,1)} %param.24) | copy-start | bytes 1769476
  7.2 17.6 %copy-start.8 = (bf16[3,3,128,128]{3,2,1,0:T(8,128)(2,1)S(1)}, bf16[3,3,128,128]{3,2,1,0:T(8,128)(2,1)}, u32[]{:S(2)}) copy-start(bf16[3,3,128,128]{3,2,1,0:T(8,128)(2,1)} %param.20) | copy-start | bytes 884740
  7.2 282.6 %all-reduce.29.cloned.1.call-start = ((), (), s32[]{:S(2)}) async-start(), calls=%async_computation | async-start | bytes 3710976 | tf_op jit(solution)/shard_map/psum | solution.py:212
  8.4 20.4 %collective-permute-start = (bf16[4,128,256]{2,1,0:T(8,128)(2,1)S(1)}, bf16[4,128,256]{2,1,0:T(8,128)(2,1)S(1)}, u32[]{:S(2)}, u32[]{:S(2)}) collective-permute-start(bf16[4,128,256]{2,1,0:T(8,128)(2,1)S(1)} %get-tuple-element.61), channel_id=1, source_target_pairs={{0,1},{1,2},{2,3},{4,5},{5,6},{6,7},{8,9},{9,10},{10,11},{12,13},{... | collective-permute-start | bytes 786440 | tf_op jit(solution)/shard_map/ppermute | solution.py:19
  13.4 15.5 %collective-permute-start.1 = (bf16[4,128,256]{2,1,0:T(8,128)(2,1)S(1)}, bf16[4,128,256]{2,1,0:T(8,128)(2,1)S(1)}, u32[]{:S(2)}, u32[]{:S(2)}) collective-permute-start(bf16[4,128,256]{2,1,0:T(8,128)(2,1)S(1)} %get-tuple-element.62), channel_id=1, source_target_pairs={{1,0},{2,1},{3,2},{5,4},{6,5},{7,6},{9,8},{10,9},{11,10},{13,12},{... | collective-permute-start | bytes 786440 | tf_op jit(solution)/shard_map/ppermute | solution.py:20
  15.4 12.1 %collective-permute-start.6 = (bf16[2,3,128]{2,1,0:T(4,128)(2,1)S(1)}, bf16[2,3,128]{2,1,0:T(4,128)(2,1)S(1)}, u32[]{:S(2)}, u32[]{:S(2)}) collective-permute-start(bf16[2,3,128]{2,1,0:T(4,128)(2,1)S(1)} %get-tuple-element.186), channel_id=1, source_target_pairs={{0,1},{1,2},{2,3},{4,5},{5,6},{6,7},{8,9},{9,10},{10,11},{12,13},{... | collective-permute-start | bytes 4616 | tf_op jit(solution)/shard_map/ppermute | solution.py:19
  20.0 7.6 %collective-permute-start.7 = (bf16[2,3,128]{2,1,0:T(4,128)(2,1)S(1)}, bf16[2,3,128]{2,1,0:T(4,128)(2,1)S(1)}, u32[]{:S(2)}, u32[]{:S(2)}) collective-permute-start(bf16[2,3,128]{2,1,0:T(4,128)(2,1)S(1)} %get-tuple-element.187), channel_id=1, source_target_pairs={{1,0},{2,1},{3,2},{5,4},{6,5},{7,6},{9,8},{10,9},{11,10},{13,12},{... | collective-permute-start | bytes 4616 | tf_op jit(solution)/shard_map/ppermute | solution.py:20
  22.0 4.2 %copy-start.51 = (s32[1,2,8,128]{3,2,1,0:T(8,128)S(1)}, s32[1,2,8,128]{3,2,1,0:T(8,128)}, u32[]{:S(2)}) copy-start(s32[1,2,8,128]{3,2,1,0:T(8,128)} %param.17) | copy-start | bytes 24580
  22.0 4.9 %copy-start.50 = (bf16[7,7,2,128]{3,2,1,0:T(2,128)(2,1)S(1)}, bf16[7,7,2,128]{3,2,1,0:T(2,128)(2,1)}, u32[]{:S(2)}) copy-start(bf16[7,7,2,128]{3,2,1,0:T(2,128)(2,1)} %param.22) | copy-start | bytes 75268
  22.0 5.6 %copy-start.44 = (bf16[1,2,8,128]{3,2,1,0:T(8,128)(2,1)S(1)}, bf16[1,2,8,128]{3,2,1,0:T(8,128)(2,1)}, u32[]{:S(2)}) copy-start(bf16[1,2,8,128]{3,2,1,0:T(8,128)(2,1)} %param.16) | copy-start | bytes 12292
  24.0 4.9 %copy-start.6 = (bf16[1,8,128,256]{3,2,1,0:T(8,128)(2,1)S(1)}, bf16[1,8,128,256]{3,2,1,0:T(8,128)(2,1)}, u32[]{:S(2)}) copy-start(bf16[1,8,128,256]{3,2,1,0:T(8,128)(2,1)} %param.14) | copy-start | bytes 1572868
  29.9 6.5 %collective-permute-start.3 = (bf16[16,128,256]{2,1,0:T(8,128)(2,1)}, bf16[16,128,256]{2,1,0:T(8,128)(2,1)S(1)}, u32[]{:S(2)}, u32[]{:S(2)}) collective-permute-start(bf16[16,128,256]{2,1,0:T(8,128)(2,1)} %pad_maximum_fusion.2), channel_id=1, source_target_pairs={{4,0},{8,4},{12,8},{5,1},{9,5},{13,9},{6,2},{10,6},{14,10},{7,3},{... | collective-permute-start | bytes 3145736 | tf_op jit(solution)/shard_map/ppermute | solution.py:28
  32.2 37.7 %collective-permute-start.2 = (bf16[16,128,256]{2,1,0:T(8,128)(2,1)}, bf16[16,128,256]{2,1,0:T(8,128)(2,1)}, u32[]{:S(2)}, u32[]{:S(2)}) collective-permute-start(bf16[16,128,256]{2,1,0:T(8,128)(2,1)} %pad_maximum_fusion.2), channel_id=1, source_target_pairs={{0,4},{4,8},{8,12},{1,5},{5,9},{9,13},{2,6},{6,10},{10,14},{3,7},{... | collective-permute-start | bytes 3145736 | tf_op jit(solution)/shard_map/ppermute | solution.py:28
  113.1 7.1 %copy-start.49 = (bf16[98,128]{1,0:T(8,128)(2,1)S(1)}, bf16[98,128]{1,0:T(8,128)(2,1)}, u32[]{:S(2)}) copy-start(bf16[98,128]{1,0:T(8,128)(2,1)} %reshape.316) | copy-start | bytes 75268
  113.1 7.1 %copy-start.54 = (f32[128]{0:T(128)S(1)}, f32[128]{0:T(128)}, u32[]{:S(2)}) copy-start(f32[128]{0:T(128)} %param.23) | copy-start | bytes 1540
  114.4 7.0 %collective-permute-start.4 = (bf16[1,128,128]{2,1,0:T(8,128)(2,1)S(1)}, bf16[1,128,128]{2,1,0:T(8,128)(2,1)S(1)}, u32[]{:S(2)}, u32[]{:S(2)}) collective-permute-start(bf16[1,128,128]{2,1,0:T(8,128)(2,1)S(1)} %get-tuple-element.85), channel_id=1, source_target_pairs={{0,1},{1,2},{2,3},{4,5},{5,6},{6,7},{8,9},{9,10},{10,11},{12,13},{... | collective-permute-start | bytes 98312 | tf_op jit(solution)/shard_map/ppermute | solution.py:19
  118.9 5.8 %collective-permute-start.5 = (bf16[1,128,128]{2,1,0:T(8,128)(2,1)S(1)}, bf16[1,128,128]{2,1,0:T(8,128)(2,1)S(1)}, u32[]{:S(2)}, u32[]{:S(2)}) collective-permute-start(bf16[1,128,128]{2,1,0:T(8,128)(2,1)S(1)} %get-tuple-element.86), channel_id=1, source_target_pairs={{1,0},{2,1},{3,2},{5,4},{6,5},{7,6},{9,8},{10,9},{11,10},{13,12},{... | collective-permute-start | bytes 98312 | tf_op jit(solution)/shard_map/ppermute | solution.py:20
  132.0 5.4 %collective-permute-start.8 = (bf16[1,128,256]{2,1,0:T(8,128)(2,1)S(1)}, bf16[1,128,256]{2,1,0:T(8,128)(2,1)S(1)}, u32[]{:S(2)}, u32[]{:S(2)}) collective-permute-start(bf16[1,128,256]{2,1,0:T(8,128)(2,1)S(1)} %get-tuple-element.59), channel_id=1, source_target_pairs={{0,1},{1,2},{2,3},{4,5},{5,6},{6,7},{8,9},{9,10},{10,11},{12,13},{... | collective-permute-start | bytes 196616 | tf_op jit(solution)/shard_map/ppermute | solution.py:19
  135.5 6.2 %collective-permute-start.9 = (bf16[1,128,256]{2,1,0:T(8,128)(2,1)S(1)}, bf16[1,128,256]{2,1,0:T(8,128)(2,1)S(1)}, u32[]{:S(2)}, u32[]{:S(2)}) collective-permute-start(bf16[1,128,256]{2,1,0:T(8,128)(2,1)S(1)} %get-tuple-element.60), channel_id=1, source_target_pairs={{1,0},{2,1},{3,2},{5,4},{6,5},{7,6},{9,8},{10,9},{11,10},{13,12},{... | collective-permute-start | bytes 196616 | tf_op jit(solution)/shard_map/ppermute | solution.py:20
  159.1 5.9 %collective-permute-start.10 = (bf16[1,128,128]{2,1,0:T(8,128)(2,1)S(1)}, bf16[1,128,128]{2,1,0:T(8,128)(2,1)S(1)}, u32[]{:S(2)}, u32[]{:S(2)}) collective-permute-start(bf16[1,128,128]{2,1,0:T(8,128)(2,1)S(1)} %get-tuple-element.83), channel_id=1, source_target_pairs={{0,1},{1,2},{2,3},{4,5},{5,6},{6,7},{8,9},{9,10},{10,11},{12,13},{... | collective-permute-start | bytes 98312 | tf_op jit(solution)/shard_map/ppermute | solution.py:19
  162.6 5.8 %collective-permute-start.11 = (bf16[1,128,128]{2,1,0:T(8,128)(2,1)S(1)}, bf16[1,128,128]{2,1,0:T(8,128)(2,1)S(1)}, u32[]{:S(2)}, u32[]{:S(2)}) collective-permute-start(bf16[1,128,128]{2,1,0:T(8,128)(2,1)S(1)} %get-tuple-element.84), channel_id=1, source_target_pairs={{1,0},{2,1},{3,2},{5,4},{6,5},{7,6},{9,8},{10,9},{11,10},{13,12},{... | collective-permute-start | bytes 98312 | tf_op jit(solution)/shard_map/ppermute | solution.py:20
  174.0 4.1 %collective-permute-start.12 = (bf16[1,128,128]{2,1,0:T(8,128)(2,1)S(1)}, bf16[1,128,128]{2,1,0:T(8,128)(2,1)S(1)}, u32[]{:S(2)}, u32[]{:S(2)}) collective-permute-start(bf16[1,128,128]{2,1,0:T(8,128)(2,1)S(1)} %get-tuple-element.81), channel_id=1, source_target_pairs={{0,1},{1,2},{2,3},{4,5},{5,6},{6,7},{8,9},{9,10},{10,11},{12,13},{... | collective-permute-start | bytes 98312 | tf_op jit(solution)/shard_map/ppermute | solution.py:19
  176.0 5.8 %collective-permute-start.13 = (bf16[1,128,128]{2,1,0:T(8,128)(2,1)S(1)}, bf16[1,128,128]{2,1,0:T(8,128)(2,1)S(1)}, u32[]{:S(2)}, u32[]{:S(2)}) collective-permute-start(bf16[1,128,128]{2,1,0:T(8,128)(2,1)S(1)} %get-tuple-element.82), channel_id=1, source_target_pairs={{1,0},{2,1},{3,2},{5,4},{6,5},{7,6},{9,8},{10,9},{11,10},{13,12},{... | collective-permute-start | bytes 98312 | tf_op jit(solution)/shard_map/ppermute | solution.py:20
  (51 other events, 63.6 us)
Sparse Core Ops, SparseCore 0:
  186.1 103.6 all-reduce.28
where the time goes:
time: 306 us; the launch traced here: 302 us
  local copies, waits for them, and re-layouts  80 us (26%)
  blocking collectives  62.3 us (20%)
  waiting for transfers between devices  54.9 us (18%)
  matrix products  45.1 us (15%)
  starting transfers between devices  36.4 us (12%)
  between operations  18.2 us (6%)
  other arithmetic  4.82 us (2%)
    psum x1, blocking collectives, local(): lax.psum((loss_local, grad_w_volume, grad_b_volume, grad_w_code, grad_b_c...  62.3 us
    psum x1, waiting for transfers between devices, local(): lax.psum((loss_local, grad_w_volume, grad_b_volume, grad_w_code, grad_b_c...  39.9 us
    dot_general x18, matrix products, correlate(): jnp.einsum('rxc,ryc->rxy', own_tile, window, preferred_element_type=jnp.f...  24.8 us
    ppermute x6, starting transfers between devices, extended_2(): before = lax.ppermute(last, axis, up)  22.9 us
    reshape x18, local copies, waits for them, and re-layouts, correlate(): flat_scores.reshape(n_rows, n_cols, n_cols + side)[:, :, :side]  20.9 us
    ppermute x6, waiting for transfers between devices, extended_2(): after = lax.ppermute(first, axis, down)  14.7 us
    unnamed x150, local copies, waits for them, and re-layouts  12.4 us
    another operation x37, local copies, waits for them, and re-layouts, correlate(): stacked = jnp.stack(bands, axis=2).reshape(n_rows, n_cols, side * side)  10.8 us
  transfers between devices with their start and end apart: 15, of which 6 were waited for; matrix products, arithmetic and copies ran while one was open for 15% of the time, Pallas kernels for 0%

commit v1 on v0

v1 whole, which is shorter than its diff:
```python
import functools

import jax
import jax.numpy as jnp
from jax import lax
from jax.experimental import pallas as pl
from jax.experimental.pallas import tpu as pltpu
from jax.sharding import PartitionSpec as P

RADIUS = 4
SIDE = 2 * RADIUS + 1
OFF = SIDE * SIDE
HALO = 4
FLOW_HALO = 6
TARGET_HALO = 2
BF = jnp.bfloat16
F32 = jnp.float32
NT = (((1,), (1,)), ((), ()))
TN = (((0,), (0,)), ((), ()))

AT_CODE = 2304
AT_VOLUME = 3456
AT_FLOW = 3632
AT_MISC = 3744
GRAD_ROWS = 3840


def dot(a, b):
    return jnp.dot(a, b, preferred_element_type=F32)


def rows(start, count, unit):
    return pl.ds(pl.multiple_of(start * unit, unit), count * unit)


def split3(s):
    hi = s.astype(BF)
    rest = s - hi.astype(F32)
    mid = rest.astype(BF)
    return jnp.concatenate([hi, mid, (rest - mid.astype(F32)).astype(BF)], axis=0)


def silu_pair(v):
    s = jax.nn.sigmoid(v)
    return v * s, s * (1.0 + v * (1.0 - s))


def correlate_kernel(
    n_rows, n_cols,
    swap_ref, own_hbm, mid_n, top_n, bot_n, mid_p, top_p, bot_p,
    wv_ref, bias_ref, up_x, dn_x,
    vol_ref, code_ref, up_ref, dn_ref,
    own, near, sems,
):
    n_chan = own.shape[1]
    swap = swap_ref[0]
    halo = RADIUS * n_cols
    body = n_rows * n_cols
    copies = [pltpu.make_async_copy(own_hbm, own, sems.at[0])]
    for at, (slot, parts) in enumerate(((swap, (mid_n, top_n, bot_n)), (1 - swap, (mid_p, top_p, bot_p)))):
        mid, top, bot = parts
        copies.append(pltpu.make_async_copy(mid, near.at[slot, pl.ds(halo, body)], sems.at[3 * at + 1]))
        copies.append(pltpu.make_async_copy(top, near.at[slot, pl.ds(0, halo)], sems.at[3 * at + 2]))
        copies.append(pltpu.make_async_copy(bot, near.at[slot, pl.ds(halo + body, halo)], sems.at[3 * at + 3]))
    for copy in copies:
        copy.start()
    for copy in copies:
        copy.wait()
    x_at = lax.broadcasted_iota(jnp.int32, (n_cols, n_cols), 0)
    y_at = lax.broadcasted_iota(jnp.int32, (n_cols, n_cols), 1)
    band = jnp.abs(x_at - y_at) <= RADIUS
    scale = n_chan ** (-0.5)

    def one_row(r, carry):
        tile = own[rows(r, 1, n_cols), :]
        for half in range(2):
            scores = lax.dot_general(
                tile, near[half, rows(r, SIDE, n_cols), :], NT, preferred_element_type=F32
            )
            total = [jnp.zeros((8, n_cols), F32) for _ in range(n_cols // 8)]
            for off in range(SIDE):
                part = jnp.where(band, scores[:, off * n_cols : (off + 1) * n_cols], 0.0)
                for g in range(n_cols // 8):
                    shift = (off * SIDE + RADIUS - 8 * g) % n_cols
                    piece = part[8 * g : 8 * g + 8]
                    total[g] = total[g] + (pltpu.roll(piece, shift, 1) if shift else piece)
            full = jnp.concatenate(total, axis=0)
            for bit in (1, 2, 4):
                full = jnp.where((x_at & bit) != 0, pltpu.roll(full, n_cols - bit, 1), full)
            vol_ref[rows(r, 1, n_cols), half * n_cols : (half + 1) * n_cols] = (full * scale).astype(BF)
        return carry

    lax.fori_loop(0, n_rows, one_row, 0)

    def one_code(r, carry):
        pre = dot(vol_ref[rows(r, 2, n_cols), :], wv_ref[...]) + bias_ref[0:1, :]
        code_ref[rows(r, 2, n_cols), :] = (pre * jax.nn.sigmoid(pre)).astype(BF)
        return carry

    lax.fori_loop(0, n_rows // 2, lambda b, c: one_code(2 * b, c), 0)
    up_ref[0:halo, :] = code_ref[0:halo, :]
    up_ref[halo : halo + 16, :] = up_x[...]
    dn_ref[0:halo, :] = code_ref[body - halo : body, :]
    dn_ref[halo : halo + 16, :] = dn_x[...]


def train_kernel(
    n_rows, n_cols,
    ints, floats, vol, code, top, bot, flow, targets,
    wv, wc, wcb, wj, wjb, wf, wht, bias,
    error_out, grads,
    c3, j3, d_motion, d_flow, s3, m3, xf, xx, xb, err, tgt, hid, s_flow, s_code, jt, acc, g_head,
):
    W = n_cols
    C = wc.shape[2]
    body = n_rows * W
    halo = HALO * W
    row0 = ints[0]
    height = ints[1]
    x_at = lax.broadcasted_iota(jnp.int32, (W, C), 0)
    first = x_at == 0
    last = x_at == W - 1

    def inside(ext):
        at = row0 + ext
        return jnp.logical_and(at >= 0, at < height)

    def stack(ref, at, v, cols):
        left = jnp.where(first, 0.0, pltpu.roll(v, 1, 0))
        right = jnp.where(last, 0.0, pltpu.roll(v, W - 1, 0))
        for col, part in zip(cols, (left, v, right)):
            ref[rows(at, 1, W), col : col + C] = part.astype(BF)

    acc[...] = jnp.zeros_like(acc)
    g_head[...] = jnp.zeros_like(g_head)

    def add_rows(k, v):
        acc[8 * k : 8 * k + 8, :] += jnp.sum(v.reshape(v.shape[0] // 8, 8, C), axis=0)

    fwd = (0, C, 2 * C)
    bwd = (2 * C, C, 0)

    def load_halo(y, carry):
        stack(c3, y, top[rows(y, 1, W), :].astype(F32), fwd)
        stack(c3, y + HALO + n_rows, bot[rows(y, 1, W), :].astype(F32), fwd)
        return carry

    def load_code(y, carry):
        stack(c3, y + HALO, code[rows(y, 1, W), :].astype(F32), fwd)
        return carry

    lax.fori_loop(0, HALO, load_halo, 0)
    lax.fori_loop(0, n_rows, load_code, 0)

    xx[...] = jnp.zeros_like(xx)
    above = top[halo : halo + 16, :].astype(F32)
    below = bot[halo : halo + 16, :].astype(F32)
    n_flow = n_rows + 2 * FLOW_HALO
    lane = lax.broadcasted_iota(jnp.int32, (n_flow, W), 1)
    for k in range(2):
        xf[0:FLOW_HALO, :] = above[8 * k : 8 * k + FLOW_HALO, :]
        xf[FLOW_HALO : FLOW_HALO + n_rows, :] = flow[k].astype(F32)
        xf[FLOW_HALO + n_rows : n_flow, :] = below[8 * k : 8 * k + FLOW_HALO, :]
        own_flow = xf[0:n_flow, :]
        for j in range(7):
            shift = (3 - j) % W
            moved = pltpu.roll(own_flow, shift, 1) if shift else own_flow
            ok = jnp.logical_and(lane + (j - 3) >= 0, lane + (j - 3) < W)
            xx[pl.ds(j * 2 + k, n_flow, stride=16), :] = jnp.where(ok, moved, 0.0)
    xb[...] = xx[...].astype(BF)

    tgt[...] = jnp.zeros_like(tgt)
    for k in range(2):
        for y in range(TARGET_HALO):
            tgt[k : k + 1, y * W : (y + 1) * W] = above[8 * k + 6 + y : 8 * k + 7 + y, :]
            lo = (TARGET_HALO + n_rows + y) * W
            tgt[k : k + 1, lo : lo + W] = below[8 * k + 6 + y : 8 * k + 7 + y, :]
        for y in range(n_rows):
            lo = (TARGET_HALO + y) * W
            tgt[k : k + 1, lo : lo + W] = targets[k, y : y + 1, :].astype(F32)

    def joint_rows(b, carry):
        y = 2 * b
        pre = bias[1:2, :] + dot(c3[rows(y, 2, W), :], wc[0])
        pre = pre + dot(c3[rows(y + 1, 2, W), :], wc[1])
        pre = pre + dot(c3[rows(y + 2, 2, W), :], wc[2])
        for u in range(2):
            value, slope = silu_pair(pre[u * W : (u + 1) * W])
            d_motion[rows(y + u, 1, W), :] = slope
            ok = inside(y + u - 3)
            stack(j3, y + u, jnp.where(ok, value, 0.0), (0, 2 * C, 4 * C))
            patch = xb[pl.ds(pl.multiple_of((y + u) * 16, 16), 112), :]
            f_pre = lax.dot_general(patch, wf[...], TN, preferred_element_type=F32) + bias[2:3, :]
            value, slope = silu_pair(f_pre)
            d_flow[rows(y + u, 1, W), :] = slope
            stack(j3, y + u, jnp.where(ok, value, 0.0), (C, 3 * C, 5 * C))
        return carry

    lax.fori_loop(0, (n_rows + 6) // 2, joint_rows, 0)

    k_row = lax.broadcasted_iota(jnp.int32, (16, 2 * W), 0)
    b_head = jnp.where(k_row == 0, floats[2], jnp.where(k_row == 1, floats[3], 0.0))

    def hidden_rows(b, carry):
        y = 2 * b
        pre = bias[3:4, :] + dot(j3[rows(y, 2, W), :], wj[0])
        pre = pre + dot(j3[rows(y + 1, 2, W), :], wj[1])
        pre = pre + dot(j3[rows(y + 2, 2, W), :], wj[2])
        value, slope = silu_pair(pre)
        hidden = value.astype(BF)
        hid[rows(y, 2, W), :] = hidden
        pred = lax.dot_general(wht[0:16, :], hidden, NT, preferred_element_type=F32)
        error = pred + b_head - tgt[:, rows(y, 2, W)]
        err[:, rows(y, 2, W)] = error
        back = lax.dot_general(split3(error * floats[0]), wht[...], TN, preferred_element_type=F32) * slope
        for u in range(2):
            v = jnp.where(inside(y + u - 2), back[u * W : (u + 1) * W], 0.0)
            stack(s3, y + u, v, bwd)
        return carry

    lax.fori_loop(0, (n_rows + 4) // 2, hidden_rows, 0)

    own = err[:, TARGET_HALO * W : TARGET_HALO * W + body]
    for k in range(2):
        for y in range(n_rows):
            error_out[k, y : y + 1, :] = own[k : k + 1, y * W : (y + 1) * W]
    s = own * floats[0]
    g_b_head = jnp.sum(s, axis=1, keepdims=True)
    loss = jnp.sum(jnp.sum(own * own, axis=1, keepdims=True), axis=0, keepdims=True) * floats[1]

    def joint_slopes(b, carry):
        y = 2 * b
        sj = dot(s3[rows(y + 2, 2, W), :], wjb[0])
        sj = sj + dot(s3[rows(y + 1, 2, W), :], wjb[1])
        sj = sj + dot(s3[rows(y, 2, W), :], wjb[2])
        for u in range(2):
            part = sj[u * W : (u + 1) * W]
            v = part[:, 0:C] * d_motion[rows(y + u + 2, 1, W), :]
            stack(m3, y + u, jnp.where(inside(y + u - 1), v, 0.0), bwd)
            s_flow[rows(y + u, 1, W), :] = (part[:, C:] * d_flow[rows(y + u + 2, 1, W), :]).astype(BF)
        return carry

    lax.fori_loop(0, (n_rows + 2) // 2, joint_slopes, 0)

    def code_slopes(b, carry):
        y = 2 * b
        sc = dot(m3[rows(y + 2, 2, W), :], wcb[0])
        sc = sc + dot(m3[rows(y + 1, 2, W), :], wcb[1])
        sc = sc + dot(m3[rows(y, 2, W), :], wcb[2])
        pre = dot(vol[rows(y, 2, W), :], wv[...]) + bias[0:1, :]
        s_code[rows(y, 2, W), :] = (sc * silu_pair(pre)[1]).astype(BF)
        add_rows(0, s_code[rows(y, 2, W), :].astype(F32))
        add_rows(1, m3[rows(y + 1, 2, W), C : 2 * C].astype(F32))
        add_rows(2, s_flow[rows(y + 1, 2, W), :].astype(F32))
        add_rows(3, s3[rows(y + 2, 2, W), C : 2 * C].astype(F32))
        g_head[...] += dot(split3(err[:, rows(y + 2, 2, W)] * floats[0]), hid[rows(y + 2, 2, W), :])
        jt[:, rows(y, 2, W)] = j3[rows(y + 3, 2, W), 2 * C : 4 * C].T
        return carry

    lax.fori_loop(0, n_rows // 2, code_slopes, 0)

    for i in range(3):
        g = dot(jt[...], s3[(3 - i) * W : (3 - i) * W + body, :])
        for j in range(3):
            at = (i * 3 + j) * 2 * C
            grads[at : at + 2 * C, :] = g[:, j * C : (j + 1) * C]
    code_t = code[...].T
    for i in range(3):
        g = dot(code_t, m3[(2 - i) * W : (2 - i) * W + body, :])
        for j in range(3):
            at = AT_CODE + (i * 3 + j) * C
            grads[at : at + C, :] = g[:, j * C : (j + 1) * C]
    gv = lax.dot_general(vol[...], s_code[...], TN, preferred_element_type=F32)
    grads[AT_VOLUME : AT_VOLUME + 88, :] = gv[0:88]
    grads[AT_VOLUME + 88 : AT_VOLUME + 176, :] = gv[W : W + 88]
    gf = jnp.zeros((112, C), F32)
    for y in range(n_rows):
        gf = gf + dot(xb[(y + 3) * 16 : (y + 3) * 16 + 112, :], s_flow[(y + 1) * W : (y + 2) * W, :])
    grads[AT_FLOW : AT_FLOW + 112, :] = gf
    col = lax.broadcasted_iota(jnp.int32, (1, C), 1)
    tail = jnp.where(col == 0, loss, jnp.where(col == 1, g_b_head[0:1], jnp.where(col == 2, g_b_head[1:2], 0.0)))
    for k in range(4):
        grads[AT_MISC + k : AT_MISC + k + 1, :] = jnp.sum(acc[8 * k : 8 * k + 8, :], axis=0, keepdims=True)
    grads[AT_MISC + 4 : AT_MISC + 6, :] = g_head[0:2, :] + g_head[16:18, :] + g_head[32:34, :]
    grads[AT_MISC + 6 : AT_MISC + 7, :] = tail
    grads[AT_MISC + 7 : GRAD_ROWS, :] = jnp.zeros((GRAD_ROWS - AT_MISC - 7, C), F32)


VMEM = pl.BlockSpec(memory_space=pltpu.VMEM)
SMEM = pl.BlockSpec(memory_space=pltpu.SMEM)
ANY = pl.BlockSpec(memory_space=pl.ANY)


def reduce_all(x):
    steps = []
    for axis in ("tm", "space"):
        bit = 1
        while bit < lax.axis_size(axis):
            steps.append((axis, bit))
            bit *= 2
    for axis, bit in steps:
        upper = (lax.axis_index(axis) // bit) % 2
        half = x.shape[0] // 2
        keep = lax.dynamic_slice_in_dim(x, upper * half, half, 0)
        send = lax.dynamic_slice_in_dim(x, (1 - upper) * half, half, 0)
        route = [(i, i ^ bit) for i in range(lax.axis_size(axis))]
        x = keep + lax.ppermute(send, axis, route)
    for axis, bit in steps[::-1]:
        upper = (lax.axis_index(axis) // bit) % 2
        route = [(i, i ^ bit) for i in range(lax.axis_size(axis))]
        got = lax.ppermute(x, axis, route)
        x = jnp.where(upper == 0, jnp.concatenate([x, got]), jnp.concatenate([got, x]))
    return x


def local(
    features, pair_order, flow_now, targets, w_volume, b_volume, w_code, b_code,
    w_flow, b_flow, w_joint, b_joint, w_head, b_head,
):
    own = features[0]
    n_rows, n_cols, n_chan = own.shape
    n_code = w_code.shape[3]
    body = n_rows * n_cols
    halo = HALO * n_cols
    n_tm, n_space = lax.axis_size("tm"), lax.axis_size("space")
    flat = own.reshape(body, n_chan)

    def route(dt, ds):
        pairs = []
        for t in range(n_tm):
            for s in range(n_space):
                if 0 <= t + dt < n_tm and 0 <= s + ds < n_space:
                    pairs.append((t * n_space + s, (t + dt) * n_space + s + ds))
        return pairs

    both = ("tm", "space")
    first, last = flat[:halo], flat[body - halo :]
    top_n = lax.ppermute(last, both, route(-1, 1))
    bot_n = lax.ppermute(first, both, route(-1, -1))
    top_p = lax.ppermute(last, both, route(1, 1))
    bot_p = lax.ppermute(first, both, route(1, -1))
    mid_n = lax.ppermute(flat, both, route(-1, 0))
    mid_p = lax.ppermute(flat, both, route(1, 0))

    wv = jnp.pad(w_volume.reshape(2, OFF, n_code), ((0, 0), (0, n_cols - OFF), (0, 0))).reshape(2 * n_cols, n_code)
    wc = w_code.reshape(3, 3 * n_code, n_code)
    wcb = w_code.transpose(0, 1, 3, 2).reshape(3, 3 * n_code, n_code)
    wj = w_joint.reshape(3, 6 * n_code, n_code)
    wjb = w_joint.transpose(0, 1, 3, 2).reshape(3, 3 * n_code, 2 * n_code)
    wf = jnp.pad(w_flow.reshape(7, 14, n_code), ((0, 0), (0, 2), (0, 0))).reshape(112, n_code)
    wht = jnp.tile(jnp.pad(w_head.T, ((0, 14), (0, 0))), (3, 1))
    bias = jnp.stack([b_volume, b_code, b_flow, b_joint])
    frame_at = lax.axis_index("tm").astype(F32)
    frame_weight = jnp.power(F32(0.25), (n_tm - 1 - frame_at) / (n_tm - 1))
    height = n_rows * n_space
    count = 2.0 * n_tm * height * n_cols
    floats = jnp.stack([2.0 * frame_weight / count, frame_weight / count, b_head[0], b_head[1]])
    ints = jnp.stack([lax.axis_index("space") * n_rows, jnp.int32(height)]).astype(jnp.int32)
    flow = flow_now[0]
    near_targets = targets[0].astype(BF)
    up_x = jnp.concatenate([flow[:, :FLOW_HALO], near_targets[:, :TARGET_HALO]], axis=1).reshape(16, n_cols)
    dn_x = jnp.concatenate(
        [flow[:, n_rows - FLOW_HALO :], near_targets[:, n_rows - TARGET_HALO :]], axis=1
    ).reshape(16, n_cols)

    vol, code, up, dn = pl.pallas_call(
        functools.partial(correlate_kernel, n_rows, n_cols),
        out_shape=(
            jax.ShapeDtypeStruct((body, 2 * n_cols), BF),
            jax.ShapeDtypeStruct((body, n_code), BF),
            jax.ShapeDtypeStruct((halo + 16, n_code), BF),
            jax.ShapeDtypeStruct((halo + 16, n_code), BF),
        ),
        in_specs=[SMEM] + [ANY] * 7 + [VMEM] * 4,
        out_specs=(VMEM,) * 4,
        scratch_shapes=[
            pltpu.VMEM((body, n_chan), BF),
            pltpu.VMEM((2, body + 2 * halo, n_chan), BF),
            pltpu.SemaphoreType.DMA((7,)),
        ],
        name="correlate",
    )(pair_order, flat, mid_n, top_n, bot_n, mid_p, top_p, bot_p, wv, bias, up_x, dn_x)

    down_route = [(s, s + 1) for s in range(n_space - 1)]
    up_route = [(s + 1, s) for s in range(n_space - 1)]
    top = lax.ppermute(dn, "space", down_route)
    bot = lax.ppermute(up, "space", up_route)

    W, C = n_cols, n_code
    flow_error, grads = pl.pallas_call(
        functools.partial(train_kernel, n_rows, n_cols),
        out_shape=(
            jax.ShapeDtypeStruct((2, n_rows, n_cols), F32),
            jax.ShapeDtypeStruct((GRAD_ROWS, n_code), F32),
        ),
        in_specs=[SMEM, SMEM] + [VMEM] * 14,
        out_specs=(VMEM, VMEM),
        scratch_shapes=[
            pltpu.VMEM(((n_rows + 8) * W, 3 * C), BF),
            pltpu.VMEM(((n_rows + 6) * W, 6 * C), BF),
            pltpu.VMEM(((n_rows + 6) * W, C), F32),
            pltpu.VMEM(((n_rows + 6) * W, C), F32),
            pltpu.VMEM(((n_rows + 4) * W, 3 * C), BF),
            pltpu.VMEM(((n_rows + 2) * W, 3 * C), BF),
            pltpu.VMEM((24, W), F32),
            pltpu.VMEM(((n_rows + 12) * 16, W), F32),
            pltpu.VMEM(((n_rows + 12) * 16, W), BF),
            pltpu.VMEM((16, (n_rows + 4) * W), F32),
            pltpu.VMEM((16, (n_rows + 4) * W), F32),
            pltpu.VMEM(((n_rows + 4) * W, C), BF),
            pltpu.VMEM(((n_rows + 2) * W, C), BF),
            pltpu.VMEM((body, C), BF),
            pltpu.VMEM((2 * C, body), BF),
            pltpu.VMEM((32, C), F32),
            pltpu.VMEM((48, C), F32),
        ],
        name="train",
    )(ints, floats, vol, code, top, bot, flow, targets[0], wv, wc, wcb, wj, wjb, wf, wht, bias)

    grads = reduce_all(grads)
    misc = grads[AT_MISC : AT_MISC + 8]
    return (
        misc[6, 0:1],
        flow_error[None],
        grads[AT_VOLUME:AT_FLOW].reshape(2, 88, n_code)[:, :OFF].reshape(2 * OFF, n_code),
        misc[0],
        grads[AT_CODE:AT_VOLUME].reshape(3, 3, n_code, n_code),
        misc[1],
        grads[AT_FLOW : AT_FLOW + 112].reshape(7, 16, n_code)[:, :14].reshape(7, 7, 2, n_code),
        misc[2],
        grads[:AT_CODE].reshape(3, 3, 2 * n_code, n_code),
        misc[3],
        misc[4:6].T,
        misc[6, 1:3],
    )


def solution(mesh):
    placed = (
        P(("groups", "tm"), "space", None, None),
        P(("groups", "tm")),
        P(("groups", "tm"), None, "space", None),
        P(("groups", "tm"), None, "space", None),
    ) + (P(),) * 10
    return jax.shard_map(
        local,
        mesh=mesh,
        in_specs=placed,
        out_specs=(
            P("groups"),
            P(("groups", "tm"), None, "space", None),
            P("groups", None),
            P("groups"),
            P("groups", None, None, None),
            P("groups"),
            P("groups", None, None, None),
            P("groups"),
            P("groups", None, None, None),
            P("groups"),
            P("groups", None),
            P("groups"),
        ),
        check_vma=False,
    )
```

time: 306 us -> 138 us (0.45); the launches traced: 302 us -> 137 us
  local copies, waits for them, and re-layouts: 80 us -> 15.8 us
  blocking collectives: 62.3 us -> 0 us
  matrix products: 45.1 us -> 0 us
  Pallas kernels: 0 us -> 27.9 us
  between operations: 18.2 us -> 1.64 us
  starting transfers between devices: 36.4 us -> 30.5 us
    psum x1 -> x0, blocking collectives: 62.3 us -> none  [local(): lax.psum((loss_local, grad_w_volume, grad_b_volume, grad_w_code, grad_b_c...]
    dot_general x43 -> x0, matrix products: 45.1 us -> none  [the longest x18 24.8 us: correlate(): jnp.einsum('rxc,ryc->rxy', own_tile, window, preferred_element_type=jnp.f...]
    ppermute x14 -> x16, waiting for transfers between devices: 15 us -> 55.1 us  [the longest x4 29 us: reduce_all(): x = keep + lax.ppermute(send, axis, route)]
    psum x1 -> x0, waiting for transfers between devices: 39.9 us -> none  [local(): lax.psum((loss_local, grad_w_volume, grad_b_volume, grad_w_code, grad_b_c...]
    reshape x44 -> x4, local copies, waits for them, and re-layouts: 39.6 us -> 2.13 us  [the longest x1 0.8 us: local(): w_volume.reshape(2, OFF, n_code)]
    pallas_call x0 -> x2, Pallas kernels: none -> 27.9 us  [the longest x1 16.9 us: local(): pl.pallas_call(functools.partial(train_kernel, n_rows, n_cols), out_shape...]
    another operation x87 -> x1, local copies, waits for them, and re-layouts: 12 us -> 0.63 us  [local(): wht = jnp.tile(jnp.pad(w_head.T, ((0, 14), (0, 0))), (3, 1))]
    unnamed x150 -> x28, local copies, waits for them, and re-layouts: 12.4 us -> 1.19 us
  transfers between devices with their start and end apart: 15 -> 16, of which waited for: 6 -> 9; matrix products, arithmetic and copies ran while one was open for 15% -> 8% of each run, Pallas kernels for 0% -> 0%
where the time goes in v1:
time: 138 us; the launch traced here: 137 us
  waiting for transfers between devices  55.1 us (40%)
  starting transfers between devices  30.5 us (22%)
  Pallas kernels  27.9 us (20%)
  local copies, waits for them, and re-layouts  15.8 us (11%)
  other arithmetic  6.22 us (5%)
  between operations  1.64 us (1%)
    ppermute x4, waiting for transfers between devices, reduce_all(): x = keep + lax.ppermute(send, axis, route)  29 us
    ppermute x4, waiting for transfers between devices, reduce_all(): got = lax.ppermute(x, axis, route)  23.2 us
    pallas_call x1, Pallas kernels, local(): pl.pallas_call(functools.partial(train_kernel, n_rows, n_cols), out_shape...  16.9 us
    pallas_call x1, Pallas kernels, local(): pl.pallas_call(functools.partial(correlate_kernel, n_rows, n_cols), out_s...  10.9 us
    ppermute x1, starting transfers between devices, local(): top = lax.ppermute(dn, 'space', down_route)  7.85 us
    ppermute x1, starting transfers between devices, local(): top_p = lax.ppermute(last, both, route(1, 1))  7.47 us
    ppermute x4, starting transfers between devices, reduce_all(): x = keep + lax.ppermute(send, axis, route)  5.07 us
    ppermute x1, starting transfers between devices, local(): mid_p = lax.ppermute(flat, both, route(1, 0))  3.07 us
  transfers between devices with their start and end apart: 16, of which 9 were waited for; matrix products, arithmetic and copies ran while one was open for 8% of the time, Pallas kernels for 0%

profile of v1, /device:TPU:0, one launch (start us, length us, event | category | flops | bytes accessed | tf_op | source)
XLA Modules:
  0.0 137.1 jit_solution(7750920089606636578)
XLA Ops:
  0.7 1.4 %collective-permute-start = (bf16[1024,256]{1,0:T(8,128)(2,1)}, bf16[1024,256]{1,0:T(8,128)(2,1)S(1)}, u32[]{:S(2)}, u32[]{:S(2)}) collective-permute-start(bf16[1024,256]{1,0:T(8,128)(2,1)} %bitcast.50), channel_id=1, source_target_pairs={{4,0},{5,1},{6,2},{7,3},{8,4},{9,5},{10,6},{11,7},{12,8},{13,9},{1... | collective-permute-start | bytes 1572872 | tf_op jit(solution)/shard_map/ppermute | solution.py:342
  2.1 3.1 %collective-permute-start.3 = (bf16[1024,256]{1,0:T(8,128)(2,1)}, bf16[1024,256]{1,0:T(8,128)(2,1)S(1)}, u32[]{:S(2)}, u32[]{:S(2)}) collective-permute-start(bf16[1024,256]{1,0:T(8,128)(2,1)} %bitcast.51), channel_id=1, source_target_pairs={{0,4},{1,5},{2,6},{3,7},{4,8},{5,9},{6,10},{7,11},{8,12},{9,13},{1... | collective-permute-start | bytes 1572872 | tf_op jit(solution)/shard_map/ppermute | solution.py:343
  7.1 7.5 %collective-permute-start.4 = (bf16[512,256]{1,0:T(8,128)(2,1)S(1)}, bf16[512,256]{1,0:T(8,128)(2,1)S(1)}, u32[]{:S(2)}, u32[]{:S(2)}) collective-permute-start(bf16[512,256]{1,0:T(8,128)(2,1)S(1)} %bitcast.64), channel_id=1, source_target_pairs={{0,5},{1,6},{2,7},{4,9},{5,10},{6,11},{8,13},{9,14},{10,15},{16,21... | collective-permute-start | bytes 786440 | tf_op jit(solution)/shard_map/ppermute | solution.py:340
  14.5 1.3 collective-permute-start.2
  16.5 1.4 fusion.1
  21.2 1.3 pad_maximum_fusion.bias_ref.bias
  22.5 1.3 maximum_bitcast_fusion
  25.1 10.9 %correlate.1 = (bf16[1024,256]{1,0:T(8,128)(2,1)}, bf16[1024,128]{1,0:T(8,128)(2,1)}, bf16[528,128]{1,0:T(8,128)(2,1)}, bf16[528,128]{1,0:T(8,128)(2,1)}) custom-call(s32[1]{0:T(128)S(6)} %copy.30.swap_ref, bf16[1024,256]{1,0:T(8,128)(2,1)} %bitcast.52, bf16[1024,256]{1,0:T(8,128)(2,1)} %copy-done.3, bf16[512,256]{1,0:T(8,128)(2,1)} %copy-done.5, ...), custom_call_target="tpu_custom_call" | custom-call | tf_op jit(solution)/shard_map/correlate/pallas_call | solution.py:366
  36.0 7.8 %collective-permute-start.6 = (bf16[528,128]{1,0:T(8,128)(2,1)}, bf16[528,128]{1,0:T(8,128)(2,1)S(1)}, u32[]{:S(2)}, u32[]{:S(2)}) collective-permute-start(bf16[528,128]{1,0:T(8,128)(2,1)} %get-tuple-element.20), channel_id=1, source_target_pairs={{0,1},{1,2},{2,3},{4,5},{5,6},{6,7},{8,9},{9,10},{10,11},{12,13},{... | collective-permute-start | bytes 405512 | tf_op jit(solution)/shard_map/ppermute | solution.py:386
  43.9 1.3 collective-permute-start.7
  49.1 2.8 %collective-permute-done.7.bot = bf16[528,128]{1,0:T(8,128)(2,1)S(1)} collective-permute-done((bf16[528,128]{1,0:T(8,128)(2,1)}, bf16[528,128]{1,0:T(8,128)(2,1)S(1)}, u32[]{:S(2)}, u32[]{:S(2)}) %collective-permute-start.7) | collective-permute-done | bytes 135200 | tf_op jit(solution)/shard_map/ppermute | solution.py:387
  52.6 16.9 %train.1 = (f32[2,8,128]{2,1,0:T(8,128)}, f32[3840,128]{1,0:T(8,128)}) custom-call(s32[2]{0:T(128)} %pad_add_fusion.ints, f32[4]{0:T(128)} %pad_maximum_fusion.1.floats, bf16[1024,256]{1,0:T(8,128)(2,1)} %get-tuple-element.18.vol, bf16[1024,128]{1,0:T(8,128)(2,1)} %get-tuple-element.19.code, bf16[528,128]{1,0:T(8,128)(2,1)} %copy-done.9, ...), custom_call_target="tpu_custom_call" | custom-call | tf_op jit(solution)/shard_map/train/pallas_call | solution.py:390
  69.5 1.4 %constant_dynamic-slice_fusion.3 = f32[1920,128]{1,0:T(8,128)S(1)} fusion(f32[3840,128]{1,0:T(8,128)} %get-tuple-element.22, s32[]{:T(128)S(6)} %select_n.107), kind=kLoop, calls=%fused_computation.14 | loop fusion | bytes 1966084 | tf_op jit(solution)/shard_map/dynamic_slice | solution.py:305
  71.4 2.3 %collective-permute-done.8 = f32[1920,128]{1,0:T(8,128)} collective-permute-done((f32[1920,128]{1,0:T(8,128)S(1)}, f32[1920,128]{1,0:T(8,128)}, u32[]{:S(2)}, u32[]{:S(2)}) %collective-permute-start.8) | collective-permute-done | bytes 983072 | tf_op jit(solution)/shard_map/ppermute | solution.py:307
  73.7 1.3 dynamic-slice_add_fusion
  75.1 3.4 %collective-permute-start.9 = (f32[960,128]{1,0:T(8,128)S(1)}, f32[960,128]{1,0:T(8,128)S(1)}, u32[]{:S(2)}, u32[]{:S(2)}) collective-permute-start(f32[960,128]{1,0:T(8,128)S(1)} %constant_dynamic-slice_fusion.2), channel_id=1, source_target_pairs={{0,8},{4,12},{8,0},{12,4},{1,9},{5,13},{9,1},{13,5},{2,10},{6,14},... | collective-permute-start | bytes 1474568 | tf_op jit(solution)/shard_map/ppermute | solution.py:307
  78.4 11.5 %collective-permute-done.9 = f32[960,128]{1,0:T(8,128)S(1)} collective-permute-done((f32[960,128]{1,0:T(8,128)S(1)}, f32[960,128]{1,0:T(8,128)S(1)}, u32[]{:S(2)}, u32[]{:S(2)}) %collective-permute-start.9) | collective-permute-done | bytes 491552 | tf_op jit(solution)/shard_map/ppermute | solution.py:307
  90.9 6.7 %collective-permute-done.10 = f32[480,128]{1,0:T(8,128)S(1)} collective-permute-done((f32[480,128]{1,0:T(8,128)S(1)}, f32[480,128]{1,0:T(8,128)S(1)}, u32[]{:S(2)}, u32[]{:S(2)}) %collective-permute-start.10) | collective-permute-done | bytes 245792 | tf_op jit(solution)/shard_map/ppermute | solution.py:307
  98.1 8.4 %collective-permute-done.11 = f32[240,128]{1,0:T(8,128)S(1)} collective-permute-done((f32[240,128]{1,0:T(8,128)S(1)}, f32[240,128]{1,0:T(8,128)S(1)}, u32[]{:S(2)}, u32[]{:S(2)}) %collective-permute-start.11) | collective-permute-done | bytes 122912 | tf_op jit(solution)/shard_map/ppermute | solution.py:307
  106.6 5.8 %collective-permute-done.12 = f32[240,128]{1,0:T(8,128)S(1)} collective-permute-done((f32[240,128]{1,0:T(8,128)S(1)}, f32[240,128]{1,0:T(8,128)S(1)}, u32[]{:S(2)}, u32[]{:S(2)}) %collective-permute-start.12) | collective-permute-done | bytes 122912 | tf_op jit(solution)/shard_map/ppermute | solution.py:311
  112.5 6.2 %collective-permute-done.13 = f32[480,128]{1,0:T(8,128)S(1)} collective-permute-done((f32[480,128]{1,0:T(8,128)S(1)}, f32[480,128]{1,0:T(8,128)S(1)}, u32[]{:S(2)}, u32[]{:S(2)}) %collective-permute-start.13) | collective-permute-done | bytes 245792 | tf_op jit(solution)/shard_map/ppermute | solution.py:311
  118.7 1.3 collective-permute-start.14
  120.0 8.7 %collective-permute-done.14 = f32[960,128]{1,0:T(8,128)S(1)} collective-permute-done((f32[960,128]{1,0:T(8,128)S(1)}, f32[960,128]{1,0:T(8,128)S(1)}, u32[]{:S(2)}, u32[]{:S(2)}) %collective-permute-start.14) | collective-permute-done | bytes 491552 | tf_op jit(solution)/shard_map/ppermute | solution.py:311
  128.9 2.5 %collective-permute-done.15 = f32[1920,128]{1,0:T(8,128)S(1)} collective-permute-done((f32[1920,128]{1,0:T(8,128)S(1)}, f32[1920,128]{1,0:T(8,128)S(1)}, u32[]{:S(2)}, u32[]{:S(2)}) %collective-permute-start.15) | collective-permute-done | bytes 983072 | tf_op jit(solution)/shard_map/ppermute | solution.py:311
  (76 shorter events, 18.7 us)
Async XLA Ops:
  0.6 45.2 %copy-start.2 = (bf16[3,3,128,128]{3,2,1,0:T(8,128)(2,1)S(1)}, bf16[3,3,128,128]{3,2,1,0:T(8,128)(2,1)}, u32[]{:S(2)}) copy-start(bf16[3,3,128,128]{3,2,1,0:T(8,128)(2,1)} %param.20) | copy-start | bytes 884740
  0.7 23.2 %collective-permute-start = (bf16[1024,256]{1,0:T(8,128)(2,1)}, bf16[1024,256]{1,0:T(8,128)(2,1)S(1)}, u32[]{:S(2)}, u32[]{:S(2)}) collective-permute-start(bf16[1024,256]{1,0:T(8,128)(2,1)} %bitcast.50), channel_id=1, source_target_pairs={{4,0},{5,1},{6,2},{7,3},{8,4},{9,5},{10,6},{11,7},{12,8},{13,9},{1... | collective-permute-start | bytes 1572872 | tf_op jit(solution)/shard_map/ppermute | solution.py:342
  2.1 21.8 %collective-permute-start.3 = (bf16[1024,256]{1,0:T(8,128)(2,1)}, bf16[1024,256]{1,0:T(8,128)(2,1)S(1)}, u32[]{:S(2)}, u32[]{:S(2)}) collective-permute-start(bf16[1024,256]{1,0:T(8,128)(2,1)} %bitcast.51), channel_id=1, source_target_pairs={{0,4},{1,5},{2,6},{3,7},{4,8},{5,9},{6,10},{7,11},{8,12},{9,13},{1... | collective-permute-start | bytes 1572872 | tf_op jit(solution)/shard_map/ppermute | solution.py:343
  6.2 40.5 %copy-start = (bf16[3,3,256,128]{3,2,1,0:T(8,128)(2,1)S(1)}, bf16[3,3,256,128]{3,2,1,0:T(8,128)(2,1)}, u32[]{:S(2)}) copy-start(bf16[3,3,256,128]{3,2,1,0:T(8,128)(2,1)} %param.24) | copy-start | bytes 1769476
  6.2 11.7 %collective-permute-start.1 = (bf16[512,256]{1,0:T(8,128)(2,1)S(1)}, bf16[512,256]{1,0:T(8,128)(2,1)S(1)}, u32[]{:S(2)}, u32[]{:S(2)}) collective-permute-start(bf16[512,256]{1,0:T(8,128)(2,1)S(1)} %bitcast.63), channel_id=1, source_target_pairs={{4,1},{5,2},{6,3},{8,5},{9,6},{10,7},{12,9},{13,10},{14,11},{20,17... | collective-permute-start | bytes 786440 | tf_op jit(solution)/shard_map/ppermute | solution.py:338
  7.1 16.8 %collective-permute-start.4 = (bf16[512,256]{1,0:T(8,128)(2,1)S(1)}, bf16[512,256]{1,0:T(8,128)(2,1)S(1)}, u32[]{:S(2)}, u32[]{:S(2)}) collective-permute-start(bf16[512,256]{1,0:T(8,128)(2,1)S(1)} %bitcast.64), channel_id=1, source_target_pairs={{0,5},{1,6},{2,7},{4,9},{5,10},{6,11},{8,13},{9,14},{10,15},{16,21... | collective-permute-start | bytes 786440 | tf_op jit(solution)/shard_map/ppermute | solution.py:340
  14.5 9.3 %collective-permute-start.2 = (bf16[512,256]{1,0:T(8,128)(2,1)S(1)}, bf16[512,256]{1,0:T(8,128)(2,1)S(1)}, u32[]{:S(2)}, u32[]{:S(2)}) collective-permute-start(bf16[512,256]{1,0:T(8,128)(2,1)S(1)} %bitcast.61), channel_id=1, source_target_pairs={{5,0},{6,1},{7,2},{9,4},{10,5},{11,6},{13,8},{14,9},{15,10},{21,16... | collective-permute-start | bytes 786440 | tf_op jit(solution)/shard_map/ppermute | solution.py:339
  17.9 6.0 %copy-start.5 = (bf16[512,256]{1,0:T(8,128)(2,1)}, bf16[512,256]{1,0:T(8,128)(2,1)S(1)}, u32[]{:S(2)}) copy-start(bf16[512,256]{1,0:T(8,128)(2,1)S(1)} %collective-permute-done.1.top_n) | copy-start | bytes 786436
  17.9 6.0 %collective-permute-start.5 = (bf16[512,256]{1,0:T(8,128)(2,1)S(1)}, bf16[512,256]{1,0:T(8,128)(2,1)S(1)}, u32[]{:S(2)}, u32[]{:S(2)}) collective-permute-start(bf16[512,256]{1,0:T(8,128)(2,1)S(1)} %bitcast.62), channel_id=1, source_target_pairs={{1,4},{2,5},{3,6},{5,8},{6,9},{7,10},{9,12},{10,13},{11,14},{17,20... | collective-permute-start | bytes 786440 | tf_op jit(solution)/shard_map/ppermute | solution.py:341
  25.1 22.7 %copy-start.11 = (bf16[7,7,2,128]{3,2,1,0:T(2,128)(2,1)S(1)}, bf16[7,7,2,128]{3,2,1,0:T(2,128)(2,1)}, u32[]{:S(2)}) copy-start(bf16[7,7,2,128]{3,2,1,0:T(2,128)(2,1)} %param.22) | copy-start | bytes 75268
  25.1 23.4 %copy-start.12 = (bf16[128,2]{0,1:T(2,128)(2,1)S(1)}, bf16[128,2]{0,1:T(2,128)(2,1)}, u32[]{:S(2)}) copy-start(bf16[128,2]{0,1:T(2,128)(2,1)} %param.26) | copy-start | bytes 1540
  25.1 23.4 %copy-start.13 = (f32[2]{0:T(128)S(1)}, f32[2]{0:T(128)}, u32[]{:S(2)}) copy-start(f32[2]{0:T(128)} %param.27) | copy-start | bytes 28
  36.0 13.0 %collective-permute-start.6 = (bf16[528,128]{1,0:T(8,128)(2,1)}, bf16[528,128]{1,0:T(8,128)(2,1)S(1)}, u32[]{:S(2)}, u32[]{:S(2)}) collective-permute-start(bf16[528,128]{1,0:T(8,128)(2,1)} %get-tuple-element.20), channel_id=1, source_target_pairs={{0,1},{1,2},{2,3},{4,5},{5,6},{6,7},{8,9},{9,10},{10,11},{12,13},{... | collective-permute-start | bytes 405512 | tf_op jit(solution)/shard_map/ppermute | solution.py:386
  43.9 8.0 %collective-permute-start.7 = (bf16[528,128]{1,0:T(8,128)(2,1)}, bf16[528,128]{1,0:T(8,128)(2,1)S(1)}, u32[]{:S(2)}, u32[]{:S(2)}) collective-permute-start(bf16[528,128]{1,0:T(8,128)(2,1)} %get-tuple-element.21), channel_id=1, source_target_pairs={{1,0},{2,1},{3,2},{5,4},{6,5},{7,6},{9,8},{10,9},{11,10},{13,12},{... | collective-permute-start | bytes 405512 | tf_op jit(solution)/shard_map/ppermute | solution.py:387
  49.1 3.5 %copy-start.9 = (bf16[528,128]{1,0:T(8,128)(2,1)}, bf16[528,128]{1,0:T(8,128)(2,1)S(1)}, u32[]{:S(2)}) copy-start(bf16[528,128]{1,0:T(8,128)(2,1)S(1)} %collective-permute-done.6.top) | copy-start | bytes 405508
  69.5 4.2 %copy-start.1 = (f32[3840,128]{1,0:T(8,128)S(1)}, f32[3840,128]{1,0:T(8,128)}, u32[]{:S(2)}) copy-start(f32[3840,128]{1,0:T(8,128)} %get-tuple-element.22) | copy-start | bytes 5898244
  70.9 2.8 %collective-permute-start.8 = (f32[1920,128]{1,0:T(8,128)S(1)}, f32[1920,128]{1,0:T(8,128)}, u32[]{:S(2)}, u32[]{:S(2)}) collective-permute-start(f32[1920,128]{1,0:T(8,128)S(1)} %constant_dynamic-slice_fusion.3), channel_id=1, source_target_pairs={{0,4},{4,0},{8,12},{12,8},{1,5},{5,1},{9,13},{13,9},{2,6},{6,2},{1... | collective-permute-start | bytes 2949128 | tf_op jit(solution)/shard_map/ppermute | solution.py:307
  75.1 14.9 %collective-permute-start.9 = (f32[960,128]{1,0:T(8,128)S(1)}, f32[960,128]{1,0:T(8,128)S(1)}, u32[]{:S(2)}, u32[]{:S(2)}) collective-permute-start(f32[960,128]{1,0:T(8,128)S(1)} %constant_dynamic-slice_fusion.2), channel_id=1, source_target_pairs={{0,8},{4,12},{8,0},{12,4},{1,9},{5,13},{9,1},{13,5},{2,10},{6,14},... | collective-permute-start | bytes 1474568 | tf_op jit(solution)/shard_map/ppermute | solution.py:307
  90.1 7.6 %collective-permute-start.10 = (f32[480,128]{1,0:T(8,128)S(1)}, f32[480,128]{1,0:T(8,128)S(1)}, u32[]{:S(2)}, u32[]{:S(2)}) collective-permute-start(f32[480,128]{1,0:T(8,128)S(1)} %constant_dynamic-slice_fusion.1), channel_id=1, source_target_pairs={{0,1},{1,0},{2,3},{3,2},{4,5},{5,4},{6,7},{7,6},{8,9},{9,8},{10,11... | collective-permute-start | bytes 737288 | tf_op jit(solution)/shard_map/ppermute | solution.py:307
  97.7 8.9 %collective-permute-start.11 = (f32[240,128]{1,0:T(8,128)S(1)}, f32[240,128]{1,0:T(8,128)S(1)}, u32[]{:S(2)}, u32[]{:S(2)}) collective-permute-start(f32[240,128]{1,0:T(8,128)S(1)} %constant_dynamic-slice_fusion), channel_id=1, source_target_pairs={{0,2},{1,3},{2,0},{3,1},{4,6},{5,7},{6,4},{7,5},{8,10},{9,11},{10,... | collective-permute-start | bytes 368648 | tf_op jit(solution)/shard_map/ppermute | solution.py:307
  106.6 5.8 %collective-permute-start.12 = (f32[240,128]{1,0:T(8,128)S(1)}, f32[240,128]{1,0:T(8,128)S(1)}, u32[]{:S(2)}, u32[]{:S(2)}) collective-permute-start(f32[240,128]{1,0:T(8,128)S(1)} %dynamic-slice_add_fusion.3), channel_id=1, source_target_pairs={{0,2},{1,3},{2,0},{3,1},{4,6},{5,7},{6,4},{7,5},{8,10},{9,11},{10,... | collective-permute-start | bytes 368648 | tf_op jit(solution)/shard_map/ppermute | solution.py:311
  112.4 6.3 %collective-permute-start.13 = (f32[480,128]{1,0:T(8,128)S(1)}, f32[480,128]{1,0:T(8,128)S(1)}, u32[]{:S(2)}, u32[]{:S(2)}) collective-permute-start(f32[480,128]{1,0:T(8,128)S(1)} %maximum_select_fusion.3), channel_id=1, source_target_pairs={{0,1},{1,0},{2,3},{3,2},{4,5},{5,4},{6,7},{7,6},{8,9},{9,8},{10,11... | collective-permute-start | bytes 737288 | tf_op jit(solution)/shard_map/ppermute | solution.py:311
  118.7 10.0 %collective-permute-start.14 = (f32[960,128]{1,0:T(8,128)S(1)}, f32[960,128]{1,0:T(8,128)S(1)}, u32[]{:S(2)}, u32[]{:S(2)}) collective-permute-start(f32[960,128]{1,0:T(8,128)S(1)} %maximum_select_fusion.2), channel_id=1, source_target_pairs={{0,8},{4,12},{8,0},{12,4},{1,9},{5,13},{9,1},{13,5},{2,10},{6,14},... | collective-permute-start | bytes 1474568 | tf_op jit(solution)/shard_map/ppermute | solution.py:311
  128.8 2.6 %collective-permute-start.15 = (f32[1920,128]{1,0:T(8,128)S(1)}, f32[1920,128]{1,0:T(8,128)S(1)}, u32[]{:S(2)}, u32[]{:S(2)}) collective-permute-start(f32[1920,128]{1,0:T(8,128)S(1)} %maximum_select_fusion.1), channel_id=1, source_target_pairs={{0,4},{4,0},{8,12},{12,8},{1,5},{5,1},{9,13},{13,9},{2,6},{6,2},{1... | collective-permute-start | bytes 2949128 | tf_op jit(solution)/shard_map/ppermute | solution.py:311
  (6 other events, 5.2 us)

commit v2 on v1

v2 whole, which is shorter than its diff:
```python
import functools

import jax
import jax.numpy as jnp
from jax import lax
from jax.experimental import pallas as pl
from jax.experimental.pallas import tpu as pltpu
from jax.sharding import PartitionSpec as P

RADIUS = 4
SIDE = 2 * RADIUS + 1
OFF = SIDE * SIDE
HALO = 4
FLOW_HALO = 6
TARGET_HALO = 2
BF = jnp.bfloat16
F32 = jnp.float32
NT = (((1,), (1,)), ((), ()))
TN = (((0,), (0,)), ((), ()))

AT_CODE = 2304
AT_VOLUME = 3456
AT_FLOW = 3648
AT_END = 3760
HALF = 96
MISC_ROWS = 8


def dot(a, b):
    return jnp.dot(a, b, preferred_element_type=F32)


def dot_nt(a, b):
    return lax.dot_general(a, b, NT, preferred_element_type=F32)


def rows(start, count, unit):
    return pl.ds(pl.multiple_of(start * unit, unit), count * unit)


def split3(s):
    hi = s.astype(BF)
    rest = s - hi.astype(F32)
    mid = rest.astype(BF)
    return jnp.concatenate([hi, mid, (rest - mid.astype(F32)).astype(BF)], axis=0)


def silu_pair(v):
    s = jax.nn.sigmoid(v)
    return v * s, s * (1.0 + v * (1.0 - s))


def correlate_kernel(n_rows, n_cols, own, mid, top, bot, out, near, rows_f):
    n_chan = own.shape[1]
    halo = RADIUS * n_cols
    body = n_rows * n_cols
    near[0:halo, :] = top[...]
    near[halo : halo + body, :] = mid[...]
    near[halo + body :, :] = bot[...]
    W = n_cols
    j_at = lax.broadcasted_iota(jnp.int32, (W, 2 * W), 0)
    x_at = lax.broadcasted_iota(jnp.int32, (W, 2 * W), 1) & (W - 1)
    band = jnp.logical_and(j_at - x_at >= -RADIUS, j_at - x_at < RADIUS)
    edge = j_at - x_at == RADIUS
    turn = lax.broadcasted_iota(jnp.int32, (8, 2 * W), 1) + RADIUS
    scale = n_chan ** (-0.5)

    def fold(v):
        parts = [v[8 * g : 8 * g + 8] for g in range(W // 8)]
        while len(parts) > 1:
            parts = [parts[k] + parts[k + 1] for k in range(0, len(parts), 2)]
        return parts[0]

    def two_rows(b, carry):
        tile = own[rows(2 * b, 2, W), :]
        rows_f[...] = jnp.zeros_like(rows_f)
        for q in range(SIDE + 1):
            scores = lax.dot_general(
                near[rows(2 * b + q, 1, W), :], tile, NT, preferred_element_type=F32
            )
            inner = fold(jnp.where(band, scores, 0.0))
            outer = jnp.sum(fold(jnp.where(edge, scores, 0.0)), axis=0, keepdims=True)
            for bit in (1, 2, 4):
                inner = jnp.where((turn & bit) != 0, pltpu.roll(inner, 8 - bit, 0), inner)
            for u in range(2):
                dy = q - u
                if 0 <= dy < SIDE:
                    rows_f[8 * dy : 8 * dy + 8, u * W : (u + 1) * W] = inner[:, u * W : (u + 1) * W]
                    rows_f[72 + dy : 73 + dy, u * W : (u + 1) * W] = outer[:, u * W : (u + 1) * W]
        out[:, rows(2 * b, 2, W)] = (rows_f[...] * scale).astype(BF)
        return carry

    lax.fori_loop(0, n_rows // 2, two_rows, 0)


def code_kernel(
    n_rows, n_cols,
    order, near_vol, far_vol, w_volume, bias, flow, targets,
    vol, code, up, dn, wv,
    wide, edge,
):
    W = n_cols
    halo = HALO * W
    body = n_rows * W
    wide[...] = jnp.zeros_like(wide)
    weight = w_volume[...].astype(F32)
    for half in range(2):
        for dy in range(SIDE):
            at = half * OFF + dy * SIDE
            wide[half * HALF + 8 * dy : half * HALF + 8 * dy + 8, :] = weight[at : at + 8]
            wide[half * HALF + 72 + dy : half * HALF + 73 + dy, :] = weight[at + 8 : at + 9]
    wv[...] = wide[...].astype(BF)
    near_second = order[0] != lax.axis_index("tm") % 2
    a, b = near_vol[...], far_vol[...]
    vol[0:HALF, :] = jnp.where(near_second, b, a)
    vol[HALF : 2 * HALF, :] = jnp.where(near_second, a, b)

    def one_code(r, carry):
        at = rows(r, 2, W)
        pre = lax.dot_general(vol[:, at], wv[...], TN, preferred_element_type=F32) + bias[0:1, :]
        code[at, :] = (pre * jax.nn.sigmoid(pre)).astype(BF)
        return carry

    lax.fori_loop(0, n_rows // 2, lambda r, c: one_code(2 * r, c), 0)
    for ref, at, flow_at, target_at in (
        (up, 0, 0, 0),
        (dn, body - halo, n_rows - FLOW_HALO, n_rows - TARGET_HALO),
    ):
        ref[0:halo, :] = code[at : at + halo, :]
        for k in range(2):
            edge[8 * k : 8 * k + FLOW_HALO, :] = flow[k].astype(F32)[flow_at : flow_at + FLOW_HALO]
            edge[8 * k + FLOW_HALO : 8 * k + 8, :] = targets[k].astype(F32)[target_at : target_at + TARGET_HALO]
        ref[halo : halo + 16, :] = edge[...].astype(BF)


def frame_scale(n_tm, per):
    frame = lax.axis_index("tm")
    value = jnp.float32(per)
    for t in range(n_tm - 1):
        value = jnp.where(frame == t, jnp.float32(per * 0.25 ** ((n_tm - 1 - t) / (n_tm - 1))), value)
    return value


def inside_frame(n_rows, ext):
    at = lax.axis_index("space") * n_rows + ext
    return jnp.logical_and(at >= 0, at < lax.axis_size("space") * n_rows)


def store_stack(ref, at, v, cols):
    W, C = v.shape
    x_at = lax.broadcasted_iota(jnp.int32, (W, C), 0)
    left = jnp.where(x_at == 0, 0.0, pltpu.roll(v, 1, 0))
    right = jnp.where(x_at == W - 1, 0.0, pltpu.roll(v, W - 1, 0))
    for col, part in zip(cols, (left, v, right)):
        ref[rows(at, 1, W), col * C : (col + 1) * C] = part.astype(BF)


FWD = (0, 1, 2)
BWD = (2, 1, 0)


def flow_kernel(n_rows, n_cols, top, bot, flow, targets, w_flow, bias, jf, d_flow, xb, tgt, xf, xx, wide, wf):
    W = n_cols
    halo = HALO * W
    wide[...] = jnp.zeros_like(wide)
    for i in range(7):
        for j in range(7):
            wide[16 * i + 2 * j : 16 * i + 2 * j + 2, :] = w_flow[i, j].astype(F32)
    wf[...] = wide[...].astype(BF)
    xx[...] = jnp.zeros_like(xx)
    above = top[halo : halo + 16, :].astype(F32)
    below = bot[halo : halo + 16, :].astype(F32)
    n_flow = n_rows + 2 * FLOW_HALO
    lane = lax.broadcasted_iota(jnp.int32, (n_flow, W), 1)
    for k in range(2):
        xf[0:FLOW_HALO, :] = above[8 * k : 8 * k + FLOW_HALO, :]
        xf[FLOW_HALO : FLOW_HALO + n_rows, :] = flow[k].astype(F32)
        xf[FLOW_HALO + n_rows : n_flow, :] = below[8 * k : 8 * k + FLOW_HALO, :]
        own_flow = xf[0:n_flow, :]
        for j in range(7):
            shift = (3 - j) % W
            moved = pltpu.roll(own_flow, shift, 1) if shift else own_flow
            ok = jnp.logical_and(lane + (j - 3) >= 0, lane + (j - 3) < W)
            xx[pl.ds(j * 2 + k, n_flow, stride=16), :] = jnp.where(ok, moved, 0.0)
    xb[...] = xx[...].astype(BF)
    tgt[...] = jnp.zeros_like(tgt)
    for k in range(2):
        for y in range(TARGET_HALO):
            tgt[k : k + 1, y * W : (y + 1) * W] = above[8 * k + 6 + y : 8 * k + 7 + y, :]
            lo = (TARGET_HALO + n_rows + y) * W
            tgt[k : k + 1, lo : lo + W] = below[8 * k + 6 + y : 8 * k + 7 + y, :]
        for y in range(n_rows):
            lo = (TARGET_HALO + y) * W
            tgt[k : k + 1, lo : lo + W] = targets[k, y : y + 1, :].astype(F32)

    def one_row(y, carry):
        patch = xb[pl.ds(pl.multiple_of(y * 16, 16), 112), :]
        pre = lax.dot_general(patch, wf[...], TN, preferred_element_type=F32) + bias[2:3, :]
        value, slope = silu_pair(pre)
        d_flow[rows(y, 1, W), :] = slope
        store_stack(jf, y, jnp.where(inside_frame(n_rows, y - 3), value, 0.0), FWD)
        return carry

    lax.fori_loop(0, n_rows + 6, one_row, 0)


def hidden_kernel(
    n_rows, n_cols, n_tm,
    b_head, code, top, bot, jf, tgt, wc, w_joint, w_head, bias,
    error_out, jt, s3, d_motion, misc,
    c3, jm, err, hid, g_head, acc, wjm, wjf, square, wht,
):
    W = n_cols
    count = 2.0 * n_tm * lax.axis_size("space") * n_rows * n_cols
    slope_scale = frame_scale(n_tm, 2.0 / count)
    for i in range(3):
        for j in range(3):
            wjm[i, j * 128 : (j + 1) * 128, :] = w_joint[i, j, 0:128, :]
            wjf[i, j * 128 : (j + 1) * 128, :] = w_joint[i, j, 128:256, :]
    square[...] = jnp.zeros_like(square)
    square[:, 0:2] = w_head[...].astype(F32)
    head_t = square[...].T[0:16].astype(BF)
    for k in range(3):
        wht[16 * k : 16 * k + 16, :] = head_t
    C = wc.shape[2]
    body = n_rows * W

    def load_halo(y, carry):
        store_stack(c3, y, top[rows(y, 1, W), :].astype(F32), FWD)
        store_stack(c3, y + HALO + n_rows, bot[rows(y, 1, W), :].astype(F32), FWD)
        return carry

    def load_code(y, carry):
        store_stack(c3, y + HALO, code[rows(y, 1, W), :].astype(F32), FWD)
        return carry

    lax.fori_loop(0, HALO, load_halo, 0)
    lax.fori_loop(0, n_rows, load_code, 0)

    def motion_rows(b, carry):
        y = 2 * b
        pre = bias[1:2, :] + dot(c3[rows(y, 2, W), :], wc[0])
        pre = pre + dot(c3[rows(y + 1, 2, W), :], wc[1])
        pre = pre + dot(c3[rows(y + 2, 2, W), :], wc[2])
        for u in range(2):
            value, slope = silu_pair(pre[u * W : (u + 1) * W])
            d_motion[rows(y + u, 1, W), :] = slope
            store_stack(jm, y + u, jnp.where(inside_frame(n_rows, y + u - 3), value, 0.0), FWD)
        return carry

    lax.fori_loop(0, (n_rows + 6) // 2, motion_rows, 0)

    k_row = lax.broadcasted_iota(jnp.int32, (16, 2 * W), 0)
    b_col = jnp.where(k_row == 0, b_head[0], jnp.where(k_row == 1, b_head[1], 0.0))

    def hidden_rows(b, carry):
        y = 2 * b
        pre = bias[3:4, :] + dot(jm[rows(y, 2, W), :], wjm[0])
        pre = pre + dot(jf[rows(y, 2, W), :], wjf[0])
        for i in (1, 2):
            pre = pre + dot(jm[rows(y + i, 2, W), :], wjm[i])
            pre = pre + dot(jf[rows(y + i, 2, W), :], wjf[i])
        value, slope = silu_pair(pre)
        hidden = value.astype(BF)
        hid[rows(y, 2, W), :] = hidden
        pred = lax.dot_general(wht[0:16, :], hidden, NT, preferred_element_type=F32)
        error = pred + b_col - tgt[:, rows(y, 2, W)]
        err[:, rows(y, 2, W)] = error
        back = lax.dot_general(split3(error * slope_scale), wht[...], TN, preferred_element_type=F32) * slope
        for u in range(2):
            v = jnp.where(inside_frame(n_rows, y + u - 2), back[u * W : (u + 1) * W], 0.0)
            store_stack(s3, y + u, v, BWD)
        return carry

    lax.fori_loop(0, (n_rows + 4) // 2, hidden_rows, 0)

    acc[...] = jnp.zeros_like(acc)
    g_head[...] = jnp.zeros_like(g_head)

    def own_rows(b, carry):
        y = 2 * b
        g_head[...] += dot(split3(err[:, rows(y + 2, 2, W)] * slope_scale), hid[rows(y + 2, 2, W), :])
        part = s3[rows(y + 2, 2, W), C : 2 * C].astype(F32)
        acc[...] += jnp.sum(part.reshape(2 * W // 8, 8, C), axis=0)
        jt[0:C, rows(y, 2, W)] = jm[rows(y + 3, 2, W), C : 2 * C].T
        jt[C : 2 * C, rows(y, 2, W)] = jf[rows(y + 3, 2, W), C : 2 * C].T
        return carry

    lax.fori_loop(0, n_rows // 2, own_rows, 0)
    own = err[:, TARGET_HALO * W : TARGET_HALO * W + body]
    for k in range(2):
        for y in range(n_rows):
            error_out[k, y : y + 1, :] = own[k : k + 1, y * W : (y + 1) * W]
    g_b_head = jnp.sum(own * slope_scale, axis=1, keepdims=True)
    loss = jnp.sum(jnp.sum(own * own, axis=1, keepdims=True), axis=0, keepdims=True)
    loss = loss * frame_scale(n_tm, 1.0 / count)
    col = lax.broadcasted_iota(jnp.int32, (1, C), 1)
    tail = jnp.where(col == 0, loss, jnp.where(col == 1, g_b_head[0:1], jnp.where(col == 2, g_b_head[1:2], 0.0)))
    misc[0:3, :] = jnp.zeros((3, C), F32)
    misc[3:4, :] = jnp.sum(acc[...], axis=0, keepdims=True)
    misc[4:6, :] = g_head[0:2, :] + g_head[16:18, :] + g_head[32:34, :]
    misc[6:7, :] = tail
    misc[7:8, :] = jnp.zeros((1, C), F32)


def rest_kernel(
    n_rows, n_cols, at_misc,
    jt, s3, d_motion, d_flow, xb, vol, code, misc, wv, w_code, w_joint, bias,
    keep, send,
    m3, s_flow, s_code, acc, grads, wcb, wjb,
):
    W = n_cols
    C = code.shape[1]
    body = n_rows * W
    for i in range(3):
        for j in range(3):
            wcb[i, :, j * C : (j + 1) * C] = w_code[i, j]
            wjb[i, :, j * C : (j + 1) * C] = w_joint[i, j]

    def joint_slopes(b, carry):
        y = 2 * b
        sj = dot_nt(s3[rows(y + 2, 2, W), :], wjb[0])
        sj = sj + dot_nt(s3[rows(y + 1, 2, W), :], wjb[1])
        sj = sj + dot_nt(s3[rows(y, 2, W), :], wjb[2])
        for u in range(2):
            part = sj[u * W : (u + 1) * W]
            v = part[:, 0:C] * d_motion[rows(y + u + 2, 1, W), :]
            store_stack(m3, y + u, jnp.where(inside_frame(n_rows, y + u - 1), v, 0.0), BWD)
            s_flow[rows(y + u, 1, W), :] = (part[:, C:] * d_flow[rows(y + u + 2, 1, W), :]).astype(BF)
        return carry

    lax.fori_loop(0, (n_rows + 2) // 2, joint_slopes, 0)
    acc[...] = jnp.zeros_like(acc)

    def add_rows(k, v):
        acc[8 * k : 8 * k + 8, :] += jnp.sum(v.reshape(v.shape[0] // 8, 8, C), axis=0)

    def code_slopes(b, carry):
        y = 2 * b
        sc = dot_nt(m3[rows(y + 2, 2, W), :], wcb[0])
        sc = sc + dot_nt(m3[rows(y + 1, 2, W), :], wcb[1])
        sc = sc + dot_nt(m3[rows(y, 2, W), :], wcb[2])
        pre = lax.dot_general(vol[:, rows(y, 2, W)], wv[...], TN, preferred_element_type=F32) + bias[0:1, :]
        s_code[rows(y, 2, W), :] = (sc * silu_pair(pre)[1]).astype(BF)
        add_rows(0, s_code[rows(y, 2, W), :].astype(F32))
        add_rows(1, m3[rows(y + 1, 2, W), C : 2 * C].astype(F32))
        add_rows(2, s_flow[rows(y + 1, 2, W), :].astype(F32))
        return carry

    lax.fori_loop(0, n_rows // 2, code_slopes, 0)

    for i in range(3):
        g = dot(jt[...], s3[(3 - i) * W : (3 - i) * W + body, :])
        for j in range(3):
            at = (i * 3 + j) * 2 * C
            grads[at : at + 2 * C, :] = g[:, j * C : (j + 1) * C]
    code_t = code[...].T
    for i in range(3):
        g = dot(code_t, m3[(2 - i) * W : (2 - i) * W + body, :])
        for j in range(3):
            at = AT_CODE + (i * 3 + j) * C
            grads[at : at + C, :] = g[:, j * C : (j + 1) * C]
    grads[AT_VOLUME:AT_FLOW, :] = dot(vol[...], s_code[...])
    gf = jnp.zeros((112, C), F32)
    for y in range(n_rows):
        gf = gf + dot(xb[(y + 3) * 16 : (y + 3) * 16 + 112, :], s_flow[(y + 1) * W : (y + 2) * W, :])
    grads[AT_FLOW : AT_FLOW + 112, :] = gf
    if at_misc > AT_END:
        grads[AT_END:at_misc, :] = jnp.zeros((at_misc - AT_END, C), F32)
    for k in range(3):
        grads[at_misc + k : at_misc + k + 1, :] = jnp.sum(acc[8 * k : 8 * k + 8, :], axis=0, keepdims=True)
    grads[at_misc + 3 : at_misc + 8, :] = misc[3:8, :]
    grads[at_misc + 8 :, :] = jnp.zeros((grads.shape[0] - at_misc - 8, C), F32)
    half = keep.shape[0]
    core = lax.axis_index("tm") % 2
    keep[...] = pick(grads, core, half)
    send[...] = pick(grads, 1 - core, half)


VMEM = pl.BlockSpec(memory_space=pltpu.VMEM)
SMEM = pl.BlockSpec(memory_space=pltpu.SMEM)
ANY = pl.BlockSpec(memory_space=pl.ANY)


def bits_of(axis):
    bits = []
    bit = 1
    while bit < lax.axis_size(axis):
        bits.append((axis, bit))
        bit *= 2
    return bits


def trade(x, axis, bit):
    return lax.ppermute(x, axis, [(i, i ^ bit) for i in range(lax.axis_size(axis))])


def upper_of(axis, bit):
    return (lax.axis_index(axis) // bit) % 2


def three_terms(x, at, is_last):
    value = x[at : at + MISC_ROWS]
    mid = value - lax.reduce_precision(value, 8, 7)
    low = mid - lax.reduce_precision(mid, 8, 7)
    terms = jnp.concatenate([x[: at + MISC_ROWS], mid, low, x[at + 3 * MISC_ROWS :]])
    return jnp.where(is_last, terms, x).astype(BF)


def halving_reduce(x, steps, is_last):
    for axis, bit in steps:
        upper = upper_of(axis, bit)
        is_last = is_last * upper
        half = x.shape[0] // 2
        mine = lax.dynamic_slice_in_dim(x, upper * half, half, 0)
        other = lax.dynamic_slice_in_dim(x, (1 - upper) * half, half, 0)
        x = mine + trade(other, axis, bit)
    x = three_terms(x, 0, is_last == 1)
    for axis, bit in steps[::-1]:
        got = trade(x, axis, bit)
        x = jnp.where(upper_of(axis, bit) == 0, jnp.concatenate([x, got]), jnp.concatenate([got, x]))
    return x


def pick(ref, which, half):
    return ref[pl.ds(pl.multiple_of(which * half, 8), half), :]


def first_split(bits, keep, got, a_keep, a_send, b_keep, b_send, total):
    quarter = a_keep.shape[0]
    total[...] = keep[...] + got[...]
    for at, (k, s, bit) in enumerate(((a_keep, a_send, bits[1]), (b_keep, b_send, bits[2]))):
        k[...] = total[pl.ds(pl.multiple_of((2 * at + bit) * quarter, 8), quarter), :]
        s[...] = total[pl.ds(pl.multiple_of((2 * at + 1 - bit) * quarter, 8), quarter), :]


def second_split(bits, a_keep, a_got, b_keep, b_got, a_mine, a_send, b_mine, b_send, total):
    half = a_mine.shape[0]
    for keep, got, mine, send, bit in (
        (a_keep, a_got, a_mine, a_send, bits[2]),
        (b_keep, b_got, b_mine, b_send, bits[1]),
    ):
        total[...] = keep[...] + got[...]
        mine[...] = pick(total, bit, half)
        send[...] = pick(total, 1 - bit, half)


def third_split(bits, a_keep, a_got, b_keep, b_got, keep, send, total):
    n = a_keep.shape[0]
    total[0:n, :] = a_keep[...] + a_got[...]
    total[n : 2 * n, :] = b_keep[...] + b_got[...]
    keep[...] = pick(total, bits[3], n)
    send[...] = pick(total, 1 - bits[3], n)


def last_sum(at, bits, keep, got, out, total):
    total[...] = keep[...] + got[...]
    value = total[at : at + MISC_ROWS, :]
    mid = value - value.astype(BF).astype(F32)
    low = mid - mid.astype(BF).astype(F32)
    is_last = bits[0] + bits[1] + bits[2] + bits[3] == 4
    total[at + MISC_ROWS : at + 2 * MISC_ROWS, :] = jnp.where(is_last, mid, total[at + MISC_ROWS : at + 2 * MISC_ROWS, :])
    total[at + 2 * MISC_ROWS : at + 3 * MISC_ROWS, :] = jnp.where(
        is_last, low, total[at + 2 * MISC_ROWS : at + 3 * MISC_ROWS, :]
    )
    out[...] = total[...].astype(BF)


def first_merge(bits, mine, got, a_out, b_out):
    first = bits[3] == 0
    a_out[...] = jnp.where(first, mine[...], got[...])
    b_out[...] = jnp.where(first, got[...], mine[...])


def pair_merge(x_first, bits, a_mine, a_got, b_mine, b_got, a_out, b_out):
    n = a_mine.shape[0]
    a_bit, b_bit = (bits[1], bits[2]) if x_first else (bits[2], bits[1])
    for mine, got, out, bit in ((a_mine, a_got, a_out, a_bit), (b_mine, b_got, b_out, b_bit)):
        out[pl.ds(pl.multiple_of(bit * n, 16), n), :] = mine[...]
        out[pl.ds(pl.multiple_of((1 - bit) * n, 16), n), :] = got[...]


def join_merge(bits, a_mine, a_got, b_mine, b_got, out):
    n = a_mine.shape[0]
    for at, (mine, got, bit) in enumerate(((a_mine, a_got, bits[1]), (b_mine, b_got, bits[2]))):
        out[pl.ds(pl.multiple_of((2 * at + bit) * n, 16), n), :] = mine[...]
        out[pl.ds(pl.multiple_of((2 * at + 1 - bit) * n, 16), n), :] = got[...]


def paired_reduce(bits, keep, got, at_misc, shape):
    half, C = keep.shape
    x, z, far_z = ("tm", 2), ("space", 1), ("space", 2)

    def stage(body, name, n_out, n, dtype, scratch, *args):
        out = (shape(n, C, dtype=dtype),) * n_out
        return call(
            body, name, out, [SMEM] + [VMEM] * len(args),
            [pltpu.VMEM((scratch, C), F32)] if scratch else [], 10_000_000, bits, *args,
        )

    ak, as_, bk, bs = stage(first_split, "split1", 4, half // 4, F32, half, keep, got)
    ag, bg = trade(as_, *x), trade(bs, *z)
    ak, as_, bk, bs = stage(second_split, "split2", 4, half // 8, F32, half // 4, ak, ag, bk, bg)
    ag, bg = trade(as_, *z), trade(bs, *x)
    keep, send = stage(third_split, "split3", 2, half // 8, F32, half // 4, ak, ag, bk, bg)
    got = trade(send, *far_z)
    chunk = half // 8
    (y,) = stage(
        functools.partial(last_sum, at_misc - (2 * half - chunk)), "last", 1, chunk, BF, chunk, keep, got
    )
    a, b = stage(first_merge, "merge1", 2, chunk, BF, 0, y, trade(y, *far_z))
    a, b = stage(
        functools.partial(pair_merge, False), "merge2", 2, half // 4, BF, 0, a, trade(a, *z), b, trade(b, *x)
    )
    (out,) = stage(join_merge, "merge3", 1, half, BF, 0, a, trade(a, *x), b, trade(b, *z))
    return out


def finish_kernel(at_misc, bits, mine, other, joint, code, volume, flow, misc, full):
    half, C = mine.shape
    full[pl.ds(pl.multiple_of(bits[0] * half, 16), half), :] = mine[...]
    full[pl.ds(pl.multiple_of((1 - bits[0]) * half, 16), half), :] = other[...]
    for i in range(3):
        for j in range(3):
            at = (i * 3 + j) * 2 * C
            joint[i, j, :, :] = full[at : at + 2 * C, :].astype(F32)
            at = AT_CODE + (i * 3 + j) * C
            code[i, j, :, :] = full[at : at + C, :].astype(F32)
    parts = full[AT_VOLUME:AT_FLOW, :].astype(F32)
    for half_at in range(2):
        for dy in range(SIDE):
            at, to = half_at * HALF, half_at * OFF + dy * SIDE
            volume[to : to + 8, :] = parts[at + 8 * dy : at + 8 * dy + 8]
            volume[to + 8 : to + 9, :] = parts[at + 72 + dy : at + 73 + dy]
    for i in range(7):
        part = full[AT_FLOW + 16 * i : AT_FLOW + 16 * i + 16, :].astype(F32)
        for j in range(7):
            flow[i, j, :, :] = part[2 * j : 2 * j + 2]
    terms = full[at_misc : at_misc + 32, :].astype(F32)
    misc[...] = terms[0:8] + terms[8:16] + terms[16:24]


def call(body, name, out_shape, in_specs, scratch, flops, *args):
    held = [
        pltpu.with_memory_space_constraint(x, pltpu.VMEM) if spec is VMEM else x
        for x, spec in zip(args, in_specs, strict=True)
    ]
    return pl.pallas_call(
        body,
        out_shape=out_shape,
        in_specs=in_specs,
        out_specs=jax.tree.map(lambda _: VMEM, out_shape),
        scratch_shapes=scratch,
        cost_estimate=pl.CostEstimate(flops=flops, bytes_accessed=flops // 300, transcendentals=0),
        compiler_params=pltpu.CompilerParams(vmem_limit_bytes=16 << 20),
        name=name,
    )(*held)


def local(
    features, pair_order, flow_now, targets, w_volume, b_volume, w_code, b_code,
    w_flow, b_flow, w_joint, b_joint, w_head, b_head,
):
    own = features[0]
    n_rows, n_cols, n_chan = own.shape
    n_code = w_code.shape[3]
    W, C = n_cols, n_code
    body = n_rows * n_cols
    halo = HALO * n_cols
    n_tm, n_space = lax.axis_size("tm"), lax.axis_size("space")
    flat = own.reshape(body, n_chan)
    both = ("tm", "space")

    def route(partner, ds):
        pairs = []
        for t in range(n_tm):
            for s in range(n_space):
                if 0 <= partner(t) < n_tm and 0 <= s + ds < n_space:
                    pairs.append((t * n_space + s, partner(t) * n_space + s + ds))
        return pairs

    def near(t):
        return t + 1 - 2 * (t % 2)

    def far(t):
        return t - 1 + 2 * (t % 2)

    first, last = flat[:halo], flat[body - halo :]
    far_mid = lax.ppermute(flat, both, route(far, 0))
    far_top = lax.ppermute(last, both, route(far, 1))
    far_bot = lax.ppermute(first, both, route(far, -1))
    near_top = lax.ppermute(last, both, route(near, 1))
    near_bot = lax.ppermute(first, both, route(near, -1))
    near_mid = lax.ppermute(flat, both, route(near, 0))

    bias = jnp.stack([b_volume, b_code, b_flow, b_joint])
    flow = flow_now[0]

    def shape(*dims, dtype=BF):
        return pltpu.VMEM(dims, dtype)

    def result(*dims):
        return jax.ShapeDtypeStruct(dims, F32)

    def correlate(mid, top, bot, name):
        return call(
            functools.partial(correlate_kernel, n_rows, n_cols), name,
            shape(HALF, body), [VMEM] * 4,
            [pltpu.VMEM((body + 2 * halo, n_chan), BF), pltpu.VMEM((HALF, 2 * W), F32)],
            4_000_000_000,
            flat, mid, top, bot,
        )

    near_vol = correlate(near_mid, near_top, near_bot, "near")
    far_vol = correlate(far_mid, far_top, far_bot, "far")
    vol, code, up, dn, wv = call(
        functools.partial(code_kernel, n_rows, n_cols), "code",
        (
            shape(2 * HALF, body), shape(body, C), shape(halo + 16, C), shape(halo + 16, C),
            shape(2 * HALF, C),
        ),
        [SMEM] + [VMEM] * 6, [pltpu.VMEM((2 * HALF, C), F32), pltpu.VMEM((16, W), F32)], 500_000_000,
        pair_order, near_vol, far_vol, w_volume, bias, flow, targets[0],
    )
    top = lax.ppermute(dn, "space", [(s, s + 1) for s in range(n_space - 1)])
    bot = lax.ppermute(up, "space", [(s + 1, s) for s in range(n_space - 1)])

    jf, d_flow, xb, tgt = call(
        functools.partial(flow_kernel, n_rows, n_cols), "flow",
        (
            shape((n_rows + 6) * W, 3 * C),
            shape((n_rows + 6) * W, C, dtype=F32),
            shape((n_rows + 12) * 16, W),
            shape(16, (n_rows + 4) * W, dtype=F32),
        ),
        [VMEM] * 6,
        [
            pltpu.VMEM((24, W), F32),
            pltpu.VMEM(((n_rows + 12) * 16, W), F32),
            pltpu.VMEM((112, C), F32),
            pltpu.VMEM((112, C), BF),
        ],
        1_000_000_000,
        top, bot, flow, targets[0], w_flow, bias,
    )
    flow_error, jt, s3, d_motion, misc = call(
        functools.partial(hidden_kernel, n_rows, n_cols, n_tm), "hidden",
        (
            result(2, n_rows, W),
            shape(2 * C, body),
            shape((n_rows + 4) * W, 3 * C),
            shape((n_rows + 6) * W, C, dtype=F32),
            shape(MISC_ROWS, C, dtype=F32),
        ),
        [SMEM] + [VMEM] * 9,
        [
            pltpu.VMEM(((n_rows + 8) * W, 3 * C), BF),
            pltpu.VMEM(((n_rows + 6) * W, 3 * C), BF),
            pltpu.VMEM((16, (n_rows + 4) * W), F32),
            pltpu.VMEM(((n_rows + 4) * W, C), BF),
            pltpu.VMEM((48, C), F32),
            pltpu.VMEM((8, C), F32),
            pltpu.VMEM((3, 3 * C, C), BF),
            pltpu.VMEM((3, 3 * C, C), BF),
            pltpu.VMEM((C, C), F32),
            pltpu.VMEM((48, C), BF),
        ],
        4_000_000_000,
        b_head, code, top, bot, jf, tgt, w_code.reshape(3, 3 * C, C), w_joint, w_head, bias,
    )
    n_dev = n_tm * n_space
    paired = n_tm == 4 and n_space == 4
    if paired:
        grad_rows, at_misc = 3840, AT_END
    else:
        chunk = -(-max(pl.cdiv(AT_END, n_dev - 1), 3 * MISC_ROWS) // 16) * 16
        grad_rows, at_misc = n_dev * chunk, (n_dev - 1) * chunk
    keep, send = call(
        functools.partial(rest_kernel, n_rows, n_cols, at_misc), "rest",
        (shape(grad_rows // 2, C, dtype=F32), shape(grad_rows // 2, C, dtype=F32)),
        [VMEM] * 12,
        [
            pltpu.VMEM(((n_rows + 2) * W, 3 * C), BF),
            pltpu.VMEM(((n_rows + 2) * W, C), BF),
            pltpu.VMEM((body, C), BF),
            pltpu.VMEM((24, C), F32),
            pltpu.VMEM((grad_rows, C), F32),
            pltpu.VMEM((3, C, 3 * C), BF),
            pltpu.VMEM((3, 2 * C, 3 * C), BF),
        ],
        3_000_000_000,
        jt, s3, d_motion, d_flow, xb, vol, code, misc, wv, w_code, w_joint, bias,
    )
    core = ("tm", 1)
    got = trade(send, *core)
    bits = jnp.stack([upper_of("tm", 1), upper_of("tm", 2), upper_of("space", 1), upper_of("space", 2)])
    bits = bits.astype(jnp.int32)
    if paired:
        mine = paired_reduce(bits, keep, got, at_misc, shape)
    else:
        mine = halving_reduce(keep + got, bits_of("tm")[1:] + bits_of("space"), upper_of(*core))
    other = trade(mine, *core)
    outs = call(
        functools.partial(finish_kernel, at_misc), "finish",
        (
            result(3, 3, 2 * C, C),
            result(3, 3, C, C),
            result(2 * OFF, C),
            result(7, 7, 2, C),
            result(MISC_ROWS, C),
        ),
        [SMEM] + [VMEM] * 2, [pltpu.VMEM((grad_rows, C), BF)], 100_000_000,
        bits, mine, other,
    )
    joint, g_code, g_volume, g_flow, misc = outs
    return (
        misc[6, 0:1], flow_error[None], g_volume, misc[0], g_code, misc[1],
        g_flow, misc[2], joint, misc[3], misc[4:6].T, misc[6, 1:3],
    )


def solution(mesh):
    placed = (
        P(("groups", "tm"), "space", None, None),
        P(("groups", "tm")),
        P(("groups", "tm"), None, "space", None),
        P(("groups", "tm"), None, "space", None),
    ) + (P(),) * 10
    return jax.shard_map(
        local,
        mesh=mesh,
        in_specs=placed,
        out_specs=(
            P("groups"),
            P(("groups", "tm"), None, "space", None),
            P("groups", None),
            P("groups"),
            P("groups", None, None, None),
            P("groups"),
            P("groups", None, None, None),
            P("groups"),
            P("groups", None, None, None),
            P("groups"),
            P("groups", None),
            P("groups"),
        ),
        check_vma=False,
    )
```

time: 138 us -> 113 us (0.82)
  local copies, waits for them, and re-layouts: 15.8 us -> 5.43 us
  waiting for transfers between devices: 55.1 us -> 45.7 us
  other arithmetic: 6.22 us -> 0.79 us
  Pallas kernels: 27.9 us -> 30.7 us
  starting transfers between devices: 30.5 us -> 28.2 us
    ppermute x16 -> x20, waiting for transfers between devices: 55.1 us -> 45.7 us  [the longest x12 34.6 us: trade(): lax.ppermute(x, axis, [(i, i ^ bit) for i in range(lax.axis_size(axis))])]
    slice x6 -> x0, local copies, waits for them, and re-layouts: 3.88 us -> none  [the longest x1 1.35 us: local(): flow[:, n_rows - FLOW_HALO:]]
    pallas_call x2 -> x14, Pallas kernels: 27.9 us -> 30.7 us  [call(): pl.pallas_call(body, out_shape=out_shape, in_specs=in_specs, out_specs=ja...]
    ppermute x16 -> x20, starting transfers between devices: 30.5 us -> 28.2 us  [the longest x12 7.51 us: trade(): lax.ppermute(x, axis, [(i, i ^ bit) for i in range(lax.axis_size(axis))])]
    reshape x4 -> x0, local copies, waits for them, and re-layouts: 2.13 us -> none  [the longest x1 0.8 us: local(): w_volume.reshape(2, OFF, n_code)]
    transpose x2 -> x0, local copies, waits for them, and re-layouts: 1.96 us -> none  [the longest x1 1.06 us: local(): wjb = w_joint.transpose(0, 1, 3, 2).reshape(3, 3 * n_code, 2 * n_code)]
    dynamic_slice x4 -> x0, local copies, waits for them, and re-layouts: 1.49 us -> none  [reduce_all(): send = lax.dynamic_slice_in_dim(x, (1 - upper) * half, half, 0)]
    add x4 -> x0, other arithmetic: 1.4 us -> none  [reduce_all(): x = keep + lax.ppermute(send, axis, route)]
  transfers between devices with their start and end apart: 16 -> 20, of which waited for: 9 -> 15; matrix products, arithmetic and copies ran while one was open for 8% -> 2% of each run, Pallas kernels for 0% -> 2%
where the time goes in v2:
time: 113 us
  waiting for transfers between devices  45.7 us (40%)
  Pallas kernels  30.7 us (27%)
  starting transfers between devices  28.2 us (25%)
  local copies, waits for them, and re-layouts  5.43 us (5%)
  between operations  1.68 us (1%)
    ppermute x12, waiting for transfers between devices, trade(): lax.ppermute(x, axis, [(i, i ^ bit) for i in range(lax.axis_size(axis))])  34.6 us
    pallas_call x14, Pallas kernels, call(): pl.pallas_call(body, out_shape=out_shape, in_specs=in_specs, out_specs=ja...  30.7 us
    ppermute x12, starting transfers between devices, trade(): lax.ppermute(x, axis, [(i, i ^ bit) for i in range(lax.axis_size(axis))])  7.51 us
    ppermute x1, starting transfers between devices, local(): near_mid = lax.ppermute(flat, both, route(near, 0))  7.22 us
    ppermute x1, starting transfers between devices, local(): near_top = lax.ppermute(last, both, route(near, 1))  5.35 us
    ppermute x1, waiting for transfers between devices, local(): near_bot = lax.ppermute(first, both, route(near, -1))  4.79 us
    ppermute x1, waiting for transfers between devices, local(): bot = lax.ppermute(up, 'space', [(s + 1, s) for s in range(n_space - 1)])  4.12 us
    ppermute x1, starting transfers between devices, local(): top = lax.ppermute(dn, 'space', [(s, s + 1) for s in range(n_space - 1)])  3.47 us
  transfers between devices with their start and end apart: 20, of which 15 were waited for; matrix products, arithmetic and copies ran while one was open for 2% of the time, Pallas kernels for 2%

profile of v2, /device:TPU:0, one launch (start us, length us, event | category | flops | bytes accessed | tf_op | source)
XLA Modules:
  0.0 112.6 jit_solution(11809768921741542209)
XLA Ops:
  3.8 7.2 %collective-permute-start = (bf16[1024,256]{1,0:T(8,128)(2,1)}, bf16[1024,256]{1,0:T(8,128)(2,1)S(1)}, u32[]{:S(2)}, u32[]{:S(2)}) collective-permute-start(bf16[1024,256]{1,0:T(8,128)(2,1)} %bitcast.29), channel_id=1, source_target_pairs={{0,4},{1,5},{2,6},{3,7},{4,0},{5,1},{6,2},{7,3},{8,12},{9,13},{10,... | collective-permute-start | bytes 1572872 | tf_op jit(solution)/shard_map/ppermute | solution.py:594
  11.0 5.4 %collective-permute-start.1 = (bf16[512,256]{1,0:T(8,128)(2,1)S(1)}, bf16[512,256]{1,0:T(8,128)(2,1)S(1)}, u32[]{:S(2)}, u32[]{:S(2)}) collective-permute-start(bf16[512,256]{1,0:T(8,128)(2,1)S(1)} %bitcast.40), channel_id=1, source_target_pairs={{0,5},{1,6},{2,7},{4,1},{5,2},{6,3},{8,13},{9,14},{10,15},{12,9},{... | collective-permute-start | bytes 786440 | tf_op jit(solution)/shard_map/ppermute | solution.py:592
  20.1 2.4 %far.1.far_vol = bf16[96,1024]{1,0:T(8,128)(2,1)S(1)} custom-call(bf16[1024,256]{1,0:T(8,128)(2,1)S(1)} %bitcast.30, bf16[1024,256]{1,0:T(8,128)(2,1)S(1)} %collective-permute-done.3.mid, bf16[512,256]{1,0:T(8,128)(2,1)S(1)} %collective-permute-done.4.top, bf16[512,256]{1,0:T(8,128)(2,1)S(1)} %collective-permute-done.5.bot), custom_call_target="tpu_custom_call" | custom-call | flops 4000000000 | bytes 13333333 | tf_op jit(solution)/shard_map/far/pallas_call | solution.py:548
  22.8 4.8 %collective-permute-done.2.bot = bf16[512,256]{1,0:T(8,128)(2,1)S(1)} collective-permute-done((bf16[512,256]{1,0:T(8,128)(2,1)S(1)}, bf16[512,256]{1,0:T(8,128)(2,1)S(1)}, u32[]{:S(2)}, u32[]{:S(2)}) %collective-permute-start.2) | collective-permute-done | bytes 262176 | tf_op jit(solution)/shard_map/ppermute | solution.py:593
  27.6 2.4 %near.1.near_vol = bf16[96,1024]{1,0:T(8,128)(2,1)S(1)} custom-call(bf16[1024,256]{1,0:T(8,128)(2,1)S(1)} %bitcast.31, bf16[1024,256]{1,0:T(8,128)(2,1)S(1)} %collective-permute-done.mid, bf16[512,256]{1,0:T(8,128)(2,1)S(1)} %collective-permute-done.1.top, bf16[512,256]{1,0:T(8,128)(2,1)S(1)} %collective-permute-done.2.bot), custom_call_target="tpu_custom_call" | custom-call | flops 4000000000 | bytes 13333333 | tf_op jit(solution)/shard_map/near/pallas_call | solution.py:548
  31.2 3.5 %collective-permute-start.6 = (bf16[528,128]{1,0:T(8,128)(2,1)S(1)}, bf16[528,128]{1,0:T(8,128)(2,1)S(1)}, u32[]{:S(2)}, u32[]{:S(2)}) collective-permute-start(bf16[528,128]{1,0:T(8,128)(2,1)S(1)} %get-tuple-element.48), channel_id=1, source_target_pairs={{0,1},{1,2},{2,3},{4,5},{5,6},{6,7},{8,9},{9,10},{10,11},{12,13},{... | collective-permute-start | bytes 405512 | tf_op jit(solution)/shard_map/ppermute | solution.py:625
  34.7 1.3 %collective-permute-start.7 = (bf16[528,128]{1,0:T(8,128)(2,1)S(1)}, bf16[528,128]{1,0:T(8,128)(2,1)S(1)}, u32[]{:S(2)}, u32[]{:S(2)}) collective-permute-start(bf16[528,128]{1,0:T(8,128)(2,1)S(1)} %get-tuple-element.49), channel_id=1, source_target_pairs={{1,0},{2,1},{3,2},{5,4},{6,5},{7,6},{9,8},{10,9},{11,10},{13,12},{... | collective-permute-start | bytes 405512 | tf_op jit(solution)/shard_map/ppermute | solution.py:626
  36.1 2.0 %collective-permute-done.6.top = bf16[528,128]{1,0:T(8,128)(2,1)S(1)} collective-permute-done((bf16[528,128]{1,0:T(8,128)(2,1)S(1)}, bf16[528,128]{1,0:T(8,128)(2,1)S(1)}, u32[]{:S(2)}, u32[]{:S(2)}) %collective-permute-start.6) | collective-permute-done | bytes 135200 | tf_op jit(solution)/shard_map/ppermute | solution.py:625
  38.1 4.1 %collective-permute-done.7.bot = bf16[528,128]{1,0:T(8,128)(2,1)S(1)} collective-permute-done((bf16[528,128]{1,0:T(8,128)(2,1)S(1)}, bf16[528,128]{1,0:T(8,128)(2,1)S(1)}, u32[]{:S(2)}, u32[]{:S(2)}) %collective-permute-start.7) | collective-permute-done | bytes 135200 | tf_op jit(solution)/shard_map/ppermute | solution.py:626
  42.2 3.2 %flow.1 = (bf16[1792,384]{1,0:T(8,128)(2,1)S(1)}, f32[1792,128]{1,0:T(8,128)S(1)}, bf16[320,128]{1,0:T(8,128)(2,1)S(1)}, f32[16,1536]{1,0:T(8,128)S(1)}) custom-call(bf16[528,128]{1,0:T(8,128)(2,1)S(1)} %collective-permute-done.6.top, bf16[528,128]{1,0:T(8,128)(2,1)S(1)} %collective-permute-done.7.bot, bf16[2,8,128]{2,1,0:T(8,128)(2,1)S(1)} %bitcast.36, ...), custom_call_target="tpu_custom_call" | custom-call | flops 1000000000 | bytes 3333333 | tf_op jit(solution)/shard_map/flow/pallas_call | solution.py:548
  45.4 9.7 %hidden.1 = (f32[2,8,128]{2,1,0:T(8,128)}, bf16[256,1024]{1,0:T(8,128)(2,1)S(1)}, bf16[1536,384]{1,0:T(8,128)(2,1)S(1)}, f32[1792,128]{1,0:T(8,128)S(1)}, f32[8,128]{1,0:T(8,128)S(1)}) custom-call(f32[2]{0:T(128)S(1)} %copy-done.7, bf16[1024,128]{1,0:T(8,128)(2,1)S(1)} %get-tuple-element.47.code, bf16[528,128]{1,0:T(8,128)(2,1)S(1)} %collective-permute-done.6.top, ...), custom_call_target="tpu_custom_call" | custom-call | flops 4000000000 | bytes 13333333 | tf_op jit(solution)/shard_map/hidden/pallas_call | solution.py:548
  56.1 5.9 %rest.1 = (f32[1920,128]{1,0:T(8,128)S(1)}, f32[1920,128]{1,0:T(8,128)S(1)}) custom-call(bf16[256,1024]{1,0:T(8,128)(2,1)S(1)} %get-tuple-element.52.jt, bf16[1536,384]{1,0:T(8,128)(2,1)S(1)} %get-tuple-element.53.s3, f32[1792,128]{1,0:T(8,128)S(1)} %get-tuple-element.54.d_motion, f32[1792,128]{1,0:T(8,128)S(1)} %get-tuple-element.55.d_flow, ...), custom_call_target="tpu_custom_call" | custom-call | flops 3000000000 | bytes 10000000 | tf_op jit(solution)/shard_map/rest/pallas_call | solution.py:548
  62.2 2.4 %collective-permute-done.8.got = f32[1920,128]{1,0:T(8,128)S(1)} collective-permute-done((f32[1920,128]{1,0:T(8,128)S(1)}, f32[1920,128]{1,0:T(8,128)S(1)}, u32[]{:S(2)}, u32[]{:S(2)}) %collective-permute-start.8) | collective-permute-done | bytes 983072 | tf_op jit(solution)/shard_map/ppermute | solution.py:395
  65.3 1.6 %collective-permute-start.10 = (f32[480,128]{1,0:T(8,128)S(1)}, f32[480,128]{1,0:T(8,128)S(1)}, u32[]{:S(2)}, u32[]{:S(2)}) collective-permute-start(f32[480,128]{1,0:T(8,128)S(1)} %get-tuple-element.65), channel_id=1, source_target_pairs={{0,1},{1,0},{2,3},{3,2},{4,5},{5,4},{6,7},{7,6},{8,9},{9,8},{10,11... | collective-permute-start | bytes 737288 | tf_op jit(solution)/shard_map/ppermute | solution.py:395
  67.4 6.0 %collective-permute-done.10.b_got = f32[480,128]{1,0:T(8,128)S(1)} collective-permute-done((f32[480,128]{1,0:T(8,128)S(1)}, f32[480,128]{1,0:T(8,128)S(1)}, u32[]{:S(2)}, u32[]{:S(2)}) %collective-permute-start.10) | collective-permute-done | bytes 245792 | tf_op jit(solution)/shard_map/ppermute | solution.py:395
  76.4 3.9 %collective-permute-done.11.a_got = f32[240,128]{1,0:T(8,128)S(1)} collective-permute-done((f32[240,128]{1,0:T(8,128)S(1)}, f32[240,128]{1,0:T(8,128)S(1)}, u32[]{:S(2)}, u32[]{:S(2)}) %collective-permute-start.11) | collective-permute-done | bytes 122912 | tf_op jit(solution)/shard_map/ppermute | solution.py:395
  81.3 1.3 %collective-permute-start.13 = (f32[240,128]{1,0:T(8,128)S(1)}, f32[240,128]{1,0:T(8,128)S(1)}, u32[]{:S(2)}, u32[]{:S(2)}) collective-permute-start(f32[240,128]{1,0:T(8,128)S(1)} %get-tuple-element.71), channel_id=1, source_target_pairs={{0,2},{1,3},{2,0},{3,1},{4,6},{5,7},{6,4},{7,5},{8,10},{9,11},{10,... | collective-permute-start | bytes 368648 | tf_op jit(solution)/shard_map/ppermute | solution.py:395
  82.7 5.8 %collective-permute-done.13.got = f32[240,128]{1,0:T(8,128)S(1)} collective-permute-done((f32[240,128]{1,0:T(8,128)S(1)}, f32[240,128]{1,0:T(8,128)S(1)}, u32[]{:S(2)}, u32[]{:S(2)}) %collective-permute-start.13) | collective-permute-done | bytes 122912 | tf_op jit(solution)/shard_map/ppermute | solution.py:395
  89.2 5.6 %collective-permute-done.14.got = bf16[240,128]{1,0:T(8,128)(2,1)S(1)} collective-permute-done((bf16[240,128]{1,0:T(8,128)(2,1)S(1)}, bf16[240,128]{1,0:T(8,128)(2,1)S(1)}, u32[]{:S(2)}, u32[]{:S(2)}) %collective-permute-start.14) | collective-permute-done | bytes 61472 | tf_op jit(solution)/shard_map/ppermute | solution.py:395
  96.0 4.1 %collective-permute-done.15.a_got = bf16[240,128]{1,0:T(8,128)(2,1)S(1)} collective-permute-done((bf16[240,128]{1,0:T(8,128)(2,1)S(1)}, bf16[240,128]{1,0:T(8,128)(2,1)S(1)}, u32[]{:S(2)}, u32[]{:S(2)}) %collective-permute-start.15) | collective-permute-done | bytes 61472 | tf_op jit(solution)/shard_map/ppermute | solution.py:395
  101.1 1.7 %collective-permute-start.18 = (bf16[480,128]{1,0:T(8,128)(2,1)S(1)}, bf16[480,128]{1,0:T(8,128)(2,1)S(1)}, u32[]{:S(2)}, u32[]{:S(2)}) collective-permute-start(bf16[480,128]{1,0:T(8,128)(2,1)S(1)} %get-tuple-element.75.b_mine), channel_id=1, source_target_pairs={{0,1},{1,0},{2,3},{3,2},{4,5},{5,4},{6,7},{7,6},{8,9},{9,8},{10,11... | collective-permute-start | bytes 368648 | tf_op jit(solution)/shard_map/ppermute | solution.py:395
  102.8 2.9 %collective-permute-done.17.a_got = bf16[480,128]{1,0:T(8,128)(2,1)S(1)} collective-permute-done((bf16[480,128]{1,0:T(8,128)(2,1)S(1)}, bf16[480,128]{1,0:T(8,128)(2,1)S(1)}, u32[]{:S(2)}, u32[]{:S(2)}) %collective-permute-start.17) | collective-permute-done | bytes 122912 | tf_op jit(solution)/shard_map/ppermute | solution.py:395
  106.6 1.9 %collective-permute-done.19.other = bf16[1920,128]{1,0:T(8,128)(2,1)S(1)} collective-permute-done((bf16[1920,128]{1,0:T(8,128)(2,1)S(1)}, bf16[1920,128]{1,0:T(8,128)(2,1)S(1)}, u32[]{:S(2)}, u32[]{:S(2)}) %collective-permute-start.19) | collective-permute-done | bytes 491552 | tf_op jit(solution)/shard_map/ppermute | solution.py:395
  108.5 1.9 %finish.1 = (f32[3,3,256,128]{3,2,1,0:T(8,128)}, f32[3,3,128,128]{3,2,1,0:T(8,128)}, f32[162,128]{1,0:T(8,128)}, f32[7,7,2,128]{3,2,1,0:T(2,128)}, f32[8,128]{1,0:T(8,128)S(1)}) custom-call(s32[4]{0:T(128)S(1)} %pad_add_fusion.bits, bf16[1920,128]{1,0:T(8,128)(2,1)S(1)} %merge3.1.mine, bf16[1920,128]{1,0:T(8,128)(2,1)S(1)} %collective-permute-done.19.other), custom_call_target="tpu_custom_call" | custom-call | flops 100000000 | bytes 333333 | tf_op jit(solution)/shard_map/finish/pallas_call | solution.py:548
  (60 shorter events, 20.0 us)
Async XLA Ops:
  0.6 18.4 %collective-permute-start.3 = (bf16[1024,256]{1,0:T(8,128)(2,1)}, bf16[1024,256]{1,0:T(8,128)(2,1)S(1)}, u32[]{:S(2)}, u32[]{:S(2)}) collective-permute-start(bf16[1024,256]{1,0:T(8,128)(2,1)} %bitcast.28), channel_id=1, source_target_pairs={{4,8},{5,9},{6,10},{7,11},{8,4},{9,5},{10,6},{11,7},{20,24},{21,25... | collective-permute-start | bytes 1572872 | tf_op jit(solution)/shard_map/ppermute | solution.py:589
  2.4 15.3 %collective-permute-start.4 = (bf16[512,256]{1,0:T(8,128)(2,1)S(1)}, bf16[512,256]{1,0:T(8,128)(2,1)S(1)}, u32[]{:S(2)}, u32[]{:S(2)}) collective-permute-start(bf16[512,256]{1,0:T(8,128)(2,1)S(1)} %bitcast.39), channel_id=1, source_target_pairs={{4,9},{5,10},{6,11},{8,5},{9,6},{10,7},{20,25},{21,26},{22,27},{24... | collective-permute-start | bytes 786440 | tf_op jit(solution)/shard_map/ppermute | solution.py:590
  3.1 15.9 %collective-permute-start.5 = (bf16[512,256]{1,0:T(8,128)(2,1)S(1)}, bf16[512,256]{1,0:T(8,128)(2,1)S(1)}, u32[]{:S(2)}, u32[]{:S(2)}) collective-permute-start(bf16[512,256]{1,0:T(8,128)(2,1)S(1)} %bitcast.37), channel_id=1, source_target_pairs={{5,8},{6,9},{7,10},{9,4},{10,5},{11,6},{21,24},{22,25},{23,26},{25... | collective-permute-start | bytes 786440 | tf_op jit(solution)/shard_map/ppermute | solution.py:591
  3.8 23.8 %collective-permute-start = (bf16[1024,256]{1,0:T(8,128)(2,1)}, bf16[1024,256]{1,0:T(8,128)(2,1)S(1)}, u32[]{:S(2)}, u32[]{:S(2)}) collective-permute-start(bf16[1024,256]{1,0:T(8,128)(2,1)} %bitcast.29), channel_id=1, source_target_pairs={{0,4},{1,5},{2,6},{3,7},{4,0},{5,1},{6,2},{7,3},{8,12},{9,13},{10,... | collective-permute-start | bytes 1572872 | tf_op jit(solution)/shard_map/ppermute | solution.py:594
  11.0 11.8 %collective-permute-start.1 = (bf16[512,256]{1,0:T(8,128)(2,1)S(1)}, bf16[512,256]{1,0:T(8,128)(2,1)S(1)}, u32[]{:S(2)}, u32[]{:S(2)}) collective-permute-start(bf16[512,256]{1,0:T(8,128)(2,1)S(1)} %bitcast.40), channel_id=1, source_target_pairs={{0,5},{1,6},{2,7},{4,1},{5,2},{6,3},{8,13},{9,14},{10,15},{12,9},{... | collective-permute-start | bytes 786440 | tf_op jit(solution)/shard_map/ppermute | solution.py:592
  17.7 9.9 %collective-permute-start.2 = (bf16[512,256]{1,0:T(8,128)(2,1)S(1)}, bf16[512,256]{1,0:T(8,128)(2,1)S(1)}, u32[]{:S(2)}, u32[]{:S(2)}) collective-permute-start(bf16[512,256]{1,0:T(8,128)(2,1)S(1)} %bitcast.38), channel_id=1, source_target_pairs={{1,4},{2,5},{3,6},{5,0},{6,1},{7,2},{9,12},{10,13},{11,14},{13,8},... | collective-permute-start | bytes 786440 | tf_op jit(solution)/shard_map/ppermute | solution.py:593
  30.1 12.1 %copy-start.4 = (bf16[7,7,2,128]{3,2,1,0:T(2,128)(2,1)S(1)}, bf16[7,7,2,128]{3,2,1,0:T(2,128)(2,1)}, u32[]{:S(2)}) copy-start(bf16[7,7,2,128]{3,2,1,0:T(2,128)(2,1)} %w_flow.1) | copy-start | bytes 75268
  31.2 14.2 %copy-start.8 = (bf16[1024,128]{1,0:T(8,128)(2,1)}, bf16[1024,128]{1,0:T(8,128)(2,1)S(1)}, u32[]{:S(2)}) copy-start(bf16[1024,128]{1,0:T(8,128)(2,1)S(1)} %get-tuple-element.47.code) | copy-start | bytes 786436
  31.2 6.9 %collective-permute-start.6 = (bf16[528,128]{1,0:T(8,128)(2,1)S(1)}, bf16[528,128]{1,0:T(8,128)(2,1)S(1)}, u32[]{:S(2)}, u32[]{:S(2)}) collective-permute-start(bf16[528,128]{1,0:T(8,128)(2,1)S(1)} %get-tuple-element.48), channel_id=1, source_target_pairs={{0,1},{1,2},{2,3},{4,5},{5,6},{6,7},{8,9},{9,10},{10,11},{12,13},{... | collective-permute-start | bytes 405512 | tf_op jit(solution)/shard_map/ppermute | solution.py:625
  34.7 7.6 %collective-permute-start.7 = (bf16[528,128]{1,0:T(8,128)(2,1)S(1)}, bf16[528,128]{1,0:T(8,128)(2,1)S(1)}, u32[]{:S(2)}, u32[]{:S(2)}) collective-permute-start(bf16[528,128]{1,0:T(8,128)(2,1)S(1)} %get-tuple-element.49), channel_id=1, source_target_pairs={{1,0},{2,1},{3,2},{5,4},{6,5},{7,6},{9,8},{10,9},{11,10},{13,12},{... | collective-permute-start | bytes 405512 | tf_op jit(solution)/shard_map/ppermute | solution.py:626
  36.1 9.3 %copy-start.2 = (bf16[3,3,128,128]{3,2,1,0:T(8,128)(2,1)S(1)}, bf16[3,3,128,128]{3,2,1,0:T(8,128)(2,1)}, u32[]{:S(2)}) copy-start(bf16[3,3,128,128]{3,2,1,0:T(8,128)(2,1)} %w_code.1) | copy-start | bytes 884740
  36.1 9.3 %copy-start.7 = (f32[2]{0:T(128)S(1)}, f32[2]{0:T(128)}, u32[]{:S(2)}) copy-start(f32[2]{0:T(128)} %b_head.1) | copy-start | bytes 28
  62.0 2.6 %collective-permute-start.8 = (f32[1920,128]{1,0:T(8,128)S(1)}, f32[1920,128]{1,0:T(8,128)S(1)}, u32[]{:S(2)}, u32[]{:S(2)}) collective-permute-start(f32[1920,128]{1,0:T(8,128)S(1)} %get-tuple-element.61), channel_id=1, source_target_pairs={{0,4},{4,0},{8,12},{12,8},{1,5},{5,1},{9,13},{13,9},{2,6},{6,2},{1... | collective-permute-start | bytes 2949128 | tf_op jit(solution)/shard_map/ppermute | solution.py:395
  65.3 8.1 %collective-permute-start.10 = (f32[480,128]{1,0:T(8,128)S(1)}, f32[480,128]{1,0:T(8,128)S(1)}, u32[]{:S(2)}, u32[]{:S(2)}) collective-permute-start(f32[480,128]{1,0:T(8,128)S(1)} %get-tuple-element.65), channel_id=1, source_target_pairs={{0,1},{1,0},{2,3},{3,2},{4,5},{5,4},{6,7},{7,6},{8,9},{9,8},{10,11... | collective-permute-start | bytes 737288 | tf_op jit(solution)/shard_map/ppermute | solution.py:395
  67.0 7.7 %collective-permute-start.9 = (f32[480,128]{1,0:T(8,128)S(1)}, f32[480,128]{1,0:T(8,128)S(1)}, u32[]{:S(2)}, u32[]{:S(2)}) collective-permute-start(f32[480,128]{1,0:T(8,128)S(1)} %get-tuple-element.63), channel_id=1, source_target_pairs={{0,8},{4,12},{8,0},{12,4},{1,9},{5,13},{9,1},{13,5},{2,10},{6,14},... | collective-permute-start | bytes 737288 | tf_op jit(solution)/shard_map/ppermute | solution.py:395
  75.3 4.9 %collective-permute-start.11 = (f32[240,128]{1,0:T(8,128)S(1)}, f32[240,128]{1,0:T(8,128)S(1)}, u32[]{:S(2)}, u32[]{:S(2)}) collective-permute-start(f32[240,128]{1,0:T(8,128)S(1)} %get-tuple-element.67), channel_id=1, source_target_pairs={{0,1},{1,0},{2,3},{3,2},{4,5},{5,4},{6,7},{7,6},{8,9},{9,8},{10,11... | collective-permute-start | bytes 368648 | tf_op jit(solution)/shard_map/ppermute | solution.py:395
  75.8 4.9 %collective-permute-start.12 = (f32[240,128]{1,0:T(8,128)S(1)}, f32[240,128]{1,0:T(8,128)S(1)}, u32[]{:S(2)}, u32[]{:S(2)}) collective-permute-start(f32[240,128]{1,0:T(8,128)S(1)} %get-tuple-element.69), channel_id=1, source_target_pairs={{0,8},{4,12},{8,0},{12,4},{1,9},{5,13},{9,1},{13,5},{2,10},{6,14},... | collective-permute-start | bytes 368648 | tf_op jit(solution)/shard_map/ppermute | solution.py:395
  81.3 7.2 %collective-permute-start.13 = (f32[240,128]{1,0:T(8,128)S(1)}, f32[240,128]{1,0:T(8,128)S(1)}, u32[]{:S(2)}, u32[]{:S(2)}) collective-permute-start(f32[240,128]{1,0:T(8,128)S(1)} %get-tuple-element.71), channel_id=1, source_target_pairs={{0,2},{1,3},{2,0},{3,1},{4,6},{5,7},{6,4},{7,5},{8,10},{9,11},{10,... | collective-permute-start | bytes 368648 | tf_op jit(solution)/shard_map/ppermute | solution.py:395
  89.0 5.7 %collective-permute-start.14 = (bf16[240,128]{1,0:T(8,128)(2,1)S(1)}, bf16[240,128]{1,0:T(8,128)(2,1)S(1)}, u32[]{:S(2)}, u32[]{:S(2)}) collective-permute-start(bf16[240,128]{1,0:T(8,128)(2,1)S(1)} %last.1.mine), channel_id=1, source_target_pairs={{0,2},{1,3},{2,0},{3,1},{4,6},{5,7},{6,4},{7,5},{8,10},{9,11},{10,... | collective-permute-start | bytes 184328 | tf_op jit(solution)/shard_map/ppermute | solution.py:395
  95.3 4.8 %collective-permute-start.15 = (bf16[240,128]{1,0:T(8,128)(2,1)S(1)}, bf16[240,128]{1,0:T(8,128)(2,1)S(1)}, u32[]{:S(2)}, u32[]{:S(2)}) collective-permute-start(bf16[240,128]{1,0:T(8,128)(2,1)S(1)} %get-tuple-element.72.a_mine), channel_id=1, source_target_pairs={{0,1},{1,0},{2,3},{3,2},{4,5},{5,4},{6,7},{7,6},{8,9},{9,8},{10,11... | collective-permute-start | bytes 184328 | tf_op jit(solution)/shard_map/ppermute | solution.py:395
  95.6 4.5 %collective-permute-start.16 = (bf16[240,128]{1,0:T(8,128)(2,1)S(1)}, bf16[240,128]{1,0:T(8,128)(2,1)S(1)}, u32[]{:S(2)}, u32[]{:S(2)}) collective-permute-start(bf16[240,128]{1,0:T(8,128)(2,1)S(1)} %get-tuple-element.73.b_mine), channel_id=1, source_target_pairs={{0,8},{4,12},{8,0},{12,4},{1,9},{5,13},{9,1},{13,5},{2,10},{6,14},... | collective-permute-start | bytes 184328 | tf_op jit(solution)/shard_map/ppermute | solution.py:395
  100.7 4.9 %collective-permute-start.17 = (bf16[480,128]{1,0:T(8,128)(2,1)S(1)}, bf16[480,128]{1,0:T(8,128)(2,1)S(1)}, u32[]{:S(2)}, u32[]{:S(2)}) collective-permute-start(bf16[480,128]{1,0:T(8,128)(2,1)S(1)} %get-tuple-element.74.a_mine), channel_id=1, source_target_pairs={{0,8},{4,12},{8,0},{12,4},{1,9},{5,13},{9,1},{13,5},{2,10},{6,14},... | collective-permute-start | bytes 368648 | tf_op jit(solution)/shard_map/ppermute | solution.py:395
  101.1 4.9 %collective-permute-start.18 = (bf16[480,128]{1,0:T(8,128)(2,1)S(1)}, bf16[480,128]{1,0:T(8,128)(2,1)S(1)}, u32[]{:S(2)}, u32[]{:S(2)}) collective-permute-start(bf16[480,128]{1,0:T(8,128)(2,1)S(1)} %get-tuple-element.75.b_mine), channel_id=1, source_target_pairs={{0,1},{1,0},{2,3},{3,2},{4,5},{5,4},{6,7},{7,6},{8,9},{9,8},{10,11... | collective-permute-start | bytes 368648 | tf_op jit(solution)/shard_map/ppermute | solution.py:395
  106.6 1.9 %collective-permute-start.19 = (bf16[1920,128]{1,0:T(8,128)(2,1)S(1)}, bf16[1920,128]{1,0:T(8,128)(2,1)S(1)}, u32[]{:S(2)}, u32[]{:S(2)}) collective-permute-start(bf16[1920,128]{1,0:T(8,128)(2,1)S(1)} %merge3.1.mine), channel_id=1, source_target_pairs={{0,4},{4,0},{8,12},{12,8},{1,5},{5,1},{9,13},{13,9},{2,6},{6,2},{1... | collective-permute-start | bytes 1474568 | tf_op jit(solution)/shard_map/ppermute | solution.py:395
  (7 other events, 39.9 us)

commit v3 on v2

--- a/solution.py
+++ b/solution.py
@@ -7,14 +7,14 @@
 from jax.experimental.pallas import tpu as pltpu
 from jax.sharding import PartitionSpec as P
 
+BF = jnp.bfloat16
+F32 = jnp.float32
 RADIUS = 4
 SIDE = 2 * RADIUS + 1
 OFF = SIDE * SIDE
 HALO = 4
 FLOW_HALO = 6
 TARGET_HALO = 2
-BF = jnp.bfloat16
-F32 = jnp.float32
 NT = (((1,), (1,)), ((), ()))
 TN = (((0,), (0,)), ((), ()))
 
@@ -23,6 +23,10 @@
 AT_FLOW = 3648
 AT_END = 3760
 HALF = 96
+MOTION_BLOCK = 7
+HIDDEN_BLOCK = 12
+SLOPE_BLOCK = 10
+CODE_BLOCK = 4
 MISC_ROWS = 8
 
 
@@ -38,11 +42,11 @@
     return pl.ds(pl.multiple_of(start * unit, unit), count * unit)
 
 
-def split3(s):
-    hi = s.astype(BF)
-    rest = s - hi.astype(F32)
-    mid = rest.astype(BF)
-    return jnp.concatenate([hi, mid, (rest - mid.astype(F32)).astype(BF)], axis=0)
+def split3(s, padded=False):
+    hi = s.astype(BF).astype(F32)
+    mid = (s - hi).astype(BF).astype(F32)
+    terms = [hi, mid, s - hi - mid] + [jnp.zeros_like(s)] * padded
+    return jnp.concatenate(terms, axis=0).astype(BF)
 
 
 def silu_pair(v):
@@ -50,7 +54,7 @@
     return v * s, s * (1.0 + v * (1.0 - s))
 
 
-def correlate_kernel(n_rows, n_cols, own, mid, top, bot, out, near, rows_f):
+def correlate(n_rows, n_cols, own, mid, top, bot, out, out_at, near, rows_f):
     n_chan = own.shape[1]
     halo = RADIUS * n_cols
     body = n_rows * n_cols
@@ -87,21 +91,32 @@
                 if 0 <= dy < SIDE:
                     rows_f[8 * dy : 8 * dy + 8, u * W : (u + 1) * W] = inner[:, u * W : (u + 1) * W]
                     rows_f[72 + dy : 73 + dy, u * W : (u + 1) * W] = outer[:, u * W : (u + 1) * W]
-        out[:, rows(2 * b, 2, W)] = (rows_f[...] * scale).astype(BF)
+        out[out_at, rows(2 * b, 2, W)] = (rows_f[...] * scale).astype(BF)
         return carry
 
     lax.fori_loop(0, n_rows // 2, two_rows, 0)
 
 
-def code_kernel(
+def near_kernel(
     n_rows, n_cols,
-    order, near_vol, far_vol, w_volume, bias, flow, targets,
-    vol, code, up, dn, wv,
-    wide, edge,
+    own_hbm, flow_hbm, targets_hbm, volume_hbm, code_hbm, joint_hbm, w_flow_hbm, bv_hbm, bc_hbm, bf_hbm, bj_hbm,
+    mid, top, bot, head,
+    out, own, flow, targets, w_code, bias, wv, wcb, wj, wjb, wf, wht,
+    near, rows_f, wide, w_volume, w_joint, w_flow, sems,
 ):
-    W = n_cols
-    halo = HALO * W
-    body = n_rows * W
+    loads = (
+        (own_hbm, own), (flow_hbm, flow), (targets_hbm, targets), (volume_hbm, w_volume), (code_hbm, w_code),
+        (joint_hbm, w_joint), (w_flow_hbm, w_flow), (bv_hbm, bias.at[0]), (bc_hbm, bias.at[1]),
+        (bf_hbm, bias.at[2]), (bj_hbm, bias.at[3]),
+    )
+    copies = [pltpu.make_async_copy(src, dst, sems.at[k]) for k, (src, dst) in enumerate(loads)]
+    for copy in copies:
+        copy.start()
+    copies[0].wait()
+    correlate(n_rows, n_cols, own, mid, top, bot, out, slice(None), near, rows_f)
+    for copy in copies[1:]:
+        copy.wait()
+    C = w_code.shape[3]
     wide[...] = jnp.zeros_like(wide)
     weight = w_volume[...].astype(F32)
     for half in range(2):
@@ -110,18 +125,47 @@
             wide[half * HALF + 8 * dy : half * HALF + 8 * dy + 8, :] = weight[at : at + 8]
             wide[half * HALF + 72 + dy : half * HALF + 73 + dy, :] = weight[at + 8 : at + 9]
     wv[...] = wide[...].astype(BF)
-    near_second = order[0] != lax.axis_index("tm") % 2
-    a, b = near_vol[...], far_vol[...]
-    vol[0:HALF, :] = jnp.where(near_second, b, a)
-    vol[HALF : 2 * HALF, :] = jnp.where(near_second, a, b)
+    wide[...] = jnp.zeros_like(wide)
+    for i in range(7):
+        for j in range(7):
+            wide[16 * i + 2 * j : 16 * i + 2 * j + 2, :] = w_flow[i, j].astype(F32)
+    wf[...] = wide[0:112, :].astype(BF)
+    for i in range(3):
+        for j in range(3):
+            at = (3 * i + j) * C
+            wcb[:, at : at + C] = w_code[i, j]
+            wjb[:, at : at + C] = w_joint[i, j]
+            for part in range(2):
+                at = (2 * i + part) * 3 * C + j * C
+                wj[at : at + C, :] = w_joint[i, j, part * C : (part + 1) * C, :]
+    wide[...] = jnp.zeros_like(wide)
+    for k in range(3):
+        wide[16 * k : 16 * k + 2, :] = head[...].astype(F32)
+    wht[...] = wide[0:48, :].astype(BF)
+
+
+def code_kernel(
+    n_rows, n_cols,
+    order, own, mid, top, bot, near_vol, wv, bias, flow, targets,
+    vol, code, up, dn,
+    near, rows_f, edge,
+):
+    W = n_cols
+    halo = HALO * W
+    body = n_rows * W
+    near_second = (order[0] != lax.axis_index("tm") % 2).astype(jnp.int32)
+    near_at = pl.multiple_of(near_second * HALF, HALF)
+    far_at = pl.multiple_of((1 - near_second) * HALF, HALF)
+    vol[pl.ds(near_at, HALF), :] = near_vol[...]
+    correlate(n_rows, n_cols, own, mid, top, bot, vol, pl.ds(far_at, HALF), near, rows_f)
 
     def one_code(r, carry):
-        at = rows(r, 2, W)
+        at = rows(r, CODE_BLOCK, W)
         pre = lax.dot_general(vol[:, at], wv[...], TN, preferred_element_type=F32) + bias[0:1, :]
         code[at, :] = (pre * jax.nn.sigmoid(pre)).astype(BF)
         return carry
 
-    lax.fori_loop(0, n_rows // 2, lambda r, c: one_code(2 * r, c), 0)
+    lax.fori_loop(0, n_rows // CODE_BLOCK, lambda r, c: one_code(CODE_BLOCK * r, c), 0)
     for ref, at, flow_at, target_at in (
         (up, 0, 0, 0),
         (dn, body - halo, n_rows - FLOW_HALO, n_rows - TARGET_HALO),
@@ -159,14 +203,9 @@
 BWD = (2, 1, 0)
 
 
-def flow_kernel(n_rows, n_cols, top, bot, flow, targets, w_flow, bias, jf, d_flow, xb, tgt, xf, xx, wide, wf):
+def flow_kernel(n_rows, n_cols, top, bot, flow, targets, wf, bias, jf, d_flow, xb, tgt, xf, xx):
     W = n_cols
     halo = HALO * W
-    wide[...] = jnp.zeros_like(wide)
-    for i in range(7):
-        for j in range(7):
-            wide[16 * i + 2 * j : 16 * i + 2 * j + 2, :] = w_flow[i, j].astype(F32)
-    wf[...] = wide[...].astype(BF)
     xx[...] = jnp.zeros_like(xx)
     above = top[halo : halo + 16, :].astype(F32)
     below = bot[halo : halo + 16, :].astype(F32)
@@ -193,36 +232,29 @@
             lo = (TARGET_HALO + y) * W
             tgt[k : k + 1, lo : lo + W] = targets[k, y : y + 1, :].astype(F32)
 
-    def one_row(y, carry):
-        patch = xb[pl.ds(pl.multiple_of(y * 16, 16), 112), :]
-        pre = lax.dot_general(patch, wf[...], TN, preferred_element_type=F32) + bias[2:3, :]
-        value, slope = silu_pair(pre)
-        d_flow[rows(y, 1, W), :] = slope
-        store_stack(jf, y, jnp.where(inside_frame(n_rows, y - 3), value, 0.0), FWD)
-        return carry
-
-    lax.fori_loop(0, n_rows + 6, one_row, 0)
+    def flow_rows(b, carry):
+        y = b * MOTION_BLOCK
+        patches = [xb[pl.ds(pl.multiple_of((y + u) * 16, 16), 112), :] for u in range(MOTION_BLOCK)]
+        pre = lax.dot_general(jnp.concatenate(patches, axis=1), wf[...], TN, preferred_element_type=F32)
+        for u in range(MOTION_BLOCK):
+            value, slope = silu_pair(pre[u * W : (u + 1) * W] + bias[2:3, :])
+            d_flow[rows(y + u, 1, W), :] = slope
+            store_stack(jf, y + u, jnp.where(inside_frame(n_rows, y + u - 3), value, 0.0), FWD)
+        return carry
+
+    lax.fori_loop(0, (n_rows + 6) // MOTION_BLOCK, flow_rows, 0)
 
 
 def hidden_kernel(
     n_rows, n_cols, n_tm,
-    b_head, code, top, bot, jf, tgt, wc, w_joint, w_head, bias,
+    b_head, code, top, bot, jf, tgt, wc, wj, wht, bias,
     error_out, jt, s3, d_motion, misc,
-    c3, jm, err, hid, g_head, acc, wjm, wjf, square, wht,
+    c3, jm, err, hid, g_head, acc,
 ):
     W = n_cols
     count = 2.0 * n_tm * lax.axis_size("space") * n_rows * n_cols
     slope_scale = frame_scale(n_tm, 2.0 / count)
-    for i in range(3):
-        for j in range(3):
-            wjm[i, j * 128 : (j + 1) * 128, :] = w_joint[i, j, 0:128, :]
-            wjf[i, j * 128 : (j + 1) * 128, :] = w_joint[i, j, 128:256, :]
-    square[...] = jnp.zeros_like(square)
-    square[:, 0:2] = w_head[...].astype(F32)
-    head_t = square[...].T[0:16].astype(BF)
-    for k in range(3):
-        wht[16 * k : 16 * k + 16, :] = head_t
-    C = wc.shape[2]
+    C = wc.shape[1]
     body = n_rows * W
 
     def load_halo(y, carry):
@@ -238,41 +270,38 @@
     lax.fori_loop(0, n_rows, load_code, 0)
 
     def motion_rows(b, carry):
-        y = 2 * b
-        pre = bias[1:2, :] + dot(c3[rows(y, 2, W), :], wc[0])
-        pre = pre + dot(c3[rows(y + 1, 2, W), :], wc[1])
-        pre = pre + dot(c3[rows(y + 2, 2, W), :], wc[2])
-        for u in range(2):
+        y = b * MOTION_BLOCK
+        taps = jnp.concatenate([c3[rows(y + i, MOTION_BLOCK, W), :] for i in range(3)], axis=1)
+        pre = dot(taps, wc[...]) + bias[1:2, :]
+        for u in range(MOTION_BLOCK):
             value, slope = silu_pair(pre[u * W : (u + 1) * W])
             d_motion[rows(y + u, 1, W), :] = slope
             store_stack(jm, y + u, jnp.where(inside_frame(n_rows, y + u - 3), value, 0.0), FWD)
         return carry
 
-    lax.fori_loop(0, (n_rows + 6) // 2, motion_rows, 0)
-
-    k_row = lax.broadcasted_iota(jnp.int32, (16, 2 * W), 0)
+    lax.fori_loop(0, (n_rows + 6) // MOTION_BLOCK, motion_rows, 0)
+
+    block = HIDDEN_BLOCK
+    k_row = lax.broadcasted_iota(jnp.int32, (16, block * W), 0)
     b_col = jnp.where(k_row == 0, b_head[0], jnp.where(k_row == 1, b_head[1], 0.0))
 
     def hidden_rows(b, carry):
-        y = 2 * b
-        pre = bias[3:4, :] + dot(jm[rows(y, 2, W), :], wjm[0])
-        pre = pre + dot(jf[rows(y, 2, W), :], wjf[0])
-        for i in (1, 2):
-            pre = pre + dot(jm[rows(y + i, 2, W), :], wjm[i])
-            pre = pre + dot(jf[rows(y + i, 2, W), :], wjf[i])
+        y = b * block
+        taps = [ref[rows(y + i, block, W), :] for i in range(3) for ref in (jm, jf)]
+        pre = dot(jnp.concatenate(taps, axis=1), wj[...]) + bias[3:4, :]
         value, slope = silu_pair(pre)
         hidden = value.astype(BF)
-        hid[rows(y, 2, W), :] = hidden
+        hid[rows(y, block, W), :] = hidden
         pred = lax.dot_general(wht[0:16, :], hidden, NT, preferred_element_type=F32)
-        error = pred + b_col - tgt[:, rows(y, 2, W)]
-        err[:, rows(y, 2, W)] = error
+        error = pred + b_col - tgt[:, rows(y, block, W)]
+        err[:, rows(y, block, W)] = error
         back = lax.dot_general(split3(error * slope_scale), wht[...], TN, preferred_element_type=F32) * slope
-        for u in range(2):
+        for u in range(block):
             v = jnp.where(inside_frame(n_rows, y + u - 2), back[u * W : (u + 1) * W], 0.0)
             store_stack(s3, y + u, v, BWD)
         return carry
 
-    lax.fori_loop(0, (n_rows + 4) // 2, hidden_rows, 0)
+    lax.fori_loop(0, (n_rows + 4) // block, hidden_rows, 0)
 
     acc[...] = jnp.zeros_like(acc)
     g_head[...] = jnp.zeros_like(g_head)
@@ -305,49 +334,45 @@
 
 def rest_kernel(
     n_rows, n_cols, at_misc,
-    jt, s3, d_motion, d_flow, xb, vol, code, misc, wv, w_code, w_joint, bias,
+    jt, s3, d_motion, d_flow, xb, vol, code, misc, wv, wcb, wjb, bias,
     keep, send,
-    m3, s_flow, s_code, acc, grads, wcb, wjb,
+    m3, s_flow, s_code, acc, grads,
 ):
     W = n_cols
     C = code.shape[1]
     body = n_rows * W
-    for i in range(3):
-        for j in range(3):
-            wcb[i, :, j * C : (j + 1) * C] = w_code[i, j]
-            wjb[i, :, j * C : (j + 1) * C] = w_joint[i, j]
 
     def joint_slopes(b, carry):
-        y = 2 * b
-        sj = dot_nt(s3[rows(y + 2, 2, W), :], wjb[0])
-        sj = sj + dot_nt(s3[rows(y + 1, 2, W), :], wjb[1])
-        sj = sj + dot_nt(s3[rows(y, 2, W), :], wjb[2])
-        for u in range(2):
+        y = b * SLOPE_BLOCK
+        taps = jnp.concatenate([s3[rows(y + 2 - i, SLOPE_BLOCK, W), :] for i in range(3)], axis=1)
+        sj = dot_nt(taps, wjb[...])
+        for u in range(SLOPE_BLOCK):
             part = sj[u * W : (u + 1) * W]
             v = part[:, 0:C] * d_motion[rows(y + u + 2, 1, W), :]
             store_stack(m3, y + u, jnp.where(inside_frame(n_rows, y + u - 1), v, 0.0), BWD)
             s_flow[rows(y + u, 1, W), :] = (part[:, C:] * d_flow[rows(y + u + 2, 1, W), :]).astype(BF)
         return carry
 
-    lax.fori_loop(0, (n_rows + 2) // 2, joint_slopes, 0)
+    lax.fori_loop(0, (n_rows + 2) // SLOPE_BLOCK, joint_slopes, 0)
     acc[...] = jnp.zeros_like(acc)
 
     def add_rows(k, v):
         acc[8 * k : 8 * k + 8, :] += jnp.sum(v.reshape(v.shape[0] // 8, 8, C), axis=0)
 
     def code_slopes(b, carry):
-        y = 2 * b
-        sc = dot_nt(m3[rows(y + 2, 2, W), :], wcb[0])
-        sc = sc + dot_nt(m3[rows(y + 1, 2, W), :], wcb[1])
-        sc = sc + dot_nt(m3[rows(y, 2, W), :], wcb[2])
-        pre = lax.dot_general(vol[:, rows(y, 2, W)], wv[...], TN, preferred_element_type=F32) + bias[0:1, :]
-        s_code[rows(y, 2, W), :] = (sc * silu_pair(pre)[1]).astype(BF)
-        add_rows(0, s_code[rows(y, 2, W), :].astype(F32))
-        add_rows(1, m3[rows(y + 1, 2, W), C : 2 * C].astype(F32))
-        add_rows(2, s_flow[rows(y + 1, 2, W), :].astype(F32))
-        return carry
-
-    lax.fori_loop(0, n_rows // 2, code_slopes, 0)
+        y = b * CODE_BLOCK
+        at = rows(y, CODE_BLOCK, W)
+        taps = jnp.concatenate([m3[rows(y + 2 - i, CODE_BLOCK, W), :] for i in range(3)], axis=1)
+        sc = dot_nt(taps, wcb[...])
+        pre = lax.dot_general(vol[:, at], wv[...], TN, preferred_element_type=F32) + bias[0:1, :]
+        slope = (sc * silu_pair(pre)[1]).astype(BF)
+        s_code[at, :] = slope
+        add_rows(0, slope.astype(F32))
+        add_rows(1, m3[rows(y + 1, CODE_BLOCK, W), C : 2 * C].astype(F32))
+        add_rows(2, s_flow[rows(y + 1, CODE_BLOCK, W), :].astype(F32))
+        return carry
+
+    lax.fori_loop(0, n_rows // CODE_BLOCK, code_slopes, 0)
 
     for i in range(3):
         g = dot(jt[...], s3[(3 - i) * W : (3 - i) * W + body, :])
@@ -379,7 +404,7 @@
 
 VMEM = pl.BlockSpec(memory_space=pltpu.VMEM)
 SMEM = pl.BlockSpec(memory_space=pltpu.SMEM)
-ANY = pl.BlockSpec(memory_space=pl.ANY)
+HBM = pl.BlockSpec(memory_space=pltpu.HBM)
 
 
 def bits_of(axis):
@@ -426,21 +451,36 @@
     return ref[pl.ds(pl.multiple_of(which * half, 8), half), :]
 
 
-def first_split(bits, keep, got, a_keep, a_send, b_keep, b_send, total):
+def first_split(at, bits, keep, got, a_keep, a_send, b_keep, b_send, total):
     quarter = a_keep.shape[0]
     total[...] = keep[...] + got[...]
-    for at, (k, s, bit) in enumerate(((a_keep, a_send, bits[1]), (b_keep, b_send, bits[2]))):
-        k[...] = total[pl.ds(pl.multiple_of((2 * at + bit) * quarter, 8), quarter), :]
-        s[...] = total[pl.ds(pl.multiple_of((2 * at + 1 - bit) * quarter, 8), quarter), :]
-
-
-def second_split(bits, a_keep, a_got, b_keep, b_got, a_mine, a_send, b_mine, b_send, total):
+    for part, (k, s, bit) in enumerate(((a_keep, a_send, bits[1]), (b_keep, b_send, bits[2]))):
+        k[...] = total[pl.ds(pl.multiple_of((2 * part + bit) * quarter, 8), quarter), :]
+        s[...] = total[pl.ds(pl.multiple_of((2 * part + 1 - bit) * quarter, 8), quarter), :].astype(s.dtype)
+    @pl.when(jnp.logical_and(bits[0] == 1, bits[2] == 0))
+    def _():
+        value = total[3 * quarter + at : 3 * quarter + at + MISC_ROWS, :]
+        b_send[at : at + 4 * MISC_ROWS, :] = split3(value, True)
+
+
+def second_split(at, bits, a_keep, a_got, b_keep, b_got, a_mine, a_send, b_mine, b_send, total):
     half = a_mine.shape[0]
-    for keep, got, mine, send, bit in (
+    for is_b, (keep, got, mine, send, bit) in enumerate((
         (a_keep, a_got, a_mine, a_send, bits[2]),
         (b_keep, b_got, b_mine, b_send, bits[1]),
-    ):
-        total[...] = keep[...] + got[...]
+    )):
+        total[...] = keep[...] + got[...].astype(F32)
+        if is_b:
+
+            @pl.when(jnp.logical_and(bits[0] == 1, bits[2] == 1))
+            def _():
+                terms = got[at : at + 4 * MISC_ROWS, :].astype(F32)
+                value = keep[at : at + MISC_ROWS, :]
+                for k in range(3):
+                    value = value + terms[k * MISC_ROWS : (k + 1) * MISC_ROWS]
+                total[at : at + MISC_ROWS, :] = value
+                total[at + MISC_ROWS : at + 4 * MISC_ROWS, :] = jnp.zeros((3 * MISC_ROWS, value.shape[1]), F32)
+
         mine[...] = pick(total, bit, half)
         send[...] = pick(total, 1 - bit, half)
 
@@ -491,32 +531,38 @@
     half, C = keep.shape
     x, z, far_z = ("tm", 2), ("space", 1), ("space", 2)
 
-    def stage(body, name, n_out, n, dtype, scratch, *args):
-        out = (shape(n, C, dtype=dtype),) * n_out
+    def stage(body, name, dtypes, n, scratch, *args):
+        out = tuple(shape(n, C, dtype=dtype) for dtype in dtypes)
         return call(
             body, name, out, [SMEM] + [VMEM] * len(args),
             [pltpu.VMEM((scratch, C), F32)] if scratch else [], 10_000_000, bits, *args,
         )
 
-    ak, as_, bk, bs = stage(first_split, "split1", 4, half // 4, F32, half, keep, got)
+    first_at = at_misc - 2 * half + half // 4
+    ak, as_, bk, bs = stage(functools.partial(first_split, first_at), "split1", (F32, BF, F32, BF), half // 4, half, keep, got)
     ag, bg = trade(as_, *x), trade(bs, *z)
-    ak, as_, bk, bs = stage(second_split, "split2", 4, half // 8, F32, half // 4, ak, ag, bk, bg)
+    ak, as_, bk, bs = stage(functools.partial(second_split, first_at), "split2", (F32,) * 4, half // 8, half // 4, ak, ag, bk, bg)
     ag, bg = trade(as_, *z), trade(bs, *x)
-    keep, send = stage(third_split, "split3", 2, half // 8, F32, half // 4, ak, ag, bk, bg)
+    keep, send = stage(third_split, "split3", (F32, F32), half // 8, half // 4, ak, ag, bk, bg)
     got = trade(send, *far_z)
     chunk = half // 8
     (y,) = stage(
-        functools.partial(last_sum, at_misc - (2 * half - chunk)), "last", 1, chunk, BF, chunk, keep, got
-    )
-    a, b = stage(first_merge, "merge1", 2, chunk, BF, 0, y, trade(y, *far_z))
+        functools.partial(last_sum, at_misc - (2 * half - chunk)), "last", (BF,), chunk, chunk, keep, got
+    )
+    a, b = stage(first_merge, "merge1", (BF, BF), chunk, 0, y, trade(y, *far_z))
     a, b = stage(
-        functools.partial(pair_merge, False), "merge2", 2, half // 4, BF, 0, a, trade(a, *z), b, trade(b, *x)
-    )
-    (out,) = stage(join_merge, "merge3", 1, half, BF, 0, a, trade(a, *x), b, trade(b, *z))
+        functools.partial(pair_merge, False), "merge2", (BF, BF), half // 4, 0, a, trade(a, *z), b, trade(b, *x)
+    )
+    (out,) = stage(join_merge, "merge3", (BF,), half, 0, a, trade(a, *x), b, trade(b, *z))
     return out
 
 
-def finish_kernel(at_misc, bits, mine, other, joint, code, volume, flow, misc, full):
+def finish_kernel(
+    at_misc,
+    bits, mine, other,
+    joint, code, volume, flow, b_volume, b_code, b_flow, b_joint, head, loss, b_head,
+    full,
+):
     half, C = mine.shape
     full[pl.ds(pl.multiple_of(bits[0] * half, 16), half), :] = mine[...]
     full[pl.ds(pl.multiple_of((1 - bits[0]) * half, 16), half), :] = other[...]
@@ -537,19 +583,26 @@
         for j in range(7):
             flow[i, j, :, :] = part[2 * j : 2 * j + 2]
     terms = full[at_misc : at_misc + 32, :].astype(F32)
-    misc[...] = terms[0:8] + terms[8:16] + terms[16:24]
-
-
-def call(body, name, out_shape, in_specs, scratch, flops, *args):
+    misc = terms[0:8] + terms[8:16] + terms[16:24]
+    for k, ref in enumerate((b_volume, b_code, b_flow, b_joint)):
+        ref[...] = misc[k]
+    head[...] = misc[4:6]
+    lane = lax.broadcasted_iota(jnp.int32, (1, C), 1)
+    loss[0] = jnp.sum(jnp.where(lane == 0, misc[6:7], 0.0))
+    b_head[0] = jnp.sum(jnp.where(lane == 1, misc[6:7], 0.0))
+    b_head[1] = jnp.sum(jnp.where(lane == 2, misc[6:7], 0.0))
+
+
+def call(body, name, out_shape, in_specs, scratch, flops, *args, out_specs=None):
     held = [
-        pltpu.with_memory_space_constraint(x, pltpu.VMEM) if spec is VMEM else x
+        x if spec is SMEM else pltpu.with_memory_space_constraint(x, spec.memory_space)
         for x, spec in zip(args, in_specs, strict=True)
     ]
     return pl.pallas_call(
         body,
         out_shape=out_shape,
         in_specs=in_specs,
-        out_specs=jax.tree.map(lambda _: VMEM, out_shape),
+        out_specs=out_specs or jax.tree.map(lambda _: VMEM, out_shape),
         scratch_shapes=scratch,
         cost_estimate=pl.CostEstimate(flops=flops, bytes_accessed=flops // 300, transcendentals=0),
         compiler_params=pltpu.CompilerParams(vmem_limit_bytes=16 << 20),
@@ -586,15 +639,12 @@
         return t - 1 + 2 * (t % 2)
 
     first, last = flat[:halo], flat[body - halo :]
-    far_mid = lax.ppermute(flat, both, route(far, 0))
-    far_top = lax.ppermute(last, both, route(far, 1))
-    far_bot = lax.ppermute(first, both, route(far, -1))
     near_top = lax.ppermute(last, both, route(near, 1))
     near_bot = lax.ppermute(first, both, route(near, -1))
     near_mid = lax.ppermute(flat, both, route(near, 0))
-
-    bias = jnp.stack([b_volume, b_code, b_flow, b_joint])
-    flow = flow_now[0]
+    far_top = lax.ppermute(last, both, route(far, 1))
+    far_bot = lax.ppermute(first, both, route(far, -1))
+    far_mid = lax.ppermute(flat, both, route(far, 0))
 
     def shape(*dims, dtype=BF):
         return pltpu.VMEM(dims, dtype)
@@ -602,25 +652,39 @@
     def result(*dims):
         return jax.ShapeDtypeStruct(dims, F32)
 
-    def correlate(mid, top, bot, name):
-        return call(
-            functools.partial(correlate_kernel, n_rows, n_cols), name,
-            shape(HALF, body), [VMEM] * 4,
-            [pltpu.VMEM((body + 2 * halo, n_chan), BF), pltpu.VMEM((HALF, 2 * W), F32)],
-            4_000_000_000,
-            flat, mid, top, bot,
-        )
-
-    near_vol = correlate(near_mid, near_top, near_bot, "near")
-    far_vol = correlate(far_mid, far_top, far_bot, "far")
-    vol, code, up, dn, wv = call(
+    near_vol, held, flow, held_targets, wc, bias, wv, wcb, wj, wjb, wf, wht = call(
+        functools.partial(near_kernel, n_rows, n_cols), "near",
+        (
+            shape(HALF, body), shape(body, n_chan), shape(*flow_now.shape[1:]),
+            shape(*targets.shape[1:], dtype=jnp.int32), shape(3, 3, C, C), shape(4, C, dtype=F32),
+            shape(2 * HALF, C), shape(C, 9 * C), shape(18 * C, C),
+            shape(2 * C, 9 * C), shape(112, C), shape(48, C),
+        ),
+        [HBM] * 11 + [VMEM] * 4,
+        [
+            pltpu.VMEM((body + 2 * halo, n_chan), BF),
+            pltpu.VMEM((HALF, 2 * W), F32),
+            pltpu.VMEM((2 * HALF, C), F32),
+            pltpu.VMEM(w_volume.shape, BF),
+            pltpu.VMEM(w_joint.shape, BF),
+            pltpu.VMEM(w_flow.shape, BF),
+            pltpu.SemaphoreType.DMA((11,)),
+        ],
+        4_000_000_000,
+        flat, flow_now[0], targets[0], w_volume, w_code, w_joint, w_flow, b_volume, b_code, b_flow, b_joint,
+        near_mid, near_top, near_bot, w_head.T,
+    )
+    vol, code, up, dn = call(
         functools.partial(code_kernel, n_rows, n_cols), "code",
-        (
-            shape(2 * HALF, body), shape(body, C), shape(halo + 16, C), shape(halo + 16, C),
-            shape(2 * HALF, C),
-        ),
-        [SMEM] + [VMEM] * 6, [pltpu.VMEM((2 * HALF, C), F32), pltpu.VMEM((16, W), F32)], 500_000_000,
-        pair_order, near_vol, far_vol, w_volume, bias, flow, targets[0],
+        (shape(2 * HALF, body), shape(body, C), shape(halo + 16, C), shape(halo + 16, C)),
+        [SMEM] + [VMEM] * 9,
+        [
+            pltpu.VMEM((body + 2 * halo, n_chan), BF),
+            pltpu.VMEM((HALF, 2 * W), F32),
+            pltpu.VMEM((16, W), F32),
+        ],
+        4_000_000_000,
+        pair_order, held, far_mid, far_top, far_bot, near_vol, wv, bias, flow, held_targets,
     )
     top = lax.ppermute(dn, "space", [(s, s + 1) for s in range(n_space - 1)])
     bot = lax.ppermute(up, "space", [(s + 1, s) for s in range(n_space - 1)])
@@ -637,11 +701,9 @@
         [
             pltpu.VMEM((24, W), F32),
             pltpu.VMEM(((n_rows + 12) * 16, W), F32),
-            pltpu.VMEM((112, C), F32),
-            pltpu.VMEM((112, C), BF),
         ],
         1_000_000_000,
-        top, bot, flow, targets[0], w_flow, bias,
+        top, bot, flow, held_targets, wf, bias,
     )
     flow_error, jt, s3, d_motion, misc = call(
         functools.partial(hidden_kernel, n_rows, n_cols, n_tm), "hidden",
@@ -660,13 +722,9 @@
             pltpu.VMEM(((n_rows + 4) * W, C), BF),
             pltpu.VMEM((48, C), F32),
             pltpu.VMEM((8, C), F32),
-            pltpu.VMEM((3, 3 * C, C), BF),
-            pltpu.VMEM((3, 3 * C, C), BF),
-            pltpu.VMEM((C, C), F32),
-            pltpu.VMEM((48, C), BF),
         ],
         4_000_000_000,
-        b_head, code, top, bot, jf, tgt, w_code.reshape(3, 3 * C, C), w_joint, w_head, bias,
+        b_head, code, top, bot, jf, tgt, wc.reshape(9 * C, C), wj, wht, bias,
     )
     n_dev = n_tm * n_space
     paired = n_tm == 4 and n_space == 4
@@ -685,11 +743,9 @@
             pltpu.VMEM((body, C), BF),
             pltpu.VMEM((24, C), F32),
             pltpu.VMEM((grad_rows, C), F32),
-            pltpu.VMEM((3, C, 3 * C), BF),
-            pltpu.VMEM((3, 2 * C, 3 * C), BF),
         ],
         3_000_000_000,
-        jt, s3, d_motion, d_flow, xb, vol, code, misc, wv, w_code, w_joint, bias,
+        jt, s3, d_motion, d_flow, xb, vol, code, misc, wv, wcb, wjb, bias,
     )
     core = ("tm", 1)
     got = trade(send, *core)
@@ -707,16 +763,15 @@
             result(3, 3, C, C),
             result(2 * OFF, C),
             result(7, 7, 2, C),
-            result(MISC_ROWS, C),
+            result(C), result(C), result(C), result(C),
+            result(2, C), result(1), result(2),
         ),
         [SMEM] + [VMEM] * 2, [pltpu.VMEM((grad_rows, C), BF)], 100_000_000,
         bits, mine, other,
-    )
-    joint, g_code, g_volume, g_flow, misc = outs
-    return (
-        misc[6, 0:1], flow_error[None], g_volume, misc[0], g_code, misc[1],
-        g_flow, misc[2], joint, misc[3], misc[4:6].T, misc[6, 1:3],
-    )
+        out_specs=(VMEM,) * 9 + (SMEM,) * 2,
+    )
+    joint, g_code, g_volume, g_flow, g_bv, g_bc, g_bf, g_bj, head, loss, g_b_head = outs
+    return loss, flow_error[None], g_volume, g_bv, g_code, g_bc, g_flow, g_bf, joint, g_bj, head.T, g_b_head
 
 
 def solution(mesh):

time: 113 us -> 97.8 us (0.87)
  Pallas kernels: 30.7 us -> 24.9 us
  waiting for transfers between devices: 45.7 us -> 40.2 us
  local copies, waits for them, and re-layouts: 5.43 us -> 1.72 us
    ppermute x12, starting transfers between devices: 7.51 us -> 15.8 us  [trade(): lax.ppermute(x, axis, [(i, i ^ bit) for i in range(lax.axis_size(axis))])]
    ppermute x1, starting transfers between devices: 7.22 us -> 0.52 us  [local(): near_mid = lax.ppermute(flat, both, route(near, 0))]
    ppermute x12, waiting for transfers between devices: 34.6 us -> 28.3 us  [trade(): lax.ppermute(x, axis, [(i, i ^ bit) for i in range(lax.axis_size(axis))])]
    pallas_call x14 -> x13, Pallas kernels: 30.7 us -> 24.9 us  [call(): pl.pallas_call(body, out_shape=out_shape, in_specs=in_specs, out_specs=ou...]
    ppermute x1, waiting for transfers between devices: 0.25 us -> 2.66 us  [local(): near_top = lax.ppermute(last, both, route(near, 1))]
    unnamed x23 -> x4, local copies, waits for them, and re-layouts: 2.18 us -> 0.66 us
    ppermute x1, waiting for transfers between devices: 4.79 us -> 3.64 us  [local(): near_bot = lax.ppermute(first, both, route(near, -1))]
  transfers between devices with their start and end apart: 20 -> 20, of which waited for: 15 -> 16; matrix products, arithmetic and copies ran while one was open for 2% -> 1% of each run, Pallas kernels for 2% -> 4%
where the time goes in v3:
time: 97.8 us; the launch traced here: 97.5 us
  waiting for transfers between devices  40.2 us (41%)
  starting transfers between devices  29 us (30%)
  Pallas kernels  24.9 us (25%)
  local copies, waits for them, and re-layouts  1.72 us (2%)
  between operations  1.48 us (2%)
    ppermute x12, waiting for transfers between devices, trade(): lax.ppermute(x, axis, [(i, i ^ bit) for i in range(lax.axis_size(axis))])  28.3 us
    pallas_call x13, Pallas kernels, call(): pl.pallas_call(body, out_shape=out_shape, in_specs=in_specs, out_specs=ou...  24.9 us
    ppermute x12, starting transfers between devices, trade(): lax.ppermute(x, axis, [(i, i ^ bit) for i in range(lax.axis_size(axis))])  15.8 us
    ppermute x1, starting transfers between devices, local(): near_top = lax.ppermute(last, both, route(near, 1))  4.61 us
    ppermute x1, waiting for transfers between devices, local(): bot = lax.ppermute(up, 'space', [(s + 1, s) for s in range(n_space - 1)])  4.37 us
    ppermute x1, waiting for transfers between devices, local(): near_bot = lax.ppermute(first, both, route(near, -1))  3.64 us
    ppermute x1, starting transfers between devices, local(): top = lax.ppermute(dn, 'space', [(s, s + 1) for s in range(n_space - 1)])  3.47 us
    ppermute x1, waiting for transfers between devices, local(): near_top = lax.ppermute(last, both, route(near, 1))  2.66 us
  transfers between devices with their start and end apart: 20, of which 16 were waited for; matrix products, arithmetic and copies ran while one was open for 1% of the time, Pallas kernels for 4%

profile of v3, /device:TPU:0, one launch (start us, length us, event | category | flops | bytes accessed | tf_op | source)
XLA Modules:
  0.0 97.5 jit_solution(433329869677514165)
XLA Ops:
  2.2 4.6 %collective-permute-start.1 = (bf16[512,256]{1,0:T(8,128)(2,1)S(1)}, bf16[512,256]{1,0:T(8,128)(2,1)S(1)}, u32[]{:S(2)}, u32[]{:S(2)}) collective-permute-start(bf16[512,256]{1,0:T(8,128)(2,1)S(1)} %bitcast.20), channel_id=1, source_target_pairs={{0,5},{1,6},{2,7},{4,1},{5,2},{6,3},{8,13},{9,14},{10,15},{12,9},{... | collective-permute-start | bytes 786440 | tf_op jit(solution)/shard_map/ppermute | solution.py:642
  10.2 2.7 %collective-permute-done.1.top = bf16[512,256]{1,0:T(8,128)(2,1)S(1)} collective-permute-done((bf16[512,256]{1,0:T(8,128)(2,1)S(1)}, bf16[512,256]{1,0:T(8,128)(2,1)S(1)}, u32[]{:S(2)}, u32[]{:S(2)}) %collective-permute-start.1) | collective-permute-done | bytes 262176 | tf_op jit(solution)/shard_map/ppermute | solution.py:642
  13.5 3.6 %collective-permute-done.2.bot = bf16[512,256]{1,0:T(8,128)(2,1)S(1)} collective-permute-done((bf16[512,256]{1,0:T(8,128)(2,1)S(1)}, bf16[512,256]{1,0:T(8,128)(2,1)S(1)}, u32[]{:S(2)}, u32[]{:S(2)}) %collective-permute-start.2) | collective-permute-done | bytes 262176 | tf_op jit(solution)/shard_map/ppermute | solution.py:643
  17.8 3.9 %near.1 = (bf16[96,1024]{1,0:T(8,128)(2,1)S(1)}, bf16[1024,256]{1,0:T(8,128)(2,1)S(1)}, bf16[2,8,128]{2,1,0:T(8,128)(2,1)S(1)}, s32[2,8,128]{2,1,0:T(8,128)S(1)}...) custom-call(bf16[1024,256]{1,0:T(8,128)(2,1)} %bitcast.17, ...), custom_call_target="tpu_custom_call" | custom-call | flops 4000000000 | bytes 13333333 | tf_op jit(solution)/shard_map/near/pallas_call | solution.py:601
  21.7 3.1 %code.1 = (bf16[192,1024]{1,0:T(8,128)(2,1)S(1)}, bf16[1024,128]{1,0:T(8,128)(2,1)S(1)}, bf16[528,128]{1,0:T(8,128)(2,1)S(1)}, bf16[528,128]{1,0:T(8,128)(2,1)S(1)}) custom-call(s32[1]{0:T(128)S(6)} %copy.26.order, bf16[1024,256]{1,0:T(8,128)(2,1)S(1)} %get-tuple-element.64.own, bf16[1024,256]{1,0:T(8,128)(2,1)S(1)} %collective-permute-done.3.mid, ...), custom_call_target="tpu_custom_call" | custom-call | flops 4000000000 | bytes 13333333 | tf_op jit(solution)/shard_map/code/pallas_call | solution.py:601
  24.8 3.5 %collective-permute-start.6 = (bf16[528,128]{1,0:T(8,128)(2,1)S(1)}, bf16[528,128]{1,0:T(8,128)(2,1)S(1)}, u32[]{:S(2)}, u32[]{:S(2)}) collective-permute-start(bf16[528,128]{1,0:T(8,128)(2,1)S(1)} %get-tuple-element.71), channel_id=1, source_target_pairs={{0,1},{1,2},{2,3},{4,5},{5,6},{6,7},{8,9},{9,10},{10,11},{12,13},{... | collective-permute-start | bytes 405512 | tf_op jit(solution)/shard_map/ppermute | solution.py:689
  30.8 4.4 %collective-permute-done.7.bot = bf16[528,128]{1,0:T(8,128)(2,1)S(1)} collective-permute-done((bf16[528,128]{1,0:T(8,128)(2,1)S(1)}, bf16[528,128]{1,0:T(8,128)(2,1)S(1)}, u32[]{:S(2)}, u32[]{:S(2)}) %collective-permute-start.7) | collective-permute-done | bytes 135200 | tf_op jit(solution)/shard_map/ppermute | solution.py:690
  36.3 6.4 %hidden.1 = (f32[2,8,128]{2,1,0:T(8,128)}, bf16[256,1024]{1,0:T(8,128)(2,1)S(1)}, bf16[1536,384]{1,0:T(8,128)(2,1)S(1)}, f32[1792,128]{1,0:T(8,128)S(1)}, f32[8,128]{1,0:T(8,128)S(1)}) custom-call(f32[2]{0:T(128)S(1)} %copy-done.1, bf16[1024,128]{1,0:T(8,128)(2,1)S(1)} %get-tuple-element.70.code, bf16[528,128]{1,0:T(8,128)(2,1)S(1)} %collective-permute-done.6.top, ...), custom_call_target="tpu_custom_call" | custom-call | flops 4000000000 | bytes 13333333 | tf_op jit(solution)/shard_map/hidden/pallas_call | solution.py:601
  42.7 4.3 %rest.1 = (f32[1920,128]{1,0:T(8,128)S(1)}, f32[1920,128]{1,0:T(8,128)S(1)}) custom-call(bf16[256,1024]{1,0:T(8,128)(2,1)S(1)} %get-tuple-element.79.jt, bf16[1536,384]{1,0:T(8,128)(2,1)S(1)} %get-tuple-element.80.s3, f32[1792,128]{1,0:T(8,128)S(1)} %get-tuple-element.81.d_motion, f32[1792,128]{1,0:T(8,128)S(1)} %get-tuple-element.82.d_flow, ...), custom_call_target="tpu_custom_call" | custom-call | flops 3000000000 | bytes 10000000 | tf_op jit(solution)/shard_map/rest/pallas_call | solution.py:601
  47.0 2.6 %collective-permute-start.8 = (f32[1920,128]{1,0:T(8,128)S(1)}, f32[1920,128]{1,0:T(8,128)S(1)}, u32[]{:S(2)}, u32[]{:S(2)}) collective-permute-start(f32[1920,128]{1,0:T(8,128)S(1)} %get-tuple-element.89), channel_id=1, source_target_pairs={{0,4},{4,0},{8,12},{12,8},{1,5},{5,1},{9,13},{13,9},{2,6},{6,2},{1... | collective-permute-start | bytes 2949128 | tf_op jit(solution)/shard_map/ppermute | solution.py:420
  49.7 2.1 %collective-permute-done.8.got = f32[1920,128]{1,0:T(8,128)S(1)} collective-permute-done((f32[1920,128]{1,0:T(8,128)S(1)}, f32[1920,128]{1,0:T(8,128)S(1)}, u32[]{:S(2)}, u32[]{:S(2)}) %collective-permute-start.8) | collective-permute-done | bytes 983072 | tf_op jit(solution)/shard_map/ppermute | solution.py:420
  52.5 1.6 %collective-permute-start.10 = (bf16[480,128]{1,0:T(8,128)(2,1)S(1)}, bf16[480,128]{1,0:T(8,128)(2,1)S(1)}, u32[]{:S(2)}, u32[]{:S(2)}) collective-permute-start(bf16[480,128]{1,0:T(8,128)(2,1)S(1)} %get-tuple-element.93), channel_id=1, source_target_pairs={{0,1},{1,0},{2,3},{3,2},{4,5},{5,4},{6,7},{7,6},{8,9},{9,8},{10,11... | collective-permute-start | bytes 368648 | tf_op jit(solution)/shard_map/ppermute | solution.py:420
  54.1 2.8 %collective-permute-start.9 = (bf16[480,128]{1,0:T(8,128)(2,1)S(1)}, bf16[480,128]{1,0:T(8,128)(2,1)S(1)}, u32[]{:S(2)}, u32[]{:S(2)}) collective-permute-start(bf16[480,128]{1,0:T(8,128)(2,1)S(1)} %get-tuple-element.91), channel_id=1, source_target_pairs={{0,8},{4,12},{8,0},{12,4},{1,9},{5,13},{9,1},{13,5},{2,10},{6,14},... | collective-permute-start | bytes 368648 | tf_op jit(solution)/shard_map/ppermute | solution.py:420
  58.2 2.1 %collective-permute-done.9.a_got = bf16[480,128]{1,0:T(8,128)(2,1)S(1)} collective-permute-done((bf16[480,128]{1,0:T(8,128)(2,1)S(1)}, bf16[480,128]{1,0:T(8,128)(2,1)S(1)}, u32[]{:S(2)}, u32[]{:S(2)}) %collective-permute-start.9) | collective-permute-done | bytes 122912 | tf_op jit(solution)/shard_map/ppermute | solution.py:420
  61.4 1.7 %collective-permute-start.12 = (f32[240,128]{1,0:T(8,128)S(1)}, f32[240,128]{1,0:T(8,128)S(1)}, u32[]{:S(2)}, u32[]{:S(2)}) collective-permute-start(f32[240,128]{1,0:T(8,128)S(1)} %get-tuple-element.97), channel_id=1, source_target_pairs={{0,8},{4,12},{8,0},{12,4},{1,9},{5,13},{9,1},{13,5},{2,10},{6,14},... | collective-permute-start | bytes 368648 | tf_op jit(solution)/shard_map/ppermute | solution.py:420
  63.2 2.7 %collective-permute-done.11.a_got = f32[240,128]{1,0:T(8,128)S(1)} collective-permute-done((f32[240,128]{1,0:T(8,128)S(1)}, f32[240,128]{1,0:T(8,128)S(1)}, u32[]{:S(2)}, u32[]{:S(2)}) %collective-permute-start.11) | collective-permute-done | bytes 122912 | tf_op jit(solution)/shard_map/ppermute | solution.py:420
  68.0 6.2 %collective-permute-done.13.got = f32[240,128]{1,0:T(8,128)S(1)} collective-permute-done((f32[240,128]{1,0:T(8,128)S(1)}, f32[240,128]{1,0:T(8,128)S(1)}, u32[]{:S(2)}, u32[]{:S(2)}) %collective-permute-start.13) | collective-permute-done | bytes 122912 | tf_op jit(solution)/shard_map/ppermute | solution.py:420
  74.9 5.6 %collective-permute-done.14.got = bf16[240,128]{1,0:T(8,128)(2,1)S(1)} collective-permute-done((bf16[240,128]{1,0:T(8,128)(2,1)S(1)}, bf16[240,128]{1,0:T(8,128)(2,1)S(1)}, u32[]{:S(2)}, u32[]{:S(2)}) %collective-permute-start.14) | collective-permute-done | bytes 61472 | tf_op jit(solution)/shard_map/ppermute | solution.py:420
  82.9 2.6 %collective-permute-done.15.a_got = bf16[240,128]{1,0:T(8,128)(2,1)S(1)} collective-permute-done((bf16[240,128]{1,0:T(8,128)(2,1)S(1)}, bf16[240,128]{1,0:T(8,128)(2,1)S(1)}, u32[]{:S(2)}, u32[]{:S(2)}) %collective-permute-start.15) | collective-permute-done | bytes 61472 | tf_op jit(solution)/shard_map/ppermute | solution.py:420
  86.2 1.9 %collective-permute-start.17 = (bf16[480,128]{1,0:T(8,128)(2,1)S(1)}, bf16[480,128]{1,0:T(8,128)(2,1)S(1)}, u32[]{:S(2)}, u32[]{:S(2)}) collective-permute-start(bf16[480,128]{1,0:T(8,128)(2,1)S(1)} %get-tuple-element.102.a_mine), channel_id=1, source_target_pairs={{0,8},{4,12},{8,0},{12,4},{1,9},{5,13},{9,1},{13,5},{2,10},{6,14},... | collective-permute-start | bytes 368648 | tf_op jit(solution)/shard_map/ppermute | solution.py:420
  89.6 1.5 %collective-permute-done.17.a_got = bf16[480,128]{1,0:T(8,128)(2,1)S(1)} collective-permute-done((bf16[480,128]{1,0:T(8,128)(2,1)S(1)}, bf16[480,128]{1,0:T(8,128)(2,1)S(1)}, u32[]{:S(2)}, u32[]{:S(2)}) %collective-permute-start.17) | collective-permute-done | bytes 122912 | tf_op jit(solution)/shard_map/ppermute | solution.py:420
  91.2 1.8 %collective-permute-done.18.b_got = bf16[480,128]{1,0:T(8,128)(2,1)S(1)} collective-permute-done((bf16[480,128]{1,0:T(8,128)(2,1)S(1)}, bf16[480,128]{1,0:T(8,128)(2,1)S(1)}, u32[]{:S(2)}, u32[]{:S(2)}) %collective-permute-start.18) | collective-permute-done | bytes 122912 | tf_op jit(solution)/shard_map/ppermute | solution.py:420
  93.6 1.9 %collective-permute-done.19.other = bf16[1920,128]{1,0:T(8,128)(2,1)S(1)} collective-permute-done((bf16[1920,128]{1,0:T(8,128)(2,1)S(1)}, bf16[1920,128]{1,0:T(8,128)(2,1)S(1)}, u32[]{:S(2)}, u32[]{:S(2)}) %collective-permute-start.19) | collective-permute-done | bytes 491552 | tf_op jit(solution)/shard_map/ppermute | solution.py:420
  95.5 2.0 %finish.1 = (f32[3,3,256,128]{3,2,1,0:T(8,128)}, f32[3,3,128,128]{3,2,1,0:T(8,128)}, f32[162,128]{1,0:T(8,128)}, f32[7,7,2,128]{3,2,1,0:T(2,128)}, f32[128]{0:T(...) custom-call(s32[4]{0:T(128)S(1)} %pad_add_fusion.bits, ...), custom_call_target="tpu_custom_call" | custom-call | flops 100000000 | bytes 333333 | tf_op jit(solution)/shard_map/finish/pallas_call | solution.py:601
  (35 shorter events, 20.4 us)
Async XLA Ops:
  0.6 16.5 %collective-permute-start = (bf16[1024,256]{1,0:T(8,128)(2,1)}, bf16[1024,256]{1,0:T(8,128)(2,1)S(1)}, u32[]{:S(2)}, u32[]{:S(2)}) collective-permute-start(bf16[1024,256]{1,0:T(8,128)(2,1)} %bitcast.15), channel_id=1, source_target_pairs={{0,4},{1,5},{2,6},{3,7},{4,0},{5,1},{6,2},{7,3},{8,12},{9,13},{10,... | collective-permute-start | bytes 1572872 | tf_op jit(solution)/shard_map/ppermute | solution.py:644
  2.2 10.6 %collective-permute-start.1 = (bf16[512,256]{1,0:T(8,128)(2,1)S(1)}, bf16[512,256]{1,0:T(8,128)(2,1)S(1)}, u32[]{:S(2)}, u32[]{:S(2)}) collective-permute-start(bf16[512,256]{1,0:T(8,128)(2,1)S(1)} %bitcast.20), channel_id=1, source_target_pairs={{0,5},{1,6},{2,7},{4,1},{5,2},{6,3},{8,13},{9,14},{10,15},{12,9},{... | collective-permute-start | bytes 786440 | tf_op jit(solution)/shard_map/ppermute | solution.py:642
  6.8 10.3 %collective-permute-start.2 = (bf16[512,256]{1,0:T(8,128)(2,1)S(1)}, bf16[512,256]{1,0:T(8,128)(2,1)S(1)}, u32[]{:S(2)}, u32[]{:S(2)}) collective-permute-start(bf16[512,256]{1,0:T(8,128)(2,1)S(1)} %bitcast.18), channel_id=1, source_target_pairs={{1,4},{2,5},{3,6},{5,0},{6,1},{7,2},{9,12},{10,13},{11,14},{13,8},... | collective-permute-start | bytes 786440 | tf_op jit(solution)/shard_map/ppermute | solution.py:643
  8.1 13.6 %collective-permute-start.3 = (bf16[1024,256]{1,0:T(8,128)(2,1)}, bf16[1024,256]{1,0:T(8,128)(2,1)S(1)}, u32[]{:S(2)}, u32[]{:S(2)}) collective-permute-start(bf16[1024,256]{1,0:T(8,128)(2,1)} %bitcast.16), channel_id=1, source_target_pairs={{4,8},{5,9},{6,10},{7,11},{8,4},{9,5},{10,6},{11,7},{20,24},{21,25... | collective-permute-start | bytes 1572872 | tf_op jit(solution)/shard_map/ppermute | solution.py:647
  8.8 12.8 %collective-permute-start.4 = (bf16[512,256]{1,0:T(8,128)(2,1)S(1)}, bf16[512,256]{1,0:T(8,128)(2,1)S(1)}, u32[]{:S(2)}, u32[]{:S(2)}) collective-permute-start(bf16[512,256]{1,0:T(8,128)(2,1)S(1)} %bitcast.21), channel_id=1, source_target_pairs={{4,9},{5,10},{6,11},{8,5},{9,6},{10,7},{20,25},{21,26},{22,27},{24... | collective-permute-start | bytes 786440 | tf_op jit(solution)/shard_map/ppermute | solution.py:645
  12.8 8.9 %collective-permute-start.5 = (bf16[512,256]{1,0:T(8,128)(2,1)S(1)}, bf16[512,256]{1,0:T(8,128)(2,1)S(1)}, u32[]{:S(2)}, u32[]{:S(2)}) collective-permute-start(bf16[512,256]{1,0:T(8,128)(2,1)S(1)} %bitcast.19), channel_id=1, source_target_pairs={{5,8},{6,9},{7,10},{9,4},{10,5},{11,6},{21,24},{22,25},{23,26},{25... | collective-permute-start | bytes 786440 | tf_op jit(solution)/shard_map/ppermute | solution.py:646
  17.1 0.7 copy-start
  24.8 6.0 %collective-permute-start.6 = (bf16[528,128]{1,0:T(8,128)(2,1)S(1)}, bf16[528,128]{1,0:T(8,128)(2,1)S(1)}, u32[]{:S(2)}, u32[]{:S(2)}) collective-permute-start(bf16[528,128]{1,0:T(8,128)(2,1)S(1)} %get-tuple-element.71), channel_id=1, source_target_pairs={{0,1},{1,2},{2,3},{4,5},{5,6},{6,7},{8,9},{9,10},{10,11},{12,13},{... | collective-permute-start | bytes 405512 | tf_op jit(solution)/shard_map/ppermute | solution.py:689
  28.3 6.9 %collective-permute-start.7 = (bf16[528,128]{1,0:T(8,128)(2,1)S(1)}, bf16[528,128]{1,0:T(8,128)(2,1)S(1)}, u32[]{:S(2)}, u32[]{:S(2)}) collective-permute-start(bf16[528,128]{1,0:T(8,128)(2,1)S(1)} %get-tuple-element.72), channel_id=1, source_target_pairs={{1,0},{2,1},{3,2},{5,4},{6,5},{7,6},{9,8},{10,9},{11,10},{13,12},{... | collective-permute-start | bytes 405512 | tf_op jit(solution)/shard_map/ppermute | solution.py:690
  35.2 1.1 %copy-start.1 = (f32[2]{0:T(128)S(1)}, f32[2]{0:T(128)}, u32[]{:S(2)}) copy-start(f32[2]{0:T(128)} %b_head.1) | copy-start | bytes 28
  47.0 4.8 %collective-permute-start.8 = (f32[1920,128]{1,0:T(8,128)S(1)}, f32[1920,128]{1,0:T(8,128)S(1)}, u32[]{:S(2)}, u32[]{:S(2)}) collective-permute-start(f32[1920,128]{1,0:T(8,128)S(1)} %get-tuple-element.89), channel_id=1, source_target_pairs={{0,4},{4,0},{8,12},{12,8},{1,5},{5,1},{9,13},{13,9},{2,6},{6,2},{1... | collective-permute-start | bytes 2949128 | tf_op jit(solution)/shard_map/ppermute | solution.py:420
  52.5 5.7 %collective-permute-start.10 = (bf16[480,128]{1,0:T(8,128)(2,1)S(1)}, bf16[480,128]{1,0:T(8,128)(2,1)S(1)}, u32[]{:S(2)}, u32[]{:S(2)}) collective-permute-start(bf16[480,128]{1,0:T(8,128)(2,1)S(1)} %get-tuple-element.93), channel_id=1, source_target_pairs={{0,1},{1,0},{2,3},{3,2},{4,5},{5,4},{6,7},{7,6},{8,9},{9,8},{10,11... | collective-permute-start | bytes 368648 | tf_op jit(solution)/shard_map/ppermute | solution.py:420
  54.1 6.1 %collective-permute-start.9 = (bf16[480,128]{1,0:T(8,128)(2,1)S(1)}, bf16[480,128]{1,0:T(8,128)(2,1)S(1)}, u32[]{:S(2)}, u32[]{:S(2)}) collective-permute-start(bf16[480,128]{1,0:T(8,128)(2,1)S(1)} %get-tuple-element.91), channel_id=1, source_target_pairs={{0,8},{4,12},{8,0},{12,4},{1,9},{5,13},{9,1},{13,5},{2,10},{6,14},... | collective-permute-start | bytes 368648 | tf_op jit(solution)/shard_map/ppermute | solution.py:420
  60.9 4.9 %collective-permute-start.11 = (f32[240,128]{1,0:T(8,128)S(1)}, f32[240,128]{1,0:T(8,128)S(1)}, u32[]{:S(2)}, u32[]{:S(2)}) collective-permute-start(f32[240,128]{1,0:T(8,128)S(1)} %get-tuple-element.95), channel_id=1, source_target_pairs={{0,1},{1,0},{2,3},{3,2},{4,5},{5,4},{6,7},{7,6},{8,9},{9,8},{10,11... | collective-permute-start | bytes 368648 | tf_op jit(solution)/shard_map/ppermute | solution.py:420
  61.4 4.9 %collective-permute-start.12 = (f32[240,128]{1,0:T(8,128)S(1)}, f32[240,128]{1,0:T(8,128)S(1)}, u32[]{:S(2)}, u32[]{:S(2)}) collective-permute-start(f32[240,128]{1,0:T(8,128)S(1)} %get-tuple-element.97), channel_id=1, source_target_pairs={{0,8},{4,12},{8,0},{12,4},{1,9},{5,13},{9,1},{13,5},{2,10},{6,14},... | collective-permute-start | bytes 368648 | tf_op jit(solution)/shard_map/ppermute | solution.py:420
  66.9 7.3 %collective-permute-start.13 = (f32[240,128]{1,0:T(8,128)S(1)}, f32[240,128]{1,0:T(8,128)S(1)}, u32[]{:S(2)}, u32[]{:S(2)}) collective-permute-start(f32[240,128]{1,0:T(8,128)S(1)} %get-tuple-element.99), channel_id=1, source_target_pairs={{0,2},{1,3},{2,0},{3,1},{4,6},{5,7},{6,4},{7,5},{8,10},{9,11},{10,... | collective-permute-start | bytes 368648 | tf_op jit(solution)/shard_map/ppermute | solution.py:420
  74.8 5.7 %collective-permute-start.14 = (bf16[240,128]{1,0:T(8,128)(2,1)S(1)}, bf16[240,128]{1,0:T(8,128)(2,1)S(1)}, u32[]{:S(2)}, u32[]{:S(2)}) collective-permute-start(bf16[240,128]{1,0:T(8,128)(2,1)S(1)} %last.1.mine), channel_id=1, source_target_pairs={{0,2},{1,3},{2,0},{3,1},{4,6},{5,7},{6,4},{7,5},{8,10},{9,11},{10,... | collective-permute-start | bytes 184328 | tf_op jit(solution)/shard_map/ppermute | solution.py:420
  81.0 4.5 %collective-permute-start.15 = (bf16[240,128]{1,0:T(8,128)(2,1)S(1)}, bf16[240,128]{1,0:T(8,128)(2,1)S(1)}, u32[]{:S(2)}, u32[]{:S(2)}) collective-permute-start(bf16[240,128]{1,0:T(8,128)(2,1)S(1)} %get-tuple-element.100.a_mine), channel_id=1, source_target_pairs={{0,1},{1,0},{2,3},{3,2},{4,5},{5,4},{6,7},{7,6},{8,9},{9,8},{10,11... | collective-permute-start | bytes 184328 | tf_op jit(solution)/shard_map/ppermute | solution.py:420
  81.4 4.2 %collective-permute-start.16 = (bf16[240,128]{1,0:T(8,128)(2,1)S(1)}, bf16[240,128]{1,0:T(8,128)(2,1)S(1)}, u32[]{:S(2)}, u32[]{:S(2)}) collective-permute-start(bf16[240,128]{1,0:T(8,128)(2,1)S(1)} %get-tuple-element.101.b_mine), channel_id=1, source_target_pairs={{0,8},{4,12},{8,0},{12,4},{1,9},{5,13},{9,1},{13,5},{2,10},{6,14},... | collective-permute-start | bytes 184328 | tf_op jit(solution)/shard_map/ppermute | solution.py:420
  86.2 4.9 %collective-permute-start.17 = (bf16[480,128]{1,0:T(8,128)(2,1)S(1)}, bf16[480,128]{1,0:T(8,128)(2,1)S(1)}, u32[]{:S(2)}, u32[]{:S(2)}) collective-permute-start(bf16[480,128]{1,0:T(8,128)(2,1)S(1)} %get-tuple-element.102.a_mine), channel_id=1, source_target_pairs={{0,8},{4,12},{8,0},{12,4},{1,9},{5,13},{9,1},{13,5},{2,10},{6,14},... | collective-permute-start | bytes 368648 | tf_op jit(solution)/shard_map/ppermute | solution.py:420
  88.1 4.9 %collective-permute-start.18 = (bf16[480,128]{1,0:T(8,128)(2,1)S(1)}, bf16[480,128]{1,0:T(8,128)(2,1)S(1)}, u32[]{:S(2)}, u32[]{:S(2)}) collective-permute-start(bf16[480,128]{1,0:T(8,128)(2,1)S(1)} %get-tuple-element.103.b_mine), channel_id=1, source_target_pairs={{0,1},{1,0},{2,3},{3,2},{4,5},{5,4},{6,7},{7,6},{8,9},{9,8},{10,11... | collective-permute-start | bytes 368648 | tf_op jit(solution)/shard_map/ppermute | solution.py:420
  93.6 1.9 %collective-permute-start.19 = (bf16[1920,128]{1,0:T(8,128)(2,1)S(1)}, bf16[1920,128]{1,0:T(8,128)(2,1)S(1)}, u32[]{:S(2)}, u32[]{:S(2)}) collective-permute-start(bf16[1920,128]{1,0:T(8,128)(2,1)S(1)} %merge3.1.mine), channel_id=1, source_target_pairs={{0,4},{4,0},{8,12},{12,8},{1,5},{5,1},{9,13},{13,9},{2,6},{6,2},{1... | collective-permute-start | bytes 1474568 | tf_op jit(solution)/shard_map/ppermute | solution.py:420

commit v4 on v3

--- a/solution.py
+++ b/solution.py
@@ -451,110 +451,43 @@
     return ref[pl.ds(pl.multiple_of(which * half, 8), half), :]
 
 
-def first_split(at, bits, keep, got, a_keep, a_send, b_keep, b_send, total):
-    quarter = a_keep.shape[0]
-    total[...] = keep[...] + got[...]
-    for part, (k, s, bit) in enumerate(((a_keep, a_send, bits[1]), (b_keep, b_send, bits[2]))):
-        k[...] = total[pl.ds(pl.multiple_of((2 * part + bit) * quarter, 8), quarter), :]
-        s[...] = total[pl.ds(pl.multiple_of((2 * part + 1 - bit) * quarter, 8), quarter), :].astype(s.dtype)
-    @pl.when(jnp.logical_and(bits[0] == 1, bits[2] == 0))
-    def _():
-        value = total[3 * quarter + at : 3 * quarter + at + MISC_ROWS, :]
-        b_send[at : at + 4 * MISC_ROWS, :] = split3(value, True)
-
-
-def second_split(at, bits, a_keep, a_got, b_keep, b_got, a_mine, a_send, b_mine, b_send, total):
-    half = a_mine.shape[0]
-    for is_b, (keep, got, mine, send, bit) in enumerate((
-        (a_keep, a_got, a_mine, a_send, bits[2]),
-        (b_keep, b_got, b_mine, b_send, bits[1]),
-    )):
-        total[...] = keep[...] + got[...].astype(F32)
-        if is_b:
-
-            @pl.when(jnp.logical_and(bits[0] == 1, bits[2] == 1))
-            def _():
-                terms = got[at : at + 4 * MISC_ROWS, :].astype(F32)
-                value = keep[at : at + MISC_ROWS, :]
-                for k in range(3):
-                    value = value + terms[k * MISC_ROWS : (k + 1) * MISC_ROWS]
-                total[at : at + MISC_ROWS, :] = value
-                total[at + MISC_ROWS : at + 4 * MISC_ROWS, :] = jnp.zeros((3 * MISC_ROWS, value.shape[1]), F32)
-
-        mine[...] = pick(total, bit, half)
-        send[...] = pick(total, 1 - bit, half)
-
-
-def third_split(bits, a_keep, a_got, b_keep, b_got, keep, send, total):
-    n = a_keep.shape[0]
-    total[0:n, :] = a_keep[...] + a_got[...]
-    total[n : 2 * n, :] = b_keep[...] + b_got[...]
-    keep[...] = pick(total, bits[3], n)
-    send[...] = pick(total, 1 - bits[3], n)
-
-
-def last_sum(at, bits, keep, got, out, total):
-    total[...] = keep[...] + got[...]
-    value = total[at : at + MISC_ROWS, :]
-    mid = value - value.astype(BF).astype(F32)
-    low = mid - mid.astype(BF).astype(F32)
-    is_last = bits[0] + bits[1] + bits[2] + bits[3] == 4
-    total[at + MISC_ROWS : at + 2 * MISC_ROWS, :] = jnp.where(is_last, mid, total[at + MISC_ROWS : at + 2 * MISC_ROWS, :])
-    total[at + 2 * MISC_ROWS : at + 3 * MISC_ROWS, :] = jnp.where(
-        is_last, low, total[at + 2 * MISC_ROWS : at + 3 * MISC_ROWS, :]
-    )
-    out[...] = total[...].astype(BF)
-
-
-def first_merge(bits, mine, got, a_out, b_out):
-    first = bits[3] == 0
-    a_out[...] = jnp.where(first, mine[...], got[...])
-    b_out[...] = jnp.where(first, got[...], mine[...])
-
-
-def pair_merge(x_first, bits, a_mine, a_got, b_mine, b_got, a_out, b_out):
-    n = a_mine.shape[0]
-    a_bit, b_bit = (bits[1], bits[2]) if x_first else (bits[2], bits[1])
-    for mine, got, out, bit in ((a_mine, a_got, a_out, a_bit), (b_mine, b_got, b_out, b_bit)):
-        out[pl.ds(pl.multiple_of(bit * n, 16), n), :] = mine[...]
-        out[pl.ds(pl.multiple_of((1 - bit) * n, 16), n), :] = got[...]
-
-
-def join_merge(bits, a_mine, a_got, b_mine, b_got, out):
-    n = a_mine.shape[0]
-    for at, (mine, got, bit) in enumerate(((a_mine, a_got, bits[1]), (b_mine, b_got, bits[2]))):
-        out[pl.ds(pl.multiple_of((2 * at + bit) * n, 16), n), :] = mine[...]
-        out[pl.ds(pl.multiple_of((2 * at + 1 - bit) * n, 16), n), :] = got[...]
-
-
-def paired_reduce(bits, keep, got, at_misc, shape):
-    half, C = keep.shape
+def cut(x, which, n):
+    return lax.dynamic_slice_in_dim(x, which * n, n, 0)
+
+
+def ordered(mine, got, axis, bit):
+    return jnp.where(upper_of(axis, bit) == 0, jnp.concatenate([mine, got]), jnp.concatenate([got, mine]))
+
+
+def paired_reduce(x_sum, at_misc):
+    half = x_sum.shape[0]
     x, z, far_z = ("tm", 2), ("space", 1), ("space", 2)
-
-    def stage(body, name, dtypes, n, scratch, *args):
-        out = tuple(shape(n, C, dtype=dtype) for dtype in dtypes)
-        return call(
-            body, name, out, [SMEM] + [VMEM] * len(args),
-            [pltpu.VMEM((scratch, C), F32)] if scratch else [], 10_000_000, bits, *args,
-        )
-
-    first_at = at_misc - 2 * half + half // 4
-    ak, as_, bk, bs = stage(functools.partial(first_split, first_at), "split1", (F32, BF, F32, BF), half // 4, half, keep, got)
-    ag, bg = trade(as_, *x), trade(bs, *z)
-    ak, as_, bk, bs = stage(functools.partial(second_split, first_at), "split2", (F32,) * 4, half // 8, half // 4, ak, ag, bk, bg)
-    ag, bg = trade(as_, *z), trade(bs, *x)
-    keep, send = stage(third_split, "split3", (F32, F32), half // 8, half // 4, ak, ag, bk, bg)
-    got = trade(send, *far_z)
-    chunk = half // 8
-    (y,) = stage(
-        functools.partial(last_sum, at_misc - (2 * half - chunk)), "last", (BF,), chunk, chunk, keep, got
-    )
-    a, b = stage(first_merge, "merge1", (BF, BF), chunk, 0, y, trade(y, *far_z))
-    a, b = stage(
-        functools.partial(pair_merge, False), "merge2", (BF, BF), half // 4, 0, a, trade(a, *z), b, trade(b, *x)
-    )
-    (out,) = stage(join_merge, "merge3", (BF,), half, 0, a, trade(a, *x), b, trade(b, *z))
-    return out
+    upper_x, upper_z, upper_far, core = upper_of(*x), upper_of(*z), upper_of(*far_z), upper_of("tm", 1)
+    a, b = x_sum[: half // 2], x_sum[half // 2 :]
+    n = half // 4
+    at = at_misc - 2 * half + n
+    sends = jnp.logical_and(core == 1, upper_z == 0)
+    holds = jnp.logical_and(core == 1, upper_z == 1)
+    a_got = trade(cut(a, 1 - upper_x, n).astype(BF), *x)
+    b_got = trade(three_terms(cut(b, 1 - upper_z, n), at, sends), *z)
+    a = cut(a, upper_x, n) + a_got.astype(F32)
+    b = cut(b, upper_z, n)
+    got = b_got.astype(F32)
+    misc = b[at : at + MISC_ROWS] + sum(got[at + k * MISC_ROWS : at + (k + 1) * MISC_ROWS] for k in range(3))
+    fixed = jnp.concatenate([misc, jnp.zeros((2 * MISC_ROWS, misc.shape[1]), F32)])
+    b = b + got
+    b = jnp.concatenate([b[:at], jnp.where(holds, fixed, b[at : at + 3 * MISC_ROWS]), b[at + 3 * MISC_ROWS :]])
+    n = half // 8
+    a_got, b_got = trade(cut(a, 1 - upper_z, n), *z), trade(cut(b, 1 - upper_x, n), *x)
+    a, b = cut(a, upper_z, n) + a_got, cut(b, upper_x, n) + b_got
+    is_far = upper_far == 1
+    y = jnp.where(is_far, b, a) + trade(jnp.where(is_far, a, b), *far_z)
+    y = three_terms(y, at_misc - (2 * half - n), core + upper_x + upper_z + upper_far == 4)
+    got = trade(y, *far_z)
+    a, b = jnp.where(is_far, got, y), jnp.where(is_far, y, got)
+    a, b = ordered(a, trade(a, *z), *z), ordered(b, trade(b, *x), *x)
+    a, b = ordered(a, trade(a, *x), *x), ordered(b, trade(b, *z), *z)
+    return jnp.concatenate([a, b])
 
 
 def finish_kernel(
@@ -752,7 +685,7 @@
     bits = jnp.stack([upper_of("tm", 1), upper_of("tm", 2), upper_of("space", 1), upper_of("space", 2)])
     bits = bits.astype(jnp.int32)
     if paired:
-        mine = paired_reduce(bits, keep, got, at_misc, shape)
+        mine = paired_reduce(keep + got, at_misc)
     else:
         mine = halving_reduce(keep + got, bits_of("tm")[1:] + bits_of("space"), upper_of(*core))
     other = trade(mine, *core)

time: 97.8 us -> 94 us (0.961)
  Pallas kernels: 24.9 us -> 20.7 us
  starting transfers between devices: 29 us -> 27.5 us
  waiting for transfers between devices: 40.2 us -> 41.3 us
    pallas_call x13 -> x6, Pallas kernels: 24.9 us -> 20.7 us  [call(): pl.pallas_call(body, out_shape=out_shape, in_specs=in_specs, out_specs=ou...]
    ppermute x12, starting transfers between devices: 15.8 us -> 14.3 us  [trade(): lax.ppermute(x, axis, [(i, i ^ bit) for i in range(lax.axis_size(axis))])]
    ppermute x12, waiting for transfers between devices: 28.3 us -> 29.4 us  [trade(): lax.ppermute(x, axis, [(i, i ^ bit) for i in range(lax.axis_size(axis))])]
  transfers between devices with their start and end apart: 20 -> 20, of which waited for: 16 -> 15; matrix products, arithmetic and copies ran while one was open for 1% -> 2% of each run, Pallas kernels for 4% -> 4%
where the time goes in v4:
time: 94 us; the launch traced here: 93.7 us
  waiting for transfers between devices  41.3 us (44%)
  starting transfers between devices  27.5 us (29%)
  Pallas kernels  20.7 us (22%)
  local copies, waits for them, and re-layouts  1.9 us (2%)
  between operations  1.6 us (2%)
    ppermute x12, waiting for transfers between devices, trade(): lax.ppermute(x, axis, [(i, i ^ bit) for i in range(lax.axis_size(axis))])  29.4 us
    pallas_call x6, Pallas kernels, call(): pl.pallas_call(body, out_shape=out_shape, in_specs=in_specs, out_specs=ou...  20.7 us
    ppermute x12, starting transfers between devices, trade(): lax.ppermute(x, axis, [(i, i ^ bit) for i in range(lax.axis_size(axis))])  14.3 us
    ppermute x1, starting transfers between devices, local(): near_top = lax.ppermute(last, both, route(near, 1))  4.61 us
    ppermute x1, waiting for transfers between devices, local(): bot = lax.ppermute(up, 'space', [(s + 1, s) for s in range(n_space - 1)])  4.37 us
    ppermute x1, waiting for transfers between devices, local(): near_bot = lax.ppermute(first, both, route(near, -1))  3.64 us
    ppermute x1, starting transfers between devices, local(): top = lax.ppermute(dn, 'space', [(s, s + 1) for s in range(n_space - 1)])  3.47 us
    ppermute x1, waiting for transfers between devices, local(): near_top = lax.ppermute(last, both, route(near, 1))  2.66 us
  transfers between devices with their start and end apart: 20, of which 15 were waited for; matrix products, arithmetic and copies ran while one was open for 2% of the time, Pallas kernels for 4%

profile of v4, /device:TPU:0, one launch (start us, length us, event | category | flops | bytes accessed | tf_op | source)
XLA Modules:
  0.0 93.7 jit_solution(16198584500741760980)
XLA Ops:
  2.2 4.6 %collective-permute-start.1 = (bf16[512,256]{1,0:T(8,128)(2,1)S(1)}, bf16[512,256]{1,0:T(8,128)(2,1)S(1)}, u32[]{:S(2)}, u32[]{:S(2)}) collective-permute-start(bf16[512,256]{1,0:T(8,128)(2,1)S(1)} %bitcast.20), channel_id=1, source_target_pairs={{0,5},{1,6},{2,7},{4,1},{5,2},{6,3},{8,13},{9,14},{10,15},{12,9},{... | collective-permute-start | bytes 786440 | tf_op jit(solution)/shard_map/ppermute | solution.py:575
  6.8 1.3 %collective-permute-start.2 = (bf16[512,256]{1,0:T(8,128)(2,1)S(1)}, bf16[512,256]{1,0:T(8,128)(2,1)S(1)}, u32[]{:S(2)}, u32[]{:S(2)}) collective-permute-start(bf16[512,256]{1,0:T(8,128)(2,1)S(1)} %bitcast.18), channel_id=1, source_target_pairs={{1,4},{2,5},{3,6},{5,0},{6,1},{7,2},{9,12},{10,13},{11,14},{13,8},... | collective-permute-start | bytes 786440 | tf_op jit(solution)/shard_map/ppermute | solution.py:576
  10.2 2.7 %collective-permute-done.1.top = bf16[512,256]{1,0:T(8,128)(2,1)S(1)} collective-permute-done((bf16[512,256]{1,0:T(8,128)(2,1)S(1)}, bf16[512,256]{1,0:T(8,128)(2,1)S(1)}, u32[]{:S(2)}, u32[]{:S(2)}) %collective-permute-start.1) | collective-permute-done | bytes 262176 | tf_op jit(solution)/shard_map/ppermute | solution.py:575
  13.5 3.6 %collective-permute-done.2.bot = bf16[512,256]{1,0:T(8,128)(2,1)S(1)} collective-permute-done((bf16[512,256]{1,0:T(8,128)(2,1)S(1)}, bf16[512,256]{1,0:T(8,128)(2,1)S(1)}, u32[]{:S(2)}, u32[]{:S(2)}) %collective-permute-start.2) | collective-permute-done | bytes 262176 | tf_op jit(solution)/shard_map/ppermute | solution.py:576
  17.8 3.9 %near.1 = (bf16[96,1024]{1,0:T(8,128)(2,1)S(1)}, bf16[1024,256]{1,0:T(8,128)(2,1)S(1)}, bf16[2,8,128]{2,1,0:T(8,128)(2,1)S(1)}, s32[2,8,128]{2,1,0:T(8,128)S(1)}...) custom-call(bf16[1024,256]{1,0:T(8,128)(2,1)} %bitcast.17, ...), custom_call_target="tpu_custom_call" | custom-call | flops 4000000000 | bytes 13333333 | tf_op jit(solution)/shard_map/near/pallas_call | solution.py:534
  21.7 3.1 %code.1 = (bf16[192,1024]{1,0:T(8,128)(2,1)S(1)}, bf16[1024,128]{1,0:T(8,128)(2,1)S(1)}, bf16[528,128]{1,0:T(8,128)(2,1)S(1)}, bf16[528,128]{1,0:T(8,128)(2,1)S(1)}) custom-call(s32[1]{0:T(128)S(6)} %copy.26.order, bf16[1024,256]{1,0:T(8,128)(2,1)S(1)} %get-tuple-element.50.own, bf16[1024,256]{1,0:T(8,128)(2,1)S(1)} %collective-permute-done.3.mid, ...), custom_call_target="tpu_custom_call" | custom-call | flops 4000000000 | bytes 13333333 | tf_op jit(solution)/shard_map/code/pallas_call | solution.py:534
  24.8 3.5 %collective-permute-start.6 = (bf16[528,128]{1,0:T(8,128)(2,1)S(1)}, bf16[528,128]{1,0:T(8,128)(2,1)S(1)}, u32[]{:S(2)}, u32[]{:S(2)}) collective-permute-start(bf16[528,128]{1,0:T(8,128)(2,1)S(1)} %get-tuple-element.57), channel_id=1, source_target_pairs={{0,1},{1,2},{2,3},{4,5},{5,6},{6,7},{8,9},{9,10},{10,11},{12,13},{... | collective-permute-start | bytes 405512 | tf_op jit(solution)/shard_map/ppermute | solution.py:622
  30.8 4.4 %collective-permute-done.7.bot = bf16[528,128]{1,0:T(8,128)(2,1)S(1)} collective-permute-done((bf16[528,128]{1,0:T(8,128)(2,1)S(1)}, bf16[528,128]{1,0:T(8,128)(2,1)S(1)}, u32[]{:S(2)}, u32[]{:S(2)}) %collective-permute-start.7) | collective-permute-done | bytes 135200 | tf_op jit(solution)/shard_map/ppermute | solution.py:623
  36.3 6.4 %hidden.1 = (f32[2,8,128]{2,1,0:T(8,128)}, bf16[256,1024]{1,0:T(8,128)(2,1)S(1)}, bf16[1536,384]{1,0:T(8,128)(2,1)S(1)}, f32[1792,128]{1,0:T(8,128)S(1)}, f32[8,128]{1,0:T(8,128)S(1)}) custom-call(f32[2]{0:T(128)S(1)} %copy-done.1, bf16[1024,128]{1,0:T(8,128)(2,1)S(1)} %get-tuple-element.56.code, bf16[528,128]{1,0:T(8,128)(2,1)S(1)} %collective-permute-done.6.top, ...), custom_call_target="tpu_custom_call" | custom-call | flops 4000000000 | bytes 13333333 | tf_op jit(solution)/shard_map/hidden/pallas_call | solution.py:534
  42.7 4.3 %rest.1 = (f32[1920,128]{1,0:T(8,128)S(1)}, f32[1920,128]{1,0:T(8,128)S(1)}) custom-call(bf16[256,1024]{1,0:T(8,128)(2,1)S(1)} %get-tuple-element.65.jt, bf16[1536,384]{1,0:T(8,128)(2,1)S(1)} %get-tuple-element.66.s3, f32[1792,128]{1,0:T(8,128)S(1)} %get-tuple-element.67.d_motion, f32[1792,128]{1,0:T(8,128)S(1)} %get-tuple-element.68.d_flow, ...), custom_call_target="tpu_custom_call" | custom-call | flops 3000000000 | bytes 10000000 | tf_op jit(solution)/shard_map/rest/pallas_call | solution.py:534
  47.0 2.6 %collective-permute-start.8 = (f32[1920,128]{1,0:T(8,128)S(1)}, f32[1920,128]{1,0:T(8,128)S(1)}, u32[]{:S(2)}, u32[]{:S(2)}) collective-permute-start(f32[1920,128]{1,0:T(8,128)S(1)} %get-tuple-element.75), channel_id=1, source_target_pairs={{0,4},{4,0},{8,12},{12,8},{1,5},{5,1},{9,13},{13,9},{2,6},{6,2},{1... | collective-permute-start | bytes 2949128 | tf_op jit(solution)/shard_map/ppermute | solution.py:420
  49.6 2.2 %collective-permute-done.8 = f32[1920,128]{1,0:T(8,128)S(1)} collective-permute-done((f32[1920,128]{1,0:T(8,128)S(1)}, f32[1920,128]{1,0:T(8,128)S(1)}, u32[]{:S(2)}, u32[]{:S(2)}) %collective-permute-start.8) | collective-permute-done | bytes 983072 | tf_op jit(solution)/shard_map/ppermute | solution.py:420
  52.1 1.6 %collective-permute-start.9 = (bf16[480,128]{1,0:T(8,128)(2,1)S(1)}, bf16[480,128]{1,0:T(8,128)(2,1)S(1)}, u32[]{:S(2)}, u32[]{:S(2)}) collective-permute-start(bf16[480,128]{1,0:T(8,128)(2,1)S(1)} %fusion), channel_id=1, source_target_pairs={{0,1},{1,0},{2,3},{3,2},{4,5},{5,4},{6,7},{7,6},{8,9},{9,8},{10,11... | collective-permute-start | bytes 368648 | tf_op jit(solution)/shard_map/ppermute | solution.py:420
  53.7 2.9 %collective-permute-start.11 = (bf16[480,128]{1,0:T(8,128)(2,1)S(1)}, bf16[480,128]{1,0:T(8,128)(2,1)S(1)}, u32[]{:S(2)}, u32[]{:S(2)}) collective-permute-start(bf16[480,128]{1,0:T(8,128)(2,1)S(1)} %dynamic-slice_convert_fusion), channel_id=1, source_target_pairs={{0,8},{4,12},{8,0},{12,4},{1,9},{5,13},{9,1},{13,5},{2,10},{6,14},... | collective-permute-start | bytes 368648 | tf_op jit(solution)/shard_map/ppermute | solution.py:420
  57.8 2.1 %collective-permute-done.11 = bf16[480,128]{1,0:T(8,128)(2,1)S(1)} collective-permute-done((bf16[480,128]{1,0:T(8,128)(2,1)S(1)}, bf16[480,128]{1,0:T(8,128)(2,1)S(1)}, u32[]{:S(2)}, u32[]{:S(2)}) %collective-permute-start.11) | collective-permute-done | bytes 122912 | tf_op jit(solution)/shard_map/ppermute | solution.py:420
  60.6 1.8 %collective-permute-start.10 = (f32[240,128]{1,0:T(8,128)S(1)}, f32[240,128]{1,0:T(8,128)S(1)}, u32[]{:S(2)}, u32[]{:S(2)}) collective-permute-start(f32[240,128]{1,0:T(8,128)S(1)} %constant_dynamic-slice_fusion.3), channel_id=1, source_target_pairs={{0,8},{4,12},{8,0},{12,4},{1,9},{5,13},{9,1},{13,5},{2,10},{6,14},... | collective-permute-start | bytes 368648 | tf_op jit(solution)/shard_map/ppermute | solution.py:420
  62.4 2.5 %collective-permute-done.12 = f32[240,128]{1,0:T(8,128)S(1)} collective-permute-done((f32[240,128]{1,0:T(8,128)S(1)}, f32[240,128]{1,0:T(8,128)S(1)}, u32[]{:S(2)}, u32[]{:S(2)}) %collective-permute-start.12) | collective-permute-done | bytes 122912 | tf_op jit(solution)/shard_map/ppermute | solution.py:420
  66.7 6.1 %collective-permute-done.13 = f32[240,128]{1,0:T(8,128)S(1)} collective-permute-done((f32[240,128]{1,0:T(8,128)S(1)}, f32[240,128]{1,0:T(8,128)S(1)}, u32[]{:S(2)}, u32[]{:S(2)}) %collective-permute-start.13) | collective-permute-done | bytes 122912 | tf_op jit(solution)/shard_map/ppermute | solution.py:420
  73.0 5.6 %collective-permute-done.14 = bf16[240,128]{1,0:T(8,128)(2,1)S(1)} collective-permute-done((bf16[240,128]{1,0:T(8,128)(2,1)S(1)}, bf16[240,128]{1,0:T(8,128)(2,1)S(1)}, u32[]{:S(2)}, u32[]{:S(2)}) %collective-permute-start.14) | collective-permute-done | bytes 61472 | tf_op jit(solution)/shard_map/ppermute | solution.py:420
  78.8 1.6 %collective-permute-start.17 = (bf16[240,128]{1,0:T(8,128)(2,1)S(1)}, bf16[240,128]{1,0:T(8,128)(2,1)S(1)}, u32[]{:S(2)}, u32[]{:S(2)}) collective-permute-start(bf16[240,128]{1,0:T(8,128)(2,1)S(1)} %get-tuple-element.95), channel_id=1, source_target_pairs={{0,8},{4,12},{8,0},{12,4},{1,9},{5,13},{9,1},{13,5},{2,10},{6,14},... | collective-permute-start | bytes 184328 | tf_op jit(solution)/shard_map/ppermute | solution.py:420
  80.4 3.0 %collective-permute-done.15 = bf16[240,128]{1,0:T(8,128)(2,1)S(1)} collective-permute-done((bf16[240,128]{1,0:T(8,128)(2,1)S(1)}, bf16[240,128]{1,0:T(8,128)(2,1)S(1)}, u32[]{:S(2)}, u32[]{:S(2)}) %collective-permute-start.15) | collective-permute-done | bytes 61472 | tf_op jit(solution)/shard_map/ppermute | solution.py:420
  85.4 3.1 %collective-permute-done.16 = bf16[480,128]{1,0:T(8,128)(2,1)S(1)} collective-permute-done((bf16[480,128]{1,0:T(8,128)(2,1)S(1)}, bf16[480,128]{1,0:T(8,128)(2,1)S(1)}, u32[]{:S(2)}, u32[]{:S(2)}) %collective-permute-start.16) | collective-permute-done | bytes 122912 | tf_op jit(solution)/shard_map/ppermute | solution.py:420
  90.0 1.8 %collective-permute-done.19.other = bf16[1920,128]{1,0:T(8,128)(2,1)S(1)} collective-permute-done((bf16[1920,128]{1,0:T(8,128)(2,1)S(1)}, bf16[1920,128]{1,0:T(8,128)(2,1)S(1)}, u32[]{:S(2)}, u32[]{:S(2)}) %collective-permute-start.19) | collective-permute-done | bytes 491552 | tf_op jit(solution)/shard_map/ppermute | solution.py:420
  91.7 2.0 %finish.1 = (f32[3,3,256,128]{3,2,1,0:T(8,128)}, f32[3,3,128,128]{3,2,1,0:T(8,128)}, f32[162,128]{1,0:T(8,128)}, f32[7,7,2,128]{3,2,1,0:T(2,128)}, f32[128]{0:T(...) custom-call(s32[4]{0:T(128)S(1)} %pad_add_fusion.bits, ...), custom_call_target="tpu_custom_call" | custom-call | flops 100000000 | bytes 333333 | tf_op jit(solution)/shard_map/finish/pallas_call | solution.py:534
  (57 shorter events, 15.5 us)
Async XLA Ops:
  0.6 16.5 %collective-permute-start = (bf16[1024,256]{1,0:T(8,128)(2,1)}, bf16[1024,256]{1,0:T(8,128)(2,1)S(1)}, u32[]{:S(2)}, u32[]{:S(2)}) collective-permute-start(bf16[1024,256]{1,0:T(8,128)(2,1)} %bitcast.15), channel_id=1, source_target_pairs={{0,4},{1,5},{2,6},{3,7},{4,0},{5,1},{6,2},{7,3},{8,12},{9,13},{10,... | collective-permute-start | bytes 1572872 | tf_op jit(solution)/shard_map/ppermute | solution.py:577
  2.2 10.6 %collective-permute-start.1 = (bf16[512,256]{1,0:T(8,128)(2,1)S(1)}, bf16[512,256]{1,0:T(8,128)(2,1)S(1)}, u32[]{:S(2)}, u32[]{:S(2)}) collective-permute-start(bf16[512,256]{1,0:T(8,128)(2,1)S(1)} %bitcast.20), channel_id=1, source_target_pairs={{0,5},{1,6},{2,7},{4,1},{5,2},{6,3},{8,13},{9,14},{10,15},{12,9},{... | collective-permute-start | bytes 786440 | tf_op jit(solution)/shard_map/ppermute | solution.py:575
  6.8 10.3 %collective-permute-start.2 = (bf16[512,256]{1,0:T(8,128)(2,1)S(1)}, bf16[512,256]{1,0:T(8,128)(2,1)S(1)}, u32[]{:S(2)}, u32[]{:S(2)}) collective-permute-start(bf16[512,256]{1,0:T(8,128)(2,1)S(1)} %bitcast.18), channel_id=1, source_target_pairs={{1,4},{2,5},{3,6},{5,0},{6,1},{7,2},{9,12},{10,13},{11,14},{13,8},... | collective-permute-start | bytes 786440 | tf_op jit(solution)/shard_map/ppermute | solution.py:576
  8.1 13.6 %collective-permute-start.3 = (bf16[1024,256]{1,0:T(8,128)(2,1)}, bf16[1024,256]{1,0:T(8,128)(2,1)S(1)}, u32[]{:S(2)}, u32[]{:S(2)}) collective-permute-start(bf16[1024,256]{1,0:T(8,128)(2,1)} %bitcast.16), channel_id=1, source_target_pairs={{4,8},{5,9},{6,10},{7,11},{8,4},{9,5},{10,6},{11,7},{20,24},{21,25... | collective-permute-start | bytes 1572872 | tf_op jit(solution)/shard_map/ppermute | solution.py:580
  8.8 12.8 %collective-permute-start.4 = (bf16[512,256]{1,0:T(8,128)(2,1)S(1)}, bf16[512,256]{1,0:T(8,128)(2,1)S(1)}, u32[]{:S(2)}, u32[]{:S(2)}) collective-permute-start(bf16[512,256]{1,0:T(8,128)(2,1)S(1)} %bitcast.21), channel_id=1, source_target_pairs={{4,9},{5,10},{6,11},{8,5},{9,6},{10,7},{20,25},{21,26},{22,27},{24... | collective-permute-start | bytes 786440 | tf_op jit(solution)/shard_map/ppermute | solution.py:578
  12.8 8.8 %collective-permute-start.5 = (bf16[512,256]{1,0:T(8,128)(2,1)S(1)}, bf16[512,256]{1,0:T(8,128)(2,1)S(1)}, u32[]{:S(2)}, u32[]{:S(2)}) collective-permute-start(bf16[512,256]{1,0:T(8,128)(2,1)S(1)} %bitcast.19), channel_id=1, source_target_pairs={{5,8},{6,9},{7,10},{9,4},{10,5},{11,6},{21,24},{22,25},{23,26},{25... | collective-permute-start | bytes 786440 | tf_op jit(solution)/shard_map/ppermute | solution.py:579
  17.1 0.7 copy-start
  24.8 6.0 %collective-permute-start.6 = (bf16[528,128]{1,0:T(8,128)(2,1)S(1)}, bf16[528,128]{1,0:T(8,128)(2,1)S(1)}, u32[]{:S(2)}, u32[]{:S(2)}) collective-permute-start(bf16[528,128]{1,0:T(8,128)(2,1)S(1)} %get-tuple-element.57), channel_id=1, source_target_pairs={{0,1},{1,2},{2,3},{4,5},{5,6},{6,7},{8,9},{9,10},{10,11},{12,13},{... | collective-permute-start | bytes 405512 | tf_op jit(solution)/shard_map/ppermute | solution.py:622
  28.3 6.9 %collective-permute-start.7 = (bf16[528,128]{1,0:T(8,128)(2,1)S(1)}, bf16[528,128]{1,0:T(8,128)(2,1)S(1)}, u32[]{:S(2)}, u32[]{:S(2)}) collective-permute-start(bf16[528,128]{1,0:T(8,128)(2,1)S(1)} %get-tuple-element.58), channel_id=1, source_target_pairs={{1,0},{2,1},{3,2},{5,4},{6,5},{7,6},{9,8},{10,9},{11,10},{13,12},{... | collective-permute-start | bytes 405512 | tf_op jit(solution)/shard_map/ppermute | solution.py:623
  35.2 1.1 %copy-start.1 = (f32[2]{0:T(128)S(1)}, f32[2]{0:T(128)}, u32[]{:S(2)}) copy-start(f32[2]{0:T(128)} %b_head.1) | copy-start | bytes 28
  47.0 4.8 %collective-permute-start.8 = (f32[1920,128]{1,0:T(8,128)S(1)}, f32[1920,128]{1,0:T(8,128)S(1)}, u32[]{:S(2)}, u32[]{:S(2)}) collective-permute-start(f32[1920,128]{1,0:T(8,128)S(1)} %get-tuple-element.75), channel_id=1, source_target_pairs={{0,4},{4,0},{8,12},{12,8},{1,5},{5,1},{9,13},{13,9},{2,6},{6,2},{1... | collective-permute-start | bytes 2949128 | tf_op jit(solution)/shard_map/ppermute | solution.py:420
  52.1 5.7 %collective-permute-start.9 = (bf16[480,128]{1,0:T(8,128)(2,1)S(1)}, bf16[480,128]{1,0:T(8,128)(2,1)S(1)}, u32[]{:S(2)}, u32[]{:S(2)}) collective-permute-start(bf16[480,128]{1,0:T(8,128)(2,1)S(1)} %fusion), channel_id=1, source_target_pairs={{0,1},{1,0},{2,3},{3,2},{4,5},{5,4},{6,7},{7,6},{8,9},{9,8},{10,11... | collective-permute-start | bytes 368648 | tf_op jit(solution)/shard_map/ppermute | solution.py:420
  53.7 6.2 %collective-permute-start.11 = (bf16[480,128]{1,0:T(8,128)(2,1)S(1)}, bf16[480,128]{1,0:T(8,128)(2,1)S(1)}, u32[]{:S(2)}, u32[]{:S(2)}) collective-permute-start(bf16[480,128]{1,0:T(8,128)(2,1)S(1)} %dynamic-slice_convert_fusion), channel_id=1, source_target_pairs={{0,8},{4,12},{8,0},{12,4},{1,9},{5,13},{9,1},{13,5},{2,10},{6,14},... | collective-permute-start | bytes 368648 | tf_op jit(solution)/shard_map/ppermute | solution.py:420
  60.0 4.9 %collective-permute-start.12 = (f32[240,128]{1,0:T(8,128)S(1)}, f32[240,128]{1,0:T(8,128)S(1)}, u32[]{:S(2)}, u32[]{:S(2)}) collective-permute-start(f32[240,128]{1,0:T(8,128)S(1)} %constant_dynamic-slice_fusion.2), channel_id=1, source_target_pairs={{0,1},{1,0},{2,3},{3,2},{4,5},{5,4},{6,7},{7,6},{8,9},{9,8},{10,11... | collective-permute-start | bytes 368648 | tf_op jit(solution)/shard_map/ppermute | solution.py:420
  60.6 4.9 %collective-permute-start.10 = (f32[240,128]{1,0:T(8,128)S(1)}, f32[240,128]{1,0:T(8,128)S(1)}, u32[]{:S(2)}, u32[]{:S(2)}) collective-permute-start(f32[240,128]{1,0:T(8,128)S(1)} %constant_dynamic-slice_fusion.3), channel_id=1, source_target_pairs={{0,8},{4,12},{8,0},{12,4},{1,9},{5,13},{9,1},{13,5},{2,10},{6,14},... | collective-permute-start | bytes 368648 | tf_op jit(solution)/shard_map/ppermute | solution.py:420
  65.6 7.2 %collective-permute-start.13 = (f32[240,128]{1,0:T(8,128)S(1)}, f32[240,128]{1,0:T(8,128)S(1)}, u32[]{:S(2)}, u32[]{:S(2)}) collective-permute-start(f32[240,128]{1,0:T(8,128)S(1)} %broadcast_select_fusion.2), channel_id=1, source_target_pairs={{0,2},{1,3},{2,0},{3,1},{4,6},{5,7},{6,4},{7,5},{8,10},{9,11},{10,... | collective-permute-start | bytes 368648 | tf_op jit(solution)/shard_map/ppermute | solution.py:420
  72.9 5.7 %collective-permute-start.14 = (bf16[240,128]{1,0:T(8,128)(2,1)S(1)}, bf16[240,128]{1,0:T(8,128)(2,1)S(1)}, u32[]{:S(2)}, u32[]{:S(2)}) collective-permute-start(bf16[240,128]{1,0:T(8,128)(2,1)S(1)} %fusion.1), channel_id=1, source_target_pairs={{0,2},{1,3},{2,0},{3,1},{4,6},{5,7},{6,4},{7,5},{8,10},{9,11},{10,... | collective-permute-start | bytes 184328 | tf_op jit(solution)/shard_map/ppermute | solution.py:420
  78.6 4.8 %collective-permute-start.15 = (bf16[240,128]{1,0:T(8,128)(2,1)S(1)}, bf16[240,128]{1,0:T(8,128)(2,1)S(1)}, u32[]{:S(2)}, u32[]{:S(2)}) collective-permute-start(bf16[240,128]{1,0:T(8,128)(2,1)S(1)} %get-tuple-element.94), channel_id=1, source_target_pairs={{0,1},{1,0},{2,3},{3,2},{4,5},{5,4},{6,7},{7,6},{8,9},{9,8},{10,11... | collective-permute-start | bytes 184328 | tf_op jit(solution)/shard_map/ppermute | solution.py:420
  78.8 5.9 %collective-permute-start.17 = (bf16[240,128]{1,0:T(8,128)(2,1)S(1)}, bf16[240,128]{1,0:T(8,128)(2,1)S(1)}, u32[]{:S(2)}, u32[]{:S(2)}) collective-permute-start(bf16[240,128]{1,0:T(8,128)(2,1)S(1)} %get-tuple-element.95), channel_id=1, source_target_pairs={{0,8},{4,12},{8,0},{12,4},{1,9},{5,13},{9,1},{13,5},{2,10},{6,14},... | collective-permute-start | bytes 184328 | tf_op jit(solution)/shard_map/ppermute | solution.py:420
  83.5 4.9 %collective-permute-start.16 = (bf16[480,128]{1,0:T(8,128)(2,1)S(1)}, bf16[480,128]{1,0:T(8,128)(2,1)S(1)}, u32[]{:S(2)}, u32[]{:S(2)}) collective-permute-start(bf16[480,128]{1,0:T(8,128)(2,1)S(1)} %maximum_select_fusion.4), channel_id=1, source_target_pairs={{0,8},{4,12},{8,0},{12,4},{1,9},{5,13},{9,1},{13,5},{2,10},{6,14},... | collective-permute-start | bytes 368648 | tf_op jit(solution)/shard_map/ppermute | solution.py:420
  84.7 4.9 %collective-permute-start.18 = (bf16[480,128]{1,0:T(8,128)(2,1)S(1)}, bf16[480,128]{1,0:T(8,128)(2,1)S(1)}, u32[]{:S(2)}, u32[]{:S(2)}) collective-permute-start(bf16[480,128]{1,0:T(8,128)(2,1)S(1)} %maximum_select_fusion.5), channel_id=1, source_target_pairs={{0,1},{1,0},{2,3},{3,2},{4,5},{5,4},{6,7},{7,6},{8,9},{9,8},{10,11... | collective-permute-start | bytes 368648 | tf_op jit(solution)/shard_map/ppermute | solution.py:420
  89.8 1.9 %collective-permute-start.19 = (bf16[1920,128]{1,0:T(8,128)(2,1)S(1)}, bf16[1920,128]{1,0:T(8,128)(2,1)S(1)}, u32[]{:S(2)}, u32[]{:S(2)}) collective-permute-start(bf16[1920,128]{1,0:T(8,128)(2,1)S(1)} %pad_maximum_fusion.mine), channel_id=1, source_target_pairs={{0,4},{4,0},{8,12},{12,8},{1,5},{5,1},{9,13},{13,9},{2,6},{6,2},{1... | collective-permute-start | bytes 1474568 | tf_op jit(solution)/shard_map/ppermute | solution.py:420

commit v5 on v4

--- a/solution.py
+++ b/solution.py
@@ -185,6 +185,12 @@
     return value
 
 
+def code_slope_kernel(vol, wv, bias, code, d_code, code_t):
+    pre = lax.dot_general(vol[...], wv[...], TN, preferred_element_type=F32) + bias[0:1, :]
+    d_code[...] = silu_pair(pre)[1]
+    code_t[...] = code[...].T
+
+
 def inside_frame(n_rows, ext):
     at = lax.axis_index("space") * n_rows + ext
     return jnp.logical_and(at >= 0, at < lax.axis_size("space") * n_rows)
@@ -334,12 +340,12 @@
 
 def rest_kernel(
     n_rows, n_cols, at_misc,
-    jt, s3, d_motion, d_flow, xb, vol, code, misc, wv, wcb, wjb, bias,
+    jt, s3, d_motion, d_flow, xb, vol, d_code, code_t, misc, wcb, wjb,
     keep, send,
     m3, s_flow, s_code, acc, grads,
 ):
     W = n_cols
-    C = code.shape[1]
+    C = d_code.shape[1]
     body = n_rows * W
 
     def joint_slopes(b, carry):
@@ -364,8 +370,7 @@
         at = rows(y, CODE_BLOCK, W)
         taps = jnp.concatenate([m3[rows(y + 2 - i, CODE_BLOCK, W), :] for i in range(3)], axis=1)
         sc = dot_nt(taps, wcb[...])
-        pre = lax.dot_general(vol[:, at], wv[...], TN, preferred_element_type=F32) + bias[0:1, :]
-        slope = (sc * silu_pair(pre)[1]).astype(BF)
+        slope = (sc * d_code[at, :]).astype(BF)
         s_code[at, :] = slope
         add_rows(0, slope.astype(F32))
         add_rows(1, m3[rows(y + 1, CODE_BLOCK, W), C : 2 * C].astype(F32))
@@ -379,9 +384,8 @@
         for j in range(3):
             at = (i * 3 + j) * 2 * C
             grads[at : at + 2 * C, :] = g[:, j * C : (j + 1) * C]
-    code_t = code[...].T
     for i in range(3):
-        g = dot(code_t, m3[(2 - i) * W : (2 - i) * W + body, :])
+        g = dot(code_t[...], m3[(2 - i) * W : (2 - i) * W + body, :])
         for j in range(3):
             at = AT_CODE + (i * 3 + j) * C
             grads[at : at + C, :] = g[:, j * C : (j + 1) * C]
@@ -572,12 +576,16 @@
         return t - 1 + 2 * (t % 2)
 
     first, last = flat[:halo], flat[body - halo :]
+    near_mid = lax.ppermute(flat, both, route(near, 0))
+    far_mid = lax.ppermute(flat, both, route(far, 0))
     near_top = lax.ppermute(last, both, route(near, 1))
     near_bot = lax.ppermute(first, both, route(near, -1))
-    near_mid = lax.ppermute(flat, both, route(near, 0))
-    far_top = lax.ppermute(last, both, route(far, 1))
-    far_bot = lax.ppermute(first, both, route(far, -1))
-    far_mid = lax.ppermute(flat, both, route(far, 0))
+
+    def down_column(ds):
+        return [(a, b + ds) for a, b in route(lambda t: t, 0) if 0 <= far(a // n_space) < n_tm and 0 <= b % n_space + ds < n_space]
+
+    far_top = lax.ppermute(far_mid[body - halo :], both, down_column(1))
+    far_bot = lax.ppermute(far_mid[:halo], both, down_column(-1))
 
     def shape(*dims, dtype=BF):
         return pltpu.VMEM(dims, dtype)
@@ -622,6 +630,10 @@
     top = lax.ppermute(dn, "space", [(s, s + 1) for s in range(n_space - 1)])
     bot = lax.ppermute(up, "space", [(s + 1, s) for s in range(n_space - 1)])
 
+    d_code, code_t = call(
+        code_slope_kernel, "slope", (shape(body, C, dtype=F32), shape(C, body)), [VMEM] * 4, [], 500_000_000,
+        vol, wv, bias, code,
+    )
     jf, d_flow, xb, tgt = call(
         functools.partial(flow_kernel, n_rows, n_cols), "flow",
         (
@@ -669,7 +681,7 @@
     keep, send = call(
         functools.partial(rest_kernel, n_rows, n_cols, at_misc), "rest",
         (shape(grad_rows // 2, C, dtype=F32), shape(grad_rows // 2, C, dtype=F32)),
-        [VMEM] * 12,
+        [VMEM] * 11,
         [
             pltpu.VMEM(((n_rows + 2) * W, 3 * C), BF),
             pltpu.VMEM(((n_rows + 2) * W, C), BF),
@@ -678,7 +690,7 @@
             pltpu.VMEM((grad_rows, C), F32),
         ],
         3_000_000_000,
-        jt, s3, d_motion, d_flow, xb, vol, code, misc, wv, wcb, wjb, bias,
+        jt, s3, d_motion, d_flow, xb, vol, d_code, code_t, misc, wcb, wjb,
     )
     core = ("tm", 1)
     got = trade(send, *core)

time: 94 us -> 93.3 us (level)
    ppermute x1, starting transfers between devices: 0.52 us -> 4.34 us  [local(): near_mid = lax.ppermute(flat, both, route(near, 0))]
    ppermute x12, starting transfers between devices: 14.3 us -> 11.1 us  [trade(): lax.ppermute(x, axis, [(i, i ^ bit) for i in range(lax.axis_size(axis))])]
    ppermute x1, starting transfers between devices: 4.61 us -> 3.12 us  [local(): near_top = lax.ppermute(last, both, route(near, 1))]
    pallas_call x6 -> x7, Pallas kernels: 20.7 us -> 21 us  [call(): pl.pallas_call(body, out_shape=out_shape, in_specs=in_specs, out_specs=ou...]
  transfers between devices with their start and end apart: 20 -> 20, of which waited for: 15 -> 15; matrix products, arithmetic and copies ran while one was open for 2% -> 2% of each run, Pallas kernels for 4% -> 5%
where the time goes in v5:
time: 93.3 us; the launch traced here: 93 us
  waiting for transfers between devices  41.7 us (45%)
  starting transfers between devices  26.6 us (29%)
  Pallas kernels  21 us (23%)
  between operations  1.68 us (2%)
  local copies, waits for them, and re-layouts  1.29 us (1%)
    ppermute x12, waiting for transfers between devices, trade(): lax.ppermute(x, axis, [(i, i ^ bit) for i in range(lax.axis_size(axis))])  29.4 us
    pallas_call x7, Pallas kernels, call(): pl.pallas_call(body, out_shape=out_shape, in_specs=in_specs, out_specs=ou...  21 us
    ppermute x12, starting transfers between devices, trade(): lax.ppermute(x, axis, [(i, i ^ bit) for i in range(lax.axis_size(axis))])  11.1 us
    ppermute x1, starting transfers between devices, local(): near_mid = lax.ppermute(flat, both, route(near, 0))  4.34 us
    ppermute x1, waiting for transfers between devices, local(): bot = lax.ppermute(up, 'space', [(s + 1, s) for s in range(n_space - 1)])  4.12 us
    ppermute x1, starting transfers between devices, local(): top = lax.ppermute(dn, 'space', [(s, s + 1) for s in range(n_space - 1)])  3.47 us
    ppermute x1, waiting for transfers between devices, local(): near_bot = lax.ppermute(first, both, route(near, -1))  3.4 us
    ppermute x1, starting transfers between devices, local(): near_top = lax.ppermute(last, both, route(near, 1))  3.12 us
  transfers between devices with their start and end apart: 20, of which 15 were waited for; matrix products, arithmetic and copies ran while one was open for 2% of the time, Pallas kernels for 5%

profile of v5, /device:TPU:0, one launch (start us, length us, event | category | flops | bytes accessed | tf_op | source)
XLA Modules:
  0.0 93.0 jit_solution(10006840016756981605)
XLA Ops:
  1.4 4.3 %collective-permute-start = (bf16[1024,256]{1,0:T(8,128)(2,1)}, bf16[1024,256]{1,0:T(8,128)(2,1)S(1)}, u32[]{:S(2)}, u32[]{:S(2)}) collective-permute-start(bf16[1024,256]{1,0:T(8,128)(2,1)} %bitcast.16), channel_id=1, source_target_pairs={{0,4},{1,5},{2,6},{3,7},{4,0},{5,1},{6,2},{7,3},{8,12},{9,13},{10,... | collective-permute-start | bytes 1572872 | tf_op jit(solution)/shard_map/ppermute | solution.py:579
  6.8 3.1 %collective-permute-start.1 = (bf16[512,256]{1,0:T(8,128)(2,1)S(1)}, bf16[512,256]{1,0:T(8,128)(2,1)S(1)}, u32[]{:S(2)}, u32[]{:S(2)}) collective-permute-start(bf16[512,256]{1,0:T(8,128)(2,1)S(1)} %bitcast.19), channel_id=1, source_target_pairs={{0,5},{1,6},{2,7},{4,1},{5,2},{6,3},{8,13},{9,14},{10,15},{12,9},{... | collective-permute-start | bytes 786440 | tf_op jit(solution)/shard_map/ppermute | solution.py:581
  13.3 3.1 %collective-permute-done.1.top = bf16[512,256]{1,0:T(8,128)(2,1)S(1)} collective-permute-done((bf16[512,256]{1,0:T(8,128)(2,1)S(1)}, bf16[512,256]{1,0:T(8,128)(2,1)S(1)}, u32[]{:S(2)}, u32[]{:S(2)}) %collective-permute-start.1) | collective-permute-done | bytes 262176 | tf_op jit(solution)/shard_map/ppermute | solution.py:581
  16.4 3.4 %collective-permute-done.2.bot = bf16[512,256]{1,0:T(8,128)(2,1)S(1)} collective-permute-done((bf16[512,256]{1,0:T(8,128)(2,1)S(1)}, bf16[512,256]{1,0:T(8,128)(2,1)S(1)}, u32[]{:S(2)}, u32[]{:S(2)}) %collective-permute-start.2) | collective-permute-done | bytes 262176 | tf_op jit(solution)/shard_map/ppermute | solution.py:582
  19.8 3.9 %near.1 = (bf16[96,1024]{1,0:T(8,128)(2,1)S(1)}, bf16[1024,256]{1,0:T(8,128)(2,1)S(1)}, bf16[2,8,128]{2,1,0:T(8,128)(2,1)S(1)}, s32[2,8,128]{2,1,0:T(8,128)S(1)}...) custom-call(bf16[1024,256]{1,0:T(8,128)(2,1)} %bitcast.17, ...), custom_call_target="tpu_custom_call" | custom-call | flops 4000000000 | bytes 13333333 | tf_op jit(solution)/shard_map/near/pallas_call | solution.py:538
  23.7 3.1 %code.1 = (bf16[192,1024]{1,0:T(8,128)(2,1)S(1)}, bf16[1024,128]{1,0:T(8,128)(2,1)S(1)}, bf16[528,128]{1,0:T(8,128)(2,1)S(1)}, bf16[528,128]{1,0:T(8,128)(2,1)S(1)}) custom-call(s32[1]{0:T(128)S(6)} %copy.26.order, bf16[1024,256]{1,0:T(8,128)(2,1)S(1)} %get-tuple-element.52.own, bf16[1024,256]{1,0:T(8,128)(2,1)S(1)} %collective-permute-done.3.mid, ...), custom_call_target="tpu_custom_call" | custom-call | flops 4000000000 | bytes 13333333 | tf_op jit(solution)/shard_map/code/pallas_call | solution.py:538
  26.7 3.5 %collective-permute-start.6 = (bf16[528,128]{1,0:T(8,128)(2,1)S(1)}, bf16[528,128]{1,0:T(8,128)(2,1)S(1)}, u32[]{:S(2)}, u32[]{:S(2)}) collective-permute-start(bf16[528,128]{1,0:T(8,128)(2,1)S(1)} %get-tuple-element.59), channel_id=1, source_target_pairs={{0,1},{1,2},{2,3},{4,5},{5,6},{6,7},{8,9},{9,10},{10,11},{12,13},{... | collective-permute-start | bytes 405512 | tf_op jit(solution)/shard_map/ppermute | solution.py:630
  31.9 1.8 %collective-permute-done.6.top = bf16[528,128]{1,0:T(8,128)(2,1)S(1)} collective-permute-done((bf16[528,128]{1,0:T(8,128)(2,1)S(1)}, bf16[528,128]{1,0:T(8,128)(2,1)S(1)}, u32[]{:S(2)}, u32[]{:S(2)}) %collective-permute-start.6) | collective-permute-done | bytes 135200 | tf_op jit(solution)/shard_map/ppermute | solution.py:630
  33.6 4.1 %collective-permute-done.7.bot = bf16[528,128]{1,0:T(8,128)(2,1)S(1)} collective-permute-done((bf16[528,128]{1,0:T(8,128)(2,1)S(1)}, bf16[528,128]{1,0:T(8,128)(2,1)S(1)}, u32[]{:S(2)}, u32[]{:S(2)}) %collective-permute-start.7) | collective-permute-done | bytes 135200 | tf_op jit(solution)/shard_map/ppermute | solution.py:631
  38.9 6.4 %hidden.1 = (f32[2,8,128]{2,1,0:T(8,128)}, bf16[256,1024]{1,0:T(8,128)(2,1)S(1)}, bf16[1536,384]{1,0:T(8,128)(2,1)S(1)}, f32[1792,128]{1,0:T(8,128)S(1)}, f32[8,128]{1,0:T(8,128)S(1)}) custom-call(f32[2]{0:T(128)S(1)} %copy-done.1, bf16[1024,128]{1,0:T(8,128)(2,1)S(1)} %get-tuple-element.58.code, bf16[528,128]{1,0:T(8,128)(2,1)S(1)} %collective-permute-done.6.top, ...), custom_call_target="tpu_custom_call" | custom-call | flops 4000000000 | bytes 13333333 | tf_op jit(solution)/shard_map/hidden/pallas_call | solution.py:538
  45.3 4.2 %rest.1 = (f32[1920,128]{1,0:T(8,128)S(1)}, f32[1920,128]{1,0:T(8,128)S(1)}) custom-call(bf16[256,1024]{1,0:T(8,128)(2,1)S(1)} %get-tuple-element.67.jt, bf16[1536,384]{1,0:T(8,128)(2,1)S(1)} %get-tuple-element.68.s3, f32[1792,128]{1,0:T(8,128)S(1)} %get-tuple-element.69.d_motion, f32[1792,128]{1,0:T(8,128)S(1)} %get-tuple-element.70.d_flow, ...), custom_call_target="tpu_custom_call" | custom-call | flops 3000000000 | bytes 10000000 | tf_op jit(solution)/shard_map/rest/pallas_call | solution.py:538
  49.6 2.5 %collective-permute-done.8 = f32[1920,128]{1,0:T(8,128)S(1)} collective-permute-done((f32[1920,128]{1,0:T(8,128)S(1)}, f32[1920,128]{1,0:T(8,128)S(1)}, u32[]{:S(2)}, u32[]{:S(2)}) %collective-permute-start.8) | collective-permute-done | bytes 983072 | tf_op jit(solution)/shard_map/ppermute | solution.py:424
  52.4 1.6 %collective-permute-start.9 = (bf16[480,128]{1,0:T(8,128)(2,1)S(1)}, bf16[480,128]{1,0:T(8,128)(2,1)S(1)}, u32[]{:S(2)}, u32[]{:S(2)}) collective-permute-start(bf16[480,128]{1,0:T(8,128)(2,1)S(1)} %fusion), channel_id=1, source_target_pairs={{0,1},{1,0},{2,3},{3,2},{4,5},{5,4},{6,7},{7,6},{8,9},{9,8},{10,11... | collective-permute-start | bytes 368648 | tf_op jit(solution)/shard_map/ppermute | solution.py:424
  54.1 1.9 %collective-permute-start.11 = (bf16[480,128]{1,0:T(8,128)(2,1)S(1)}, bf16[480,128]{1,0:T(8,128)(2,1)S(1)}, u32[]{:S(2)}, u32[]{:S(2)}) collective-permute-start(bf16[480,128]{1,0:T(8,128)(2,1)S(1)} %dynamic-slice_convert_fusion), channel_id=1, source_target_pairs={{0,8},{4,12},{8,0},{12,4},{1,9},{5,13},{9,1},{13,5},{2,10},{6,14},... | collective-permute-start | bytes 368648 | tf_op jit(solution)/shard_map/ppermute | solution.py:424
  55.9 1.9 %collective-permute-done.9 = bf16[480,128]{1,0:T(8,128)(2,1)S(1)} collective-permute-done((bf16[480,128]{1,0:T(8,128)(2,1)S(1)}, bf16[480,128]{1,0:T(8,128)(2,1)S(1)}, u32[]{:S(2)}, u32[]{:S(2)}) %collective-permute-start.9) | collective-permute-done | bytes 122912 | tf_op jit(solution)/shard_map/ppermute | solution.py:424
  60.0 1.8 %collective-permute-start.10 = (f32[240,128]{1,0:T(8,128)S(1)}, f32[240,128]{1,0:T(8,128)S(1)}, u32[]{:S(2)}, u32[]{:S(2)}) collective-permute-start(f32[240,128]{1,0:T(8,128)S(1)} %constant_dynamic-slice_fusion.3), channel_id=1, source_target_pairs={{0,8},{4,12},{8,0},{12,4},{1,9},{5,13},{9,1},{13,5},{2,10},{6,14},... | collective-permute-start | bytes 368648 | tf_op jit(solution)/shard_map/ppermute | solution.py:424
  61.8 2.5 %collective-permute-done.12 = f32[240,128]{1,0:T(8,128)S(1)} collective-permute-done((f32[240,128]{1,0:T(8,128)S(1)}, f32[240,128]{1,0:T(8,128)S(1)}, u32[]{:S(2)}, u32[]{:S(2)}) %collective-permute-start.12) | collective-permute-done | bytes 122912 | tf_op jit(solution)/shard_map/ppermute | solution.py:424
  66.2 6.0 %collective-permute-done.13 = f32[240,128]{1,0:T(8,128)S(1)} collective-permute-done((f32[240,128]{1,0:T(8,128)S(1)}, f32[240,128]{1,0:T(8,128)S(1)}, u32[]{:S(2)}, u32[]{:S(2)}) %collective-permute-start.13) | collective-permute-done | bytes 122912 | tf_op jit(solution)/shard_map/ppermute | solution.py:424
  72.4 5.4 %collective-permute-done.14 = bf16[240,128]{1,0:T(8,128)(2,1)S(1)} collective-permute-done((bf16[240,128]{1,0:T(8,128)(2,1)S(1)}, bf16[240,128]{1,0:T(8,128)(2,1)S(1)}, u32[]{:S(2)}, u32[]{:S(2)}) %collective-permute-start.14) | collective-permute-done | bytes 61472 | tf_op jit(solution)/shard_map/ppermute | solution.py:424
  78.0 1.8 %collective-permute-start.17 = (bf16[240,128]{1,0:T(8,128)(2,1)S(1)}, bf16[240,128]{1,0:T(8,128)(2,1)S(1)}, u32[]{:S(2)}, u32[]{:S(2)}) collective-permute-start(bf16[240,128]{1,0:T(8,128)(2,1)S(1)} %get-tuple-element.101), channel_id=1, source_target_pairs={{0,8},{4,12},{8,0},{12,4},{1,9},{5,13},{9,1},{13,5},{2,10},{6,14},... | collective-permute-start | bytes 184328 | tf_op jit(solution)/shard_map/ppermute | solution.py:424
  79.8 3.0 %collective-permute-done.15 = bf16[240,128]{1,0:T(8,128)(2,1)S(1)} collective-permute-done((bf16[240,128]{1,0:T(8,128)(2,1)S(1)}, bf16[240,128]{1,0:T(8,128)(2,1)S(1)}, u32[]{:S(2)}, u32[]{:S(2)}) %collective-permute-start.15) | collective-permute-done | bytes 61472 | tf_op jit(solution)/shard_map/ppermute | solution.py:424
  84.7 3.1 %collective-permute-done.16 = bf16[480,128]{1,0:T(8,128)(2,1)S(1)} collective-permute-done((bf16[480,128]{1,0:T(8,128)(2,1)S(1)}, bf16[480,128]{1,0:T(8,128)(2,1)S(1)}, u32[]{:S(2)}, u32[]{:S(2)}) %collective-permute-start.16) | collective-permute-done | bytes 122912 | tf_op jit(solution)/shard_map/ppermute | solution.py:424
  89.3 1.8 %collective-permute-done.19.other = bf16[1920,128]{1,0:T(8,128)(2,1)S(1)} collective-permute-done((bf16[1920,128]{1,0:T(8,128)(2,1)S(1)}, bf16[1920,128]{1,0:T(8,128)(2,1)S(1)}, u32[]{:S(2)}, u32[]{:S(2)}) %collective-permute-start.19) | collective-permute-done | bytes 491552 | tf_op jit(solution)/shard_map/ppermute | solution.py:424
  91.0 2.0 %finish.1 = (f32[3,3,256,128]{3,2,1,0:T(8,128)}, f32[3,3,128,128]{3,2,1,0:T(8,128)}, f32[162,128]{1,0:T(8,128)}, f32[7,7,2,128]{3,2,1,0:T(2,128)}, f32[128]{0:T(...) custom-call(s32[4]{0:T(128)S(1)} %pad_add_fusion.bits, ...), custom_call_target="tpu_custom_call" | custom-call | flops 100000000 | bytes 333333 | tf_op jit(solution)/shard_map/finish/pallas_call | solution.py:538
  (59 shorter events, 15.2 us)
Async XLA Ops:
  0.6 19.1 %copy-start = (bf16[128,2]{0,1:T(2,128)(2,1)S(1)}, bf16[128,2]{0,1:T(2,128)(2,1)}, u32[]{:S(2)}) copy-start(bf16[128,2]{0,1:T(2,128)(2,1)} %param.26) | copy-start | bytes 1540
  0.7 11.2 %collective-permute-start.3 = (bf16[1024,256]{1,0:T(8,128)(2,1)}, bf16[1024,256]{1,0:T(8,128)(2,1)S(1)}, u32[]{:S(2)}, u32[]{:S(2)}) collective-permute-start(bf16[1024,256]{1,0:T(8,128)(2,1)} %bitcast.15), channel_id=1, source_target_pairs={{4,8},{5,9},{6,10},{7,11},{8,4},{9,5},{10,6},{11,7},{20,24},{21,25... | collective-permute-start | bytes 1572872 | tf_op jit(solution)/shard_map/ppermute | solution.py:580
  1.4 18.4 %collective-permute-start = (bf16[1024,256]{1,0:T(8,128)(2,1)}, bf16[1024,256]{1,0:T(8,128)(2,1)S(1)}, u32[]{:S(2)}, u32[]{:S(2)}) collective-permute-start(bf16[1024,256]{1,0:T(8,128)(2,1)} %bitcast.16), channel_id=1, source_target_pairs={{0,4},{1,5},{2,6},{3,7},{4,0},{5,1},{6,2},{7,3},{8,12},{9,13},{10,... | collective-permute-start | bytes 1572872 | tf_op jit(solution)/shard_map/ppermute | solution.py:579
  6.8 9.6 %collective-permute-start.1 = (bf16[512,256]{1,0:T(8,128)(2,1)S(1)}, bf16[512,256]{1,0:T(8,128)(2,1)S(1)}, u32[]{:S(2)}, u32[]{:S(2)}) collective-permute-start(bf16[512,256]{1,0:T(8,128)(2,1)S(1)} %bitcast.19), channel_id=1, source_target_pairs={{0,5},{1,6},{2,7},{4,1},{5,2},{6,3},{8,13},{9,14},{10,15},{12,9},{... | collective-permute-start | bytes 786440 | tf_op jit(solution)/shard_map/ppermute | solution.py:581
  9.9 9.9 %collective-permute-start.2 = (bf16[512,256]{1,0:T(8,128)(2,1)S(1)}, bf16[512,256]{1,0:T(8,128)(2,1)S(1)}, u32[]{:S(2)}, u32[]{:S(2)}) collective-permute-start(bf16[512,256]{1,0:T(8,128)(2,1)S(1)} %bitcast.18), channel_id=1, source_target_pairs={{1,4},{2,5},{3,6},{5,0},{6,1},{7,2},{9,12},{10,13},{11,14},{13,8},... | collective-permute-start | bytes 786440 | tf_op jit(solution)/shard_map/ppermute | solution.py:582
  11.9 11.8 %collective-permute-start.4 = (bf16[512,256]{1,0:T(8,128)(2,1)S(1)}, bf16[512,256]{1,0:T(8,128)(2,1)S(1)}, u32[]{:S(2)}, u32[]{:S(2)}) collective-permute-start(bf16[512,256]{1,0:T(8,128)(2,1)S(1)} %get-tuple-element.97), channel_id=1, source_target_pairs={{4,5},{5,6},{6,7},{8,9},{9,10},{10,11},{20,21},{21,22},{22,23},{24... | collective-permute-start | bytes 786440 | tf_op jit(solution)/shard_map/ppermute | solution.py:587
  12.6 11.1 %collective-permute-start.5 = (bf16[512,256]{1,0:T(8,128)(2,1)S(1)}, bf16[512,256]{1,0:T(8,128)(2,1)S(1)}, u32[]{:S(2)}, u32[]{:S(2)}) collective-permute-start(bf16[512,256]{1,0:T(8,128)(2,1)S(1)} %get-tuple-element.96), channel_id=1, source_target_pairs={{5,4},{6,5},{7,6},{9,8},{10,9},{11,10},{21,20},{22,21},{23,22},{25... | collective-permute-start | bytes 786440 | tf_op jit(solution)/shard_map/ppermute | solution.py:588
  26.7 6.9 %collective-permute-start.6 = (bf16[528,128]{1,0:T(8,128)(2,1)S(1)}, bf16[528,128]{1,0:T(8,128)(2,1)S(1)}, u32[]{:S(2)}, u32[]{:S(2)}) collective-permute-start(bf16[528,128]{1,0:T(8,128)(2,1)S(1)} %get-tuple-element.59), channel_id=1, source_target_pairs={{0,1},{1,2},{2,3},{4,5},{5,6},{6,7},{8,9},{9,10},{10,11},{12,13},{... | collective-permute-start | bytes 405512 | tf_op jit(solution)/shard_map/ppermute | solution.py:630
  30.2 7.6 %collective-permute-start.7 = (bf16[528,128]{1,0:T(8,128)(2,1)S(1)}, bf16[528,128]{1,0:T(8,128)(2,1)S(1)}, u32[]{:S(2)}, u32[]{:S(2)}) collective-permute-start(bf16[528,128]{1,0:T(8,128)(2,1)S(1)} %get-tuple-element.60), channel_id=1, source_target_pairs={{1,0},{2,1},{3,2},{5,4},{6,5},{7,6},{9,8},{10,9},{11,10},{13,12},{... | collective-permute-start | bytes 405512 | tf_op jit(solution)/shard_map/ppermute | solution.py:631
  37.8 1.1 %copy-start.1 = (f32[2]{0:T(128)S(1)}, f32[2]{0:T(128)}, u32[]{:S(2)}) copy-start(f32[2]{0:T(128)} %b_head.1) | copy-start | bytes 28
  49.5 2.6 %collective-permute-start.8 = (f32[1920,128]{1,0:T(8,128)S(1)}, f32[1920,128]{1,0:T(8,128)S(1)}, u32[]{:S(2)}, u32[]{:S(2)}) collective-permute-start(f32[1920,128]{1,0:T(8,128)S(1)} %get-tuple-element.79), channel_id=1, source_target_pairs={{0,4},{4,0},{8,12},{12,8},{1,5},{5,1},{9,13},{13,9},{2,6},{6,2},{1... | collective-permute-start | bytes 2949128 | tf_op jit(solution)/shard_map/ppermute | solution.py:424
  52.4 5.4 %collective-permute-start.9 = (bf16[480,128]{1,0:T(8,128)(2,1)S(1)}, bf16[480,128]{1,0:T(8,128)(2,1)S(1)}, u32[]{:S(2)}, u32[]{:S(2)}) collective-permute-start(bf16[480,128]{1,0:T(8,128)(2,1)S(1)} %fusion), channel_id=1, source_target_pairs={{0,1},{1,0},{2,3},{3,2},{4,5},{5,4},{6,7},{7,6},{8,9},{9,8},{10,11... | collective-permute-start | bytes 368648 | tf_op jit(solution)/shard_map/ppermute | solution.py:424
  54.1 5.2 %collective-permute-start.11 = (bf16[480,128]{1,0:T(8,128)(2,1)S(1)}, bf16[480,128]{1,0:T(8,128)(2,1)S(1)}, u32[]{:S(2)}, u32[]{:S(2)}) collective-permute-start(bf16[480,128]{1,0:T(8,128)(2,1)S(1)} %dynamic-slice_convert_fusion), channel_id=1, source_target_pairs={{0,8},{4,12},{8,0},{12,4},{1,9},{5,13},{9,1},{13,5},{2,10},{6,14},... | collective-permute-start | bytes 368648 | tf_op jit(solution)/shard_map/ppermute | solution.py:424
  59.3 4.9 %collective-permute-start.12 = (f32[240,128]{1,0:T(8,128)S(1)}, f32[240,128]{1,0:T(8,128)S(1)}, u32[]{:S(2)}, u32[]{:S(2)}) collective-permute-start(f32[240,128]{1,0:T(8,128)S(1)} %constant_dynamic-slice_fusion.2), channel_id=1, source_target_pairs={{0,1},{1,0},{2,3},{3,2},{4,5},{5,4},{6,7},{7,6},{8,9},{9,8},{10,11... | collective-permute-start | bytes 368648 | tf_op jit(solution)/shard_map/ppermute | solution.py:424
  60.0 4.9 %collective-permute-start.10 = (f32[240,128]{1,0:T(8,128)S(1)}, f32[240,128]{1,0:T(8,128)S(1)}, u32[]{:S(2)}, u32[]{:S(2)}) collective-permute-start(f32[240,128]{1,0:T(8,128)S(1)} %constant_dynamic-slice_fusion.3), channel_id=1, source_target_pairs={{0,8},{4,12},{8,0},{12,4},{1,9},{5,13},{9,1},{13,5},{2,10},{6,14},... | collective-permute-start | bytes 368648 | tf_op jit(solution)/shard_map/ppermute | solution.py:424
  65.0 7.3 %collective-permute-start.13 = (f32[240,128]{1,0:T(8,128)S(1)}, f32[240,128]{1,0:T(8,128)S(1)}, u32[]{:S(2)}, u32[]{:S(2)}) collective-permute-start(f32[240,128]{1,0:T(8,128)S(1)} %broadcast_select_fusion.2), channel_id=1, source_target_pairs={{0,2},{1,3},{2,0},{3,1},{4,6},{5,7},{6,4},{7,5},{8,10},{9,11},{10,... | collective-permute-start | bytes 368648 | tf_op jit(solution)/shard_map/ppermute | solution.py:424
  72.4 5.5 %collective-permute-start.14 = (bf16[240,128]{1,0:T(8,128)(2,1)S(1)}, bf16[240,128]{1,0:T(8,128)(2,1)S(1)}, u32[]{:S(2)}, u32[]{:S(2)}) collective-permute-start(bf16[240,128]{1,0:T(8,128)(2,1)S(1)} %fusion.1), channel_id=1, source_target_pairs={{0,2},{1,3},{2,0},{3,1},{4,6},{5,7},{6,4},{7,5},{8,10},{9,11},{10,... | collective-permute-start | bytes 184328 | tf_op jit(solution)/shard_map/ppermute | solution.py:424
  77.9 4.9 %collective-permute-start.15 = (bf16[240,128]{1,0:T(8,128)(2,1)S(1)}, bf16[240,128]{1,0:T(8,128)(2,1)S(1)}, u32[]{:S(2)}, u32[]{:S(2)}) collective-permute-start(bf16[240,128]{1,0:T(8,128)(2,1)S(1)} %get-tuple-element.100), channel_id=1, source_target_pairs={{0,1},{1,0},{2,3},{3,2},{4,5},{5,4},{6,7},{7,6},{8,9},{9,8},{10,11... | collective-permute-start | bytes 184328 | tf_op jit(solution)/shard_map/ppermute | solution.py:424
  78.0 6.0 %collective-permute-start.17 = (bf16[240,128]{1,0:T(8,128)(2,1)S(1)}, bf16[240,128]{1,0:T(8,128)(2,1)S(1)}, u32[]{:S(2)}, u32[]{:S(2)}) collective-permute-start(bf16[240,128]{1,0:T(8,128)(2,1)S(1)} %get-tuple-element.101), channel_id=1, source_target_pairs={{0,8},{4,12},{8,0},{12,4},{1,9},{5,13},{9,1},{13,5},{2,10},{6,14},... | collective-permute-start | bytes 184328 | tf_op jit(solution)/shard_map/ppermute | solution.py:424
  82.8 4.9 %collective-permute-start.16 = (bf16[480,128]{1,0:T(8,128)(2,1)S(1)}, bf16[480,128]{1,0:T(8,128)(2,1)S(1)}, u32[]{:S(2)}, u32[]{:S(2)}) collective-permute-start(bf16[480,128]{1,0:T(8,128)(2,1)S(1)} %maximum_select_fusion.4), channel_id=1, source_target_pairs={{0,8},{4,12},{8,0},{12,4},{1,9},{5,13},{9,1},{13,5},{2,10},{6,14},... | collective-permute-start | bytes 368648 | tf_op jit(solution)/shard_map/ppermute | solution.py:424
  84.0 4.9 %collective-permute-start.18 = (bf16[480,128]{1,0:T(8,128)(2,1)S(1)}, bf16[480,128]{1,0:T(8,128)(2,1)S(1)}, u32[]{:S(2)}, u32[]{:S(2)}) collective-permute-start(bf16[480,128]{1,0:T(8,128)(2,1)S(1)} %maximum_select_fusion.5), channel_id=1, source_target_pairs={{0,1},{1,0},{2,3},{3,2},{4,5},{5,4},{6,7},{7,6},{8,9},{9,8},{10,11... | collective-permute-start | bytes 368648 | tf_op jit(solution)/shard_map/ppermute | solution.py:424
  89.1 1.9 %collective-permute-start.19 = (bf16[1920,128]{1,0:T(8,128)(2,1)S(1)}, bf16[1920,128]{1,0:T(8,128)(2,1)S(1)}, u32[]{:S(2)}, u32[]{:S(2)}) collective-permute-start(bf16[1920,128]{1,0:T(8,128)(2,1)S(1)} %pad_maximum_fusion.mine), channel_id=1, source_target_pairs={{0,4},{4,0},{8,12},{12,8},{1,5},{5,1},{9,13},{13,9},{2,6},{6,2},{1... | collective-permute-start | bytes 1474568 | tf_op jit(solution)/shard_map/ppermute | solution.py:424

commit v6 on v5

--- a/solution.py
+++ b/solution.py
@@ -463,6 +463,13 @@
     return jnp.where(upper_of(axis, bit) == 0, jnp.concatenate([mine, got]), jnp.concatenate([got, mine]))
 
 
+def add_terms(x, got, at, holds):
+    misc = x[at : at + MISC_ROWS] + sum(got[at + k * MISC_ROWS : at + (k + 1) * MISC_ROWS] for k in range(3))
+    fixed = jnp.concatenate([misc, jnp.zeros((2 * MISC_ROWS, misc.shape[1]), F32)])
+    x = x + got
+    return jnp.concatenate([x[:at], jnp.where(holds, fixed, x[at : at + 3 * MISC_ROWS]), x[at + 3 * MISC_ROWS :]])
+
+
 def paired_reduce(x_sum, at_misc):
     half = x_sum.shape[0]
     x, z, far_z = ("tm", 2), ("space", 1), ("space", 2)
@@ -475,18 +482,16 @@
     a_got = trade(cut(a, 1 - upper_x, n).astype(BF), *x)
     b_got = trade(three_terms(cut(b, 1 - upper_z, n), at, sends), *z)
     a = cut(a, upper_x, n) + a_got.astype(F32)
-    b = cut(b, upper_z, n)
-    got = b_got.astype(F32)
-    misc = b[at : at + MISC_ROWS] + sum(got[at + k * MISC_ROWS : at + (k + 1) * MISC_ROWS] for k in range(3))
-    fixed = jnp.concatenate([misc, jnp.zeros((2 * MISC_ROWS, misc.shape[1]), F32)])
-    b = b + got
-    b = jnp.concatenate([b[:at], jnp.where(holds, fixed, b[at : at + 3 * MISC_ROWS]), b[at + 3 * MISC_ROWS :]])
+    b = add_terms(cut(b, upper_z, n), b_got.astype(F32), at, holds)
     n = half // 8
     a_got, b_got = trade(cut(a, 1 - upper_z, n), *z), trade(cut(b, 1 - upper_x, n), *x)
     a, b = cut(a, upper_z, n) + a_got, cut(b, upper_x, n) + b_got
     is_far = upper_far == 1
-    y = jnp.where(is_far, b, a) + trade(jnp.where(is_far, a, b), *far_z)
-    y = three_terms(y, at_misc - (2 * half - n), core + upper_x + upper_z + upper_far == 4)
+    at = at_misc - (2 * half - n)
+    corner = core + upper_x + upper_z
+    sent = three_terms(jnp.where(is_far, a, b), at, corner - upper_far == 3)
+    y = add_terms(jnp.where(is_far, b, a), trade(sent, *far_z).astype(F32), at, corner + upper_far == 4)
+    y = three_terms(y, at, corner + upper_far == 4)
     got = trade(y, *far_z)
     a, b = jnp.where(is_far, got, y), jnp.where(is_far, y, got)
     a, b = ordered(a, trade(a, *z), *z), ordered(b, trade(b, *x), *x)

time: 93.3 us -> 91.7 us (0.983)
  waiting for transfers between devices: 41.7 us -> 35.1 us
  starting transfers between devices: 26.6 us -> 31.5 us
    ppermute x12, waiting for transfers between devices: 29.4 us -> 22.7 us  [trade(): lax.ppermute(x, axis, [(i, i ^ bit) for i in range(lax.axis_size(axis))])]
    ppermute x12, starting transfers between devices: 11.1 us -> 16 us  [trade(): lax.ppermute(x, axis, [(i, i ^ bit) for i in range(lax.axis_size(axis))])]
where the time goes in v6:
time: 91.7 us; the launch traced here: 91.3 us
  waiting for transfers between devices  35.1 us (38%)
  starting transfers between devices  31.5 us (34%)
  Pallas kernels  21 us (23%)
  between operations  1.71 us (2%)
  local copies, waits for them, and re-layouts  1.3 us (1%)
    ppermute x12, waiting for transfers between devices, trade(): lax.ppermute(x, axis, [(i, i ^ bit) for i in range(lax.axis_size(axis))])  22.7 us
    pallas_call x7, Pallas kernels, call(): pl.pallas_call(body, out_shape=out_shape, in_specs=in_specs, out_specs=ou...  21 us
    ppermute x12, starting transfers between devices, trade(): lax.ppermute(x, axis, [(i, i ^ bit) for i in range(lax.axis_size(axis))])  16 us
    ppermute x1, starting transfers between devices, local(): near_mid = lax.ppermute(flat, both, route(near, 0))  4.34 us
    ppermute x1, waiting for transfers between devices, local(): bot = lax.ppermute(up, 'space', [(s + 1, s) for s in range(n_space - 1)])  4.12 us
    ppermute x1, starting transfers between devices, local(): top = lax.ppermute(dn, 'space', [(s, s + 1) for s in range(n_space - 1)])  3.47 us
    ppermute x1, waiting for transfers between devices, local(): near_bot = lax.ppermute(first, both, route(near, -1))  3.4 us
    ppermute x1, starting transfers between devices, local(): near_top = lax.ppermute(last, both, route(near, 1))  3.12 us
  transfers between devices with their start and end apart: 20, of which 15 were waited for; matrix products, arithmetic and copies ran while one was open for 2% of the time, Pallas kernels for 5%

profile of v6, /device:TPU:0, one launch (start us, length us, event | category | flops | bytes accessed | tf_op | source)
XLA Modules:
  0.0 91.3 jit_solution(7708595806382733311)
XLA Ops:
  1.4 4.3 %collective-permute-start = (bf16[1024,256]{1,0:T(8,128)(2,1)}, bf16[1024,256]{1,0:T(8,128)(2,1)S(1)}, u32[]{:S(2)}, u32[]{:S(2)}) collective-permute-start(bf16[1024,256]{1,0:T(8,128)(2,1)} %bitcast.16), channel_id=1, source_target_pairs={{0,4},{1,5},{2,6},{3,7},{4,0},{5,1},{6,2},{7,3},{8,12},{9,13},{10,... | collective-permute-start | bytes 1572872 | tf_op jit(solution)/shard_map/ppermute | solution.py:584
  6.8 3.1 %collective-permute-start.1 = (bf16[512,256]{1,0:T(8,128)(2,1)S(1)}, bf16[512,256]{1,0:T(8,128)(2,1)S(1)}, u32[]{:S(2)}, u32[]{:S(2)}) collective-permute-start(bf16[512,256]{1,0:T(8,128)(2,1)S(1)} %bitcast.19), channel_id=1, source_target_pairs={{0,5},{1,6},{2,7},{4,1},{5,2},{6,3},{8,13},{9,14},{10,15},{12,9},{... | collective-permute-start | bytes 786440 | tf_op jit(solution)/shard_map/ppermute | solution.py:586
  13.3 3.1 %collective-permute-done.1.top = bf16[512,256]{1,0:T(8,128)(2,1)S(1)} collective-permute-done((bf16[512,256]{1,0:T(8,128)(2,1)S(1)}, bf16[512,256]{1,0:T(8,128)(2,1)S(1)}, u32[]{:S(2)}, u32[]{:S(2)}) %collective-permute-start.1) | collective-permute-done | bytes 262176 | tf_op jit(solution)/shard_map/ppermute | solution.py:586
  16.4 3.4 %collective-permute-done.2.bot = bf16[512,256]{1,0:T(8,128)(2,1)S(1)} collective-permute-done((bf16[512,256]{1,0:T(8,128)(2,1)S(1)}, bf16[512,256]{1,0:T(8,128)(2,1)S(1)}, u32[]{:S(2)}, u32[]{:S(2)}) %collective-permute-start.2) | collective-permute-done | bytes 262176 | tf_op jit(solution)/shard_map/ppermute | solution.py:587
  19.8 3.9 %near.1 = (bf16[96,1024]{1,0:T(8,128)(2,1)S(1)}, bf16[1024,256]{1,0:T(8,128)(2,1)S(1)}, bf16[2,8,128]{2,1,0:T(8,128)(2,1)S(1)}, s32[2,8,128]{2,1,0:T(8,128)S(1)}...) custom-call(bf16[1024,256]{1,0:T(8,128)(2,1)} %bitcast.17, ...), custom_call_target="tpu_custom_call" | custom-call | flops 4000000000 | bytes 13333333 | tf_op jit(solution)/shard_map/near/pallas_call | solution.py:543
  23.7 3.1 %code.1 = (bf16[192,1024]{1,0:T(8,128)(2,1)S(1)}, bf16[1024,128]{1,0:T(8,128)(2,1)S(1)}, bf16[528,128]{1,0:T(8,128)(2,1)S(1)}, bf16[528,128]{1,0:T(8,128)(2,1)S(1)}) custom-call(s32[1]{0:T(128)S(6)} %copy.26.order, bf16[1024,256]{1,0:T(8,128)(2,1)S(1)} %get-tuple-element.52.own, bf16[1024,256]{1,0:T(8,128)(2,1)S(1)} %collective-permute-done.3.mid, ...), custom_call_target="tpu_custom_call" | custom-call | flops 4000000000 | bytes 13333333 | tf_op jit(solution)/shard_map/code/pallas_call | solution.py:543
  26.7 3.5 %collective-permute-start.6 = (bf16[528,128]{1,0:T(8,128)(2,1)S(1)}, bf16[528,128]{1,0:T(8,128)(2,1)S(1)}, u32[]{:S(2)}, u32[]{:S(2)}) collective-permute-start(bf16[528,128]{1,0:T(8,128)(2,1)S(1)} %get-tuple-element.59), channel_id=1, source_target_pairs={{0,1},{1,2},{2,3},{4,5},{5,6},{6,7},{8,9},{9,10},{10,11},{12,13},{... | collective-permute-start | bytes 405512 | tf_op jit(solution)/shard_map/ppermute | solution.py:635
  31.9 1.8 %collective-permute-done.6.top = bf16[528,128]{1,0:T(8,128)(2,1)S(1)} collective-permute-done((bf16[528,128]{1,0:T(8,128)(2,1)S(1)}, bf16[528,128]{1,0:T(8,128)(2,1)S(1)}, u32[]{:S(2)}, u32[]{:S(2)}) %collective-permute-start.6) | collective-permute-done | bytes 135200 | tf_op jit(solution)/shard_map/ppermute | solution.py:635
  33.6 4.1 %collective-permute-done.7.bot = bf16[528,128]{1,0:T(8,128)(2,1)S(1)} collective-permute-done((bf16[528,128]{1,0:T(8,128)(2,1)S(1)}, bf16[528,128]{1,0:T(8,128)(2,1)S(1)}, u32[]{:S(2)}, u32[]{:S(2)}) %collective-permute-start.7) | collective-permute-done | bytes 135200 | tf_op jit(solution)/shard_map/ppermute | solution.py:636
  38.9 6.4 %hidden.1 = (f32[2,8,128]{2,1,0:T(8,128)}, bf16[256,1024]{1,0:T(8,128)(2,1)S(1)}, bf16[1536,384]{1,0:T(8,128)(2,1)S(1)}, f32[1792,128]{1,0:T(8,128)S(1)}, f32[8,128]{1,0:T(8,128)S(1)}) custom-call(f32[2]{0:T(128)S(1)} %copy-done.1, bf16[1024,128]{1,0:T(8,128)(2,1)S(1)} %get-tuple-element.58.code, bf16[528,128]{1,0:T(8,128)(2,1)S(1)} %collective-permute-done.6.top, ...), custom_call_target="tpu_custom_call" | custom-call | flops 4000000000 | bytes 13333333 | tf_op jit(solution)/shard_map/hidden/pallas_call | solution.py:543
  45.3 4.2 %rest.1 = (f32[1920,128]{1,0:T(8,128)S(1)}, f32[1920,128]{1,0:T(8,128)S(1)}) custom-call(bf16[256,1024]{1,0:T(8,128)(2,1)S(1)} %get-tuple-element.67.jt, bf16[1536,384]{1,0:T(8,128)(2,1)S(1)} %get-tuple-element.68.s3, f32[1792,128]{1,0:T(8,128)S(1)} %get-tuple-element.69.d_motion, f32[1792,128]{1,0:T(8,128)S(1)} %get-tuple-element.70.d_flow, ...), custom_call_target="tpu_custom_call" | custom-call | flops 3000000000 | bytes 10000000 | tf_op jit(solution)/shard_map/rest/pallas_call | solution.py:543
  49.6 2.5 %collective-permute-done.8 = f32[1920,128]{1,0:T(8,128)S(1)} collective-permute-done((f32[1920,128]{1,0:T(8,128)S(1)}, f32[1920,128]{1,0:T(8,128)S(1)}, u32[]{:S(2)}, u32[]{:S(2)}) %collective-permute-start.8) | collective-permute-done | bytes 983072 | tf_op jit(solution)/shard_map/ppermute | solution.py:424
  54.1 1.9 %collective-permute-start.11 = (bf16[480,128]{1,0:T(8,128)(2,1)S(1)}, bf16[480,128]{1,0:T(8,128)(2,1)S(1)}, u32[]{:S(2)}, u32[]{:S(2)}) collective-permute-start(bf16[480,128]{1,0:T(8,128)(2,1)S(1)} %dynamic-slice_convert_fusion), channel_id=1, source_target_pairs={{0,8},{4,12},{8,0},{12,4},{1,9},{5,13},{9,1},{13,5},{2,10},{6,14},... | collective-permute-start | bytes 368648 | tf_op jit(solution)/shard_map/ppermute | solution.py:424
  55.9 1.9 %collective-permute-done.9 = bf16[480,128]{1,0:T(8,128)(2,1)S(1)} collective-permute-done((bf16[480,128]{1,0:T(8,128)(2,1)S(1)}, bf16[480,128]{1,0:T(8,128)(2,1)S(1)}, u32[]{:S(2)}, u32[]{:S(2)}) %collective-permute-start.9) | collective-permute-done | bytes 122912 | tf_op jit(solution)/shard_map/ppermute | solution.py:424
  60.0 1.8 %collective-permute-start.10 = (f32[240,128]{1,0:T(8,128)S(1)}, f32[240,128]{1,0:T(8,128)S(1)}, u32[]{:S(2)}, u32[]{:S(2)}) collective-permute-start(f32[240,128]{1,0:T(8,128)S(1)} %constant_dynamic-slice_fusion.3), channel_id=1, source_target_pairs={{0,8},{4,12},{8,0},{12,4},{1,9},{5,13},{9,1},{13,5},{2,10},{6,14},... | collective-permute-start | bytes 368648 | tf_op jit(solution)/shard_map/ppermute | solution.py:424
  61.8 2.5 %collective-permute-done.12 = f32[240,128]{1,0:T(8,128)S(1)} collective-permute-done((f32[240,128]{1,0:T(8,128)S(1)}, f32[240,128]{1,0:T(8,128)S(1)}, u32[]{:S(2)}, u32[]{:S(2)}) %collective-permute-start.12) | collective-permute-done | bytes 122912 | tf_op jit(solution)/shard_map/ppermute | solution.py:424
  66.3 3.9 %collective-permute-done.13 = bf16[240,128]{1,0:T(8,128)(2,1)S(1)} collective-permute-done((bf16[240,128]{1,0:T(8,128)(2,1)S(1)}, bf16[240,128]{1,0:T(8,128)(2,1)S(1)}, u32[]{:S(2)}, u32[]{:S(2)}) %collective-permute-start.13) | collective-permute-done | bytes 61472 | tf_op jit(solution)/shard_map/ppermute | solution.py:424
  71.7 3.9 %collective-permute-done.14 = bf16[240,128]{1,0:T(8,128)(2,1)S(1)} collective-permute-done((bf16[240,128]{1,0:T(8,128)(2,1)S(1)}, bf16[240,128]{1,0:T(8,128)(2,1)S(1)}, u32[]{:S(2)}, u32[]{:S(2)}) %collective-permute-start.14) | collective-permute-done | bytes 61472 | tf_op jit(solution)/shard_map/ppermute | solution.py:424
  75.6 1.7 %collective-permute-start.15 = (bf16[240,128]{1,0:T(8,128)(2,1)S(1)}, bf16[240,128]{1,0:T(8,128)(2,1)S(1)}, u32[]{:S(2)}, u32[]{:S(2)}) collective-permute-start(bf16[240,128]{1,0:T(8,128)(2,1)S(1)} %get-tuple-element.102), channel_id=1, source_target_pairs={{0,1},{1,0},{2,3},{3,2},{4,5},{5,4},{6,7},{7,6},{8,9},{9,8},{10,11... | collective-permute-start | bytes 184328 | tf_op jit(solution)/shard_map/ppermute | solution.py:424
  77.3 1.7 %collective-permute-start.17 = (bf16[240,128]{1,0:T(8,128)(2,1)S(1)}, bf16[240,128]{1,0:T(8,128)(2,1)S(1)}, u32[]{:S(2)}, u32[]{:S(2)}) collective-permute-start(bf16[240,128]{1,0:T(8,128)(2,1)S(1)} %get-tuple-element.103), channel_id=1, source_target_pairs={{0,8},{4,12},{8,0},{12,4},{1,9},{5,13},{9,1},{13,5},{2,10},{6,14},... | collective-permute-start | bytes 184328 | tf_op jit(solution)/shard_map/ppermute | solution.py:424
  79.9 2.4 %collective-permute-start.16 = (bf16[480,128]{1,0:T(8,128)(2,1)S(1)}, bf16[480,128]{1,0:T(8,128)(2,1)S(1)}, u32[]{:S(2)}, u32[]{:S(2)}) collective-permute-start(bf16[480,128]{1,0:T(8,128)(2,1)S(1)} %maximum_select_fusion.4), channel_id=1, source_target_pairs={{0,8},{4,12},{8,0},{12,4},{1,9},{5,13},{9,1},{13,5},{2,10},{6,14},... | collective-permute-start | bytes 368648 | tf_op jit(solution)/shard_map/ppermute | solution.py:424
  85.3 2.0 %collective-permute-done.18 = bf16[480,128]{1,0:T(8,128)(2,1)S(1)} collective-permute-done((bf16[480,128]{1,0:T(8,128)(2,1)S(1)}, bf16[480,128]{1,0:T(8,128)(2,1)S(1)}, u32[]{:S(2)}, u32[]{:S(2)}) %collective-permute-start.18) | collective-permute-done | bytes 122912 | tf_op jit(solution)/shard_map/ppermute | solution.py:424
  87.6 1.8 %collective-permute-done.19.other = bf16[1920,128]{1,0:T(8,128)(2,1)S(1)} collective-permute-done((bf16[1920,128]{1,0:T(8,128)(2,1)S(1)}, bf16[1920,128]{1,0:T(8,128)(2,1)S(1)}, u32[]{:S(2)}, u32[]{:S(2)}) %collective-permute-start.19) | collective-permute-done | bytes 491552 | tf_op jit(solution)/shard_map/ppermute | solution.py:424
  89.4 2.0 %finish.1 = (f32[3,3,256,128]{3,2,1,0:T(8,128)}, f32[3,3,128,128]{3,2,1,0:T(8,128)}, f32[162,128]{1,0:T(8,128)}, f32[7,7,2,128]{3,2,1,0:T(2,128)}, f32[128]{0:T(...) custom-call(s32[4]{0:T(128)S(1)} %pad_add_fusion.bits, ...), custom_call_target="tpu_custom_call" | custom-call | flops 100000000 | bytes 333333 | tf_op jit(solution)/shard_map/finish/pallas_call | solution.py:543
  (66 shorter events, 18.8 us)
Async XLA Ops:
  0.6 19.1 %copy-start = (bf16[128,2]{0,1:T(2,128)(2,1)S(1)}, bf16[128,2]{0,1:T(2,128)(2,1)}, u32[]{:S(2)}) copy-start(bf16[128,2]{0,1:T(2,128)(2,1)} %param.26) | copy-start | bytes 1540
  0.7 11.2 %collective-permute-start.3 = (bf16[1024,256]{1,0:T(8,128)(2,1)}, bf16[1024,256]{1,0:T(8,128)(2,1)S(1)}, u32[]{:S(2)}, u32[]{:S(2)}) collective-permute-start(bf16[1024,256]{1,0:T(8,128)(2,1)} %bitcast.15), channel_id=1, source_target_pairs={{4,8},{5,9},{6,10},{7,11},{8,4},{9,5},{10,6},{11,7},{20,24},{21,25... | collective-permute-start | bytes 1572872 | tf_op jit(solution)/shard_map/ppermute | solution.py:585
  1.4 18.4 %collective-permute-start = (bf16[1024,256]{1,0:T(8,128)(2,1)}, bf16[1024,256]{1,0:T(8,128)(2,1)S(1)}, u32[]{:S(2)}, u32[]{:S(2)}) collective-permute-start(bf16[1024,256]{1,0:T(8,128)(2,1)} %bitcast.16), channel_id=1, source_target_pairs={{0,4},{1,5},{2,6},{3,7},{4,0},{5,1},{6,2},{7,3},{8,12},{9,13},{10,... | collective-permute-start | bytes 1572872 | tf_op jit(solution)/shard_map/ppermute | solution.py:584
  6.8 9.6 %collective-permute-start.1 = (bf16[512,256]{1,0:T(8,128)(2,1)S(1)}, bf16[512,256]{1,0:T(8,128)(2,1)S(1)}, u32[]{:S(2)}, u32[]{:S(2)}) collective-permute-start(bf16[512,256]{1,0:T(8,128)(2,1)S(1)} %bitcast.19), channel_id=1, source_target_pairs={{0,5},{1,6},{2,7},{4,1},{5,2},{6,3},{8,13},{9,14},{10,15},{12,9},{... | collective-permute-start | bytes 786440 | tf_op jit(solution)/shard_map/ppermute | solution.py:586
  9.9 9.9 %collective-permute-start.2 = (bf16[512,256]{1,0:T(8,128)(2,1)S(1)}, bf16[512,256]{1,0:T(8,128)(2,1)S(1)}, u32[]{:S(2)}, u32[]{:S(2)}) collective-permute-start(bf16[512,256]{1,0:T(8,128)(2,1)S(1)} %bitcast.18), channel_id=1, source_target_pairs={{1,4},{2,5},{3,6},{5,0},{6,1},{7,2},{9,12},{10,13},{11,14},{13,8},... | collective-permute-start | bytes 786440 | tf_op jit(solution)/shard_map/ppermute | solution.py:587
  11.9 11.8 %collective-permute-start.4 = (bf16[512,256]{1,0:T(8,128)(2,1)S(1)}, bf16[512,256]{1,0:T(8,128)(2,1)S(1)}, u32[]{:S(2)}, u32[]{:S(2)}) collective-permute-start(bf16[512,256]{1,0:T(8,128)(2,1)S(1)} %get-tuple-element.99), channel_id=1, source_target_pairs={{4,5},{5,6},{6,7},{8,9},{9,10},{10,11},{20,21},{21,22},{22,23},{24... | collective-permute-start | bytes 786440 | tf_op jit(solution)/shard_map/ppermute | solution.py:592
  12.6 11.1 %collective-permute-start.5 = (bf16[512,256]{1,0:T(8,128)(2,1)S(1)}, bf16[512,256]{1,0:T(8,128)(2,1)S(1)}, u32[]{:S(2)}, u32[]{:S(2)}) collective-permute-start(bf16[512,256]{1,0:T(8,128)(2,1)S(1)} %get-tuple-element.98), channel_id=1, source_target_pairs={{5,4},{6,5},{7,6},{9,8},{10,9},{11,10},{21,20},{22,21},{23,22},{25... | collective-permute-start | bytes 786440 | tf_op jit(solution)/shard_map/ppermute | solution.py:593
  26.7 6.9 %collective-permute-start.6 = (bf16[528,128]{1,0:T(8,128)(2,1)S(1)}, bf16[528,128]{1,0:T(8,128)(2,1)S(1)}, u32[]{:S(2)}, u32[]{:S(2)}) collective-permute-start(bf16[528,128]{1,0:T(8,128)(2,1)S(1)} %get-tuple-element.59), channel_id=1, source_target_pairs={{0,1},{1,2},{2,3},{4,5},{5,6},{6,7},{8,9},{9,10},{10,11},{12,13},{... | collective-permute-start | bytes 405512 | tf_op jit(solution)/shard_map/ppermute | solution.py:635
  30.2 7.6 %collective-permute-start.7 = (bf16[528,128]{1,0:T(8,128)(2,1)S(1)}, bf16[528,128]{1,0:T(8,128)(2,1)S(1)}, u32[]{:S(2)}, u32[]{:S(2)}) collective-permute-start(bf16[528,128]{1,0:T(8,128)(2,1)S(1)} %get-tuple-element.60), channel_id=1, source_target_pairs={{1,0},{2,1},{3,2},{5,4},{6,5},{7,6},{9,8},{10,9},{11,10},{13,12},{... | collective-permute-start | bytes 405512 | tf_op jit(solution)/shard_map/ppermute | solution.py:636
  37.8 1.1 %copy-start.1 = (f32[2]{0:T(128)S(1)}, f32[2]{0:T(128)}, u32[]{:S(2)}) copy-start(f32[2]{0:T(128)} %b_head.1) | copy-start | bytes 28
  49.5 2.6 %collective-permute-start.8 = (f32[1920,128]{1,0:T(8,128)S(1)}, f32[1920,128]{1,0:T(8,128)S(1)}, u32[]{:S(2)}, u32[]{:S(2)}) collective-permute-start(f32[1920,128]{1,0:T(8,128)S(1)} %get-tuple-element.79), channel_id=1, source_target_pairs={{0,4},{4,0},{8,12},{12,8},{1,5},{5,1},{9,13},{13,9},{2,6},{6,2},{1... | collective-permute-start | bytes 2949128 | tf_op jit(solution)/shard_map/ppermute | solution.py:424
  52.4 5.4 %collective-permute-start.9 = (bf16[480,128]{1,0:T(8,128)(2,1)S(1)}, bf16[480,128]{1,0:T(8,128)(2,1)S(1)}, u32[]{:S(2)}, u32[]{:S(2)}) collective-permute-start(bf16[480,128]{1,0:T(8,128)(2,1)S(1)} %fusion), channel_id=1, source_target_pairs={{0,1},{1,0},{2,3},{3,2},{4,5},{5,4},{6,7},{7,6},{8,9},{9,8},{10,11... | collective-permute-start | bytes 368648 | tf_op jit(solution)/shard_map/ppermute | solution.py:424
  54.1 5.2 %collective-permute-start.11 = (bf16[480,128]{1,0:T(8,128)(2,1)S(1)}, bf16[480,128]{1,0:T(8,128)(2,1)S(1)}, u32[]{:S(2)}, u32[]{:S(2)}) collective-permute-start(bf16[480,128]{1,0:T(8,128)(2,1)S(1)} %dynamic-slice_convert_fusion), channel_id=1, source_target_pairs={{0,8},{4,12},{8,0},{12,4},{1,9},{5,13},{9,1},{13,5},{2,10},{6,14},... | collective-permute-start | bytes 368648 | tf_op jit(solution)/shard_map/ppermute | solution.py:424
  59.3 4.9 %collective-permute-start.12 = (f32[240,128]{1,0:T(8,128)S(1)}, f32[240,128]{1,0:T(8,128)S(1)}, u32[]{:S(2)}, u32[]{:S(2)}) collective-permute-start(f32[240,128]{1,0:T(8,128)S(1)} %constant_dynamic-slice_fusion.2), channel_id=1, source_target_pairs={{0,1},{1,0},{2,3},{3,2},{4,5},{5,4},{6,7},{7,6},{8,9},{9,8},{10,11... | collective-permute-start | bytes 368648 | tf_op jit(solution)/shard_map/ppermute | solution.py:424
  60.0 4.9 %collective-permute-start.10 = (f32[240,128]{1,0:T(8,128)S(1)}, f32[240,128]{1,0:T(8,128)S(1)}, u32[]{:S(2)}, u32[]{:S(2)}) collective-permute-start(f32[240,128]{1,0:T(8,128)S(1)} %constant_dynamic-slice_fusion.3), channel_id=1, source_target_pairs={{0,8},{4,12},{8,0},{12,4},{1,9},{5,13},{9,1},{13,5},{2,10},{6,14},... | collective-permute-start | bytes 368648 | tf_op jit(solution)/shard_map/ppermute | solution.py:424
  65.0 5.2 %collective-permute-start.13 = (bf16[240,128]{1,0:T(8,128)(2,1)S(1)}, bf16[240,128]{1,0:T(8,128)(2,1)S(1)}, u32[]{:S(2)}, u32[]{:S(2)}) collective-permute-start(bf16[240,128]{1,0:T(8,128)(2,1)S(1)} %fusion.5), channel_id=1, source_target_pairs={{0,2},{1,3},{2,0},{3,1},{4,6},{5,7},{6,4},{7,5},{8,10},{9,11},{10,... | collective-permute-start | bytes 184328 | tf_op jit(solution)/shard_map/ppermute | solution.py:424
  70.4 5.3 %collective-permute-start.14 = (bf16[240,128]{1,0:T(8,128)(2,1)S(1)}, bf16[240,128]{1,0:T(8,128)(2,1)S(1)}, u32[]{:S(2)}, u32[]{:S(2)}) collective-permute-start(bf16[240,128]{1,0:T(8,128)(2,1)S(1)} %fusion.4), channel_id=1, source_target_pairs={{0,2},{1,3},{2,0},{3,1},{4,6},{5,7},{6,4},{7,5},{8,10},{9,11},{10,... | collective-permute-start | bytes 184328 | tf_op jit(solution)/shard_map/ppermute | solution.py:424
  75.6 4.3 %collective-permute-start.15 = (bf16[240,128]{1,0:T(8,128)(2,1)S(1)}, bf16[240,128]{1,0:T(8,128)(2,1)S(1)}, u32[]{:S(2)}, u32[]{:S(2)}) collective-permute-start(bf16[240,128]{1,0:T(8,128)(2,1)S(1)} %get-tuple-element.102), channel_id=1, source_target_pairs={{0,1},{1,0},{2,3},{3,2},{4,5},{5,4},{6,7},{7,6},{8,9},{9,8},{10,11... | collective-permute-start | bytes 184328 | tf_op jit(solution)/shard_map/ppermute | solution.py:424
  77.3 5.0 %collective-permute-start.17 = (bf16[240,128]{1,0:T(8,128)(2,1)S(1)}, bf16[240,128]{1,0:T(8,128)(2,1)S(1)}, u32[]{:S(2)}, u32[]{:S(2)}) collective-permute-start(bf16[240,128]{1,0:T(8,128)(2,1)S(1)} %get-tuple-element.103), channel_id=1, source_target_pairs={{0,8},{4,12},{8,0},{12,4},{1,9},{5,13},{9,1},{13,5},{2,10},{6,14},... | collective-permute-start | bytes 184328 | tf_op jit(solution)/shard_map/ppermute | solution.py:424
  79.9 5.2 %collective-permute-start.16 = (bf16[480,128]{1,0:T(8,128)(2,1)S(1)}, bf16[480,128]{1,0:T(8,128)(2,1)S(1)}, u32[]{:S(2)}, u32[]{:S(2)}) collective-permute-start(bf16[480,128]{1,0:T(8,128)(2,1)S(1)} %maximum_select_fusion.4), channel_id=1, source_target_pairs={{0,8},{4,12},{8,0},{12,4},{1,9},{5,13},{9,1},{13,5},{2,10},{6,14},... | collective-permute-start | bytes 368648 | tf_op jit(solution)/shard_map/ppermute | solution.py:424
  82.4 4.9 %collective-permute-start.18 = (bf16[480,128]{1,0:T(8,128)(2,1)S(1)}, bf16[480,128]{1,0:T(8,128)(2,1)S(1)}, u32[]{:S(2)}, u32[]{:S(2)}) collective-permute-start(bf16[480,128]{1,0:T(8,128)(2,1)S(1)} %maximum_select_fusion.5), channel_id=1, source_target_pairs={{0,1},{1,0},{2,3},{3,2},{4,5},{5,4},{6,7},{7,6},{8,9},{9,8},{10,11... | collective-permute-start | bytes 368648 | tf_op jit(solution)/shard_map/ppermute | solution.py:424
  87.4 1.9 %collective-permute-start.19 = (bf16[1920,128]{1,0:T(8,128)(2,1)S(1)}, bf16[1920,128]{1,0:T(8,128)(2,1)S(1)}, u32[]{:S(2)}, u32[]{:S(2)}) collective-permute-start(bf16[1920,128]{1,0:T(8,128)(2,1)S(1)} %pad_maximum_fusion.mine), channel_id=1, source_target_pairs={{0,4},{4,0},{8,12},{12,8},{1,5},{5,1},{9,13},{13,9},{2,6},{6,2},{1... | collective-permute-start | bytes 1474568 | tf_op jit(solution)/shard_map/ppermute | solution.py:424

commit v7 on v6

--- a/solution.py
+++ b/solution.py
@@ -484,10 +484,12 @@
     a = cut(a, upper_x, n) + a_got.astype(F32)
     b = add_terms(cut(b, upper_z, n), b_got.astype(F32), at, holds)
     n = half // 8
-    a_got, b_got = trade(cut(a, 1 - upper_z, n), *z), trade(cut(b, 1 - upper_x, n), *x)
-    a, b = cut(a, upper_z, n) + a_got, cut(b, upper_x, n) + b_got
+    at = at_misc - (2 * half - n)
+    a_got = trade(cut(a, 1 - upper_z, n).astype(BF), *z)
+    b_got = trade(three_terms(cut(b, 1 - upper_x, n), at, core + upper_z - upper_x == 2), *x)
+    a = cut(a, upper_z, n) + a_got.astype(F32)
+    b = add_terms(cut(b, upper_x, n), b_got.astype(F32), at, core + upper_z + upper_x == 3)
     is_far = upper_far == 1
-    at = at_misc - (2 * half - n)
     corner = core + upper_x + upper_z
     sent = three_terms(jnp.where(is_far, a, b), at, corner - upper_far == 3)
     y = add_terms(jnp.where(is_far, b, a), trade(sent, *far_z).astype(F32), at, corner + upper_far == 4)

time: 91.7 us -> 91 us (level)
  starting transfers between devices: 31.5 us -> 29 us
  waiting for transfers between devices: 35.1 us -> 36.8 us
    ppermute x12, starting transfers between devices: 16 us -> 13.4 us  [trade(): lax.ppermute(x, axis, [(i, i ^ bit) for i in range(lax.axis_size(axis))])]
    ppermute x12, waiting for transfers between devices: 22.7 us -> 24.4 us  [trade(): lax.ppermute(x, axis, [(i, i ^ bit) for i in range(lax.axis_size(axis))])]
  transfers between devices with their start and end apart: 20 -> 20, of which waited for: 15 -> 14; matrix products, arithmetic and copies ran while one was open for 2% -> 2% of each run, Pallas kernels for 5% -> 5%
where the time goes in v7:
time: 91 us; the launch traced here: 90.7 us
  waiting for transfers between devices  36.8 us (40%)
  starting transfers between devices  29 us (32%)
  Pallas kernels  21 us (23%)
  between operations  1.79 us (2%)
  local copies, waits for them, and re-layouts  1.32 us (1%)
    ppermute x12, waiting for transfers between devices, trade(): lax.ppermute(x, axis, [(i, i ^ bit) for i in range(lax.axis_size(axis))])  24.4 us
    pallas_call x7, Pallas kernels, call(): pl.pallas_call(body, out_shape=out_shape, in_specs=in_specs, out_specs=ou...  21 us
    ppermute x12, starting transfers between devices, trade(): lax.ppermute(x, axis, [(i, i ^ bit) for i in range(lax.axis_size(axis))])  13.4 us
    ppermute x1, starting transfers between devices, local(): near_mid = lax.ppermute(flat, both, route(near, 0))  4.34 us
    ppermute x1, waiting for transfers between devices, local(): bot = lax.ppermute(up, 'space', [(s + 1, s) for s in range(n_space - 1)])  4.12 us
    ppermute x1, starting transfers between devices, local(): top = lax.ppermute(dn, 'space', [(s, s + 1) for s in range(n_space - 1)])  3.47 us
    ppermute x1, waiting for transfers between devices, local(): near_bot = lax.ppermute(first, both, route(near, -1))  3.4 us
    ppermute x1, starting transfers between devices, local(): near_top = lax.ppermute(last, both, route(near, 1))  3.12 us
  transfers between devices with their start and end apart: 20, of which 14 were waited for; matrix products, arithmetic and copies ran while one was open for 2% of the time, Pallas kernels for 5%

profile of v7, /device:TPU:0, one launch (start us, length us, event | category | flops | bytes accessed | tf_op | source)
XLA Modules:
  0.0 90.7 jit_solution(10676442646110261752)
XLA Ops:
  1.4 4.3 %collective-permute-start = (bf16[1024,256]{1,0:T(8,128)(2,1)}, bf16[1024,256]{1,0:T(8,128)(2,1)S(1)}, u32[]{:S(2)}, u32[]{:S(2)}) collective-permute-start(bf16[1024,256]{1,0:T(8,128)(2,1)} %bitcast.16), channel_id=1, source_target_pairs={{0,4},{1,5},{2,6},{3,7},{4,0},{5,1},{6,2},{7,3},{8,12},{9,13},{10,... | collective-permute-start | bytes 1572872 | tf_op jit(solution)/shard_map/ppermute | solution.py:586
  6.8 3.1 %collective-permute-start.1 = (bf16[512,256]{1,0:T(8,128)(2,1)S(1)}, bf16[512,256]{1,0:T(8,128)(2,1)S(1)}, u32[]{:S(2)}, u32[]{:S(2)}) collective-permute-start(bf16[512,256]{1,0:T(8,128)(2,1)S(1)} %bitcast.19), channel_id=1, source_target_pairs={{0,5},{1,6},{2,7},{4,1},{5,2},{6,3},{8,13},{9,14},{10,15},{12,9},{... | collective-permute-start | bytes 786440 | tf_op jit(solution)/shard_map/ppermute | solution.py:588
  13.3 3.1 %collective-permute-done.1.top = bf16[512,256]{1,0:T(8,128)(2,1)S(1)} collective-permute-done((bf16[512,256]{1,0:T(8,128)(2,1)S(1)}, bf16[512,256]{1,0:T(8,128)(2,1)S(1)}, u32[]{:S(2)}, u32[]{:S(2)}) %collective-permute-start.1) | collective-permute-done | bytes 262176 | tf_op jit(solution)/shard_map/ppermute | solution.py:588
  16.4 3.4 %collective-permute-done.2.bot = bf16[512,256]{1,0:T(8,128)(2,1)S(1)} collective-permute-done((bf16[512,256]{1,0:T(8,128)(2,1)S(1)}, bf16[512,256]{1,0:T(8,128)(2,1)S(1)}, u32[]{:S(2)}, u32[]{:S(2)}) %collective-permute-start.2) | collective-permute-done | bytes 262176 | tf_op jit(solution)/shard_map/ppermute | solution.py:589
  19.8 3.9 %near.1 = (bf16[96,1024]{1,0:T(8,128)(2,1)S(1)}, bf16[1024,256]{1,0:T(8,128)(2,1)S(1)}, bf16[2,8,128]{2,1,0:T(8,128)(2,1)S(1)}, s32[2,8,128]{2,1,0:T(8,128)S(1)}...) custom-call(bf16[1024,256]{1,0:T(8,128)(2,1)} %bitcast.17, ...), custom_call_target="tpu_custom_call" | custom-call | flops 4000000000 | bytes 13333333 | tf_op jit(solution)/shard_map/near/pallas_call | solution.py:545
  23.7 3.1 %code.1 = (bf16[192,1024]{1,0:T(8,128)(2,1)S(1)}, bf16[1024,128]{1,0:T(8,128)(2,1)S(1)}, bf16[528,128]{1,0:T(8,128)(2,1)S(1)}, bf16[528,128]{1,0:T(8,128)(2,1)S(1)}) custom-call(s32[1]{0:T(128)S(6)} %copy.26.order, bf16[1024,256]{1,0:T(8,128)(2,1)S(1)} %get-tuple-element.52.own, bf16[1024,256]{1,0:T(8,128)(2,1)S(1)} %collective-permute-done.3.mid, ...), custom_call_target="tpu_custom_call" | custom-call | flops 4000000000 | bytes 13333333 | tf_op jit(solution)/shard_map/code/pallas_call | solution.py:545
  26.7 3.5 %collective-permute-start.6 = (bf16[528,128]{1,0:T(8,128)(2,1)S(1)}, bf16[528,128]{1,0:T(8,128)(2,1)S(1)}, u32[]{:S(2)}, u32[]{:S(2)}) collective-permute-start(bf16[528,128]{1,0:T(8,128)(2,1)S(1)} %get-tuple-element.59), channel_id=1, source_target_pairs={{0,1},{1,2},{2,3},{4,5},{5,6},{6,7},{8,9},{9,10},{10,11},{12,13},{... | collective-permute-start | bytes 405512 | tf_op jit(solution)/shard_map/ppermute | solution.py:637
  31.9 1.8 %collective-permute-done.6.top = bf16[528,128]{1,0:T(8,128)(2,1)S(1)} collective-permute-done((bf16[528,128]{1,0:T(8,128)(2,1)S(1)}, bf16[528,128]{1,0:T(8,128)(2,1)S(1)}, u32[]{:S(2)}, u32[]{:S(2)}) %collective-permute-start.6) | collective-permute-done | bytes 135200 | tf_op jit(solution)/shard_map/ppermute | solution.py:637
  33.6 4.1 %collective-permute-done.7.bot = bf16[528,128]{1,0:T(8,128)(2,1)S(1)} collective-permute-done((bf16[528,128]{1,0:T(8,128)(2,1)S(1)}, bf16[528,128]{1,0:T(8,128)(2,1)S(1)}, u32[]{:S(2)}, u32[]{:S(2)}) %collective-permute-start.7) | collective-permute-done | bytes 135200 | tf_op jit(solution)/shard_map/ppermute | solution.py:638
  38.9 6.4 %hidden.1 = (f32[2,8,128]{2,1,0:T(8,128)}, bf16[256,1024]{1,0:T(8,128)(2,1)S(1)}, bf16[1536,384]{1,0:T(8,128)(2,1)S(1)}, f32[1792,128]{1,0:T(8,128)S(1)}, f32[8,128]{1,0:T(8,128)S(1)}) custom-call(f32[2]{0:T(128)S(1)} %copy-done.1, bf16[1024,128]{1,0:T(8,128)(2,1)S(1)} %get-tuple-element.58.code, bf16[528,128]{1,0:T(8,128)(2,1)S(1)} %collective-permute-done.6.top, ...), custom_call_target="tpu_custom_call" | custom-call | flops 4000000000 | bytes 13333333 | tf_op jit(solution)/shard_map/hidden/pallas_call | solution.py:545
  45.3 4.2 %rest.1 = (f32[1920,128]{1,0:T(8,128)S(1)}, f32[1920,128]{1,0:T(8,128)S(1)}) custom-call(bf16[256,1024]{1,0:T(8,128)(2,1)S(1)} %get-tuple-element.67.jt, bf16[1536,384]{1,0:T(8,128)(2,1)S(1)} %get-tuple-element.68.s3, f32[1792,128]{1,0:T(8,128)S(1)} %get-tuple-element.69.d_motion, f32[1792,128]{1,0:T(8,128)S(1)} %get-tuple-element.70.d_flow, ...), custom_call_target="tpu_custom_call" | custom-call | flops 3000000000 | bytes 10000000 | tf_op jit(solution)/shard_map/rest/pallas_call | solution.py:545
  49.6 2.5 %collective-permute-done.8 = f32[1920,128]{1,0:T(8,128)S(1)} collective-permute-done((f32[1920,128]{1,0:T(8,128)S(1)}, f32[1920,128]{1,0:T(8,128)S(1)}, u32[]{:S(2)}, u32[]{:S(2)}) %collective-permute-start.8) | collective-permute-done | bytes 983072 | tf_op jit(solution)/shard_map/ppermute | solution.py:424
  54.1 1.9 %collective-permute-start.11 = (bf16[480,128]{1,0:T(8,128)(2,1)S(1)}, bf16[480,128]{1,0:T(8,128)(2,1)S(1)}, u32[]{:S(2)}, u32[]{:S(2)}) collective-permute-start(bf16[480,128]{1,0:T(8,128)(2,1)S(1)} %dynamic-slice_convert_fusion), channel_id=1, source_target_pairs={{0,8},{4,12},{8,0},{12,4},{1,9},{5,13},{9,1},{13,5},{2,10},{6,14},... | collective-permute-start | bytes 368648 | tf_op jit(solution)/shard_map/ppermute | solution.py:424
  55.9 1.9 %collective-permute-done.9 = bf16[480,128]{1,0:T(8,128)(2,1)S(1)} collective-permute-done((bf16[480,128]{1,0:T(8,128)(2,1)S(1)}, bf16[480,128]{1,0:T(8,128)(2,1)S(1)}, u32[]{:S(2)}, u32[]{:S(2)}) %collective-permute-start.9) | collective-permute-done | bytes 122912 | tf_op jit(solution)/shard_map/ppermute | solution.py:424
  58.1 1.9 %collective-permute-start.10 = (bf16[240,128]{1,0:T(8,128)(2,1)S(1)}, bf16[240,128]{1,0:T(8,128)(2,1)S(1)}, u32[]{:S(2)}, u32[]{:S(2)}) collective-permute-start(bf16[240,128]{1,0:T(8,128)(2,1)S(1)} %fusion.5), channel_id=1, source_target_pairs={{0,8},{4,12},{8,0},{12,4},{1,9},{5,13},{9,1},{13,5},{2,10},{6,14},... | collective-permute-start | bytes 184328 | tf_op jit(solution)/shard_map/ppermute | solution.py:424
  62.5 1.8 %collective-permute-done.12 = bf16[240,128]{1,0:T(8,128)(2,1)S(1)} collective-permute-done((bf16[240,128]{1,0:T(8,128)(2,1)S(1)}, bf16[240,128]{1,0:T(8,128)(2,1)S(1)}, u32[]{:S(2)}, u32[]{:S(2)}) %collective-permute-start.12) | collective-permute-done | bytes 61472 | tf_op jit(solution)/shard_map/ppermute | solution.py:424
  65.5 4.1 %collective-permute-done.13 = bf16[240,128]{1,0:T(8,128)(2,1)S(1)} collective-permute-done((bf16[240,128]{1,0:T(8,128)(2,1)S(1)}, bf16[240,128]{1,0:T(8,128)(2,1)S(1)}, u32[]{:S(2)}, u32[]{:S(2)}) %collective-permute-start.13) | collective-permute-done | bytes 61472 | tf_op jit(solution)/shard_map/ppermute | solution.py:424
  70.8 4.2 %collective-permute-done.14 = bf16[240,128]{1,0:T(8,128)(2,1)S(1)} collective-permute-done((bf16[240,128]{1,0:T(8,128)(2,1)S(1)}, bf16[240,128]{1,0:T(8,128)(2,1)S(1)}, u32[]{:S(2)}, u32[]{:S(2)}) %collective-permute-start.14) | collective-permute-done | bytes 61472 | tf_op jit(solution)/shard_map/ppermute | solution.py:424
  77.1 2.8 %collective-permute-done.15 = bf16[240,128]{1,0:T(8,128)(2,1)S(1)} collective-permute-done((bf16[240,128]{1,0:T(8,128)(2,1)S(1)}, bf16[240,128]{1,0:T(8,128)(2,1)S(1)}, u32[]{:S(2)}, u32[]{:S(2)}) %collective-permute-start.15) | collective-permute-done | bytes 61472 | tf_op jit(solution)/shard_map/ppermute | solution.py:424
  79.9 1.7 %collective-permute-start.16 = (bf16[480,128]{1,0:T(8,128)(2,1)S(1)}, bf16[480,128]{1,0:T(8,128)(2,1)S(1)}, u32[]{:S(2)}, u32[]{:S(2)}) collective-permute-start(bf16[480,128]{1,0:T(8,128)(2,1)S(1)} %maximum_select_fusion.5), channel_id=1, source_target_pairs={{0,8},{4,12},{8,0},{12,4},{1,9},{5,13},{9,1},{13,5},{2,10},{6,14},... | collective-permute-start | bytes 368648 | tf_op jit(solution)/shard_map/ppermute | solution.py:424
  82.0 2.9 %collective-permute-done.16 = bf16[480,128]{1,0:T(8,128)(2,1)S(1)} collective-permute-done((bf16[480,128]{1,0:T(8,128)(2,1)S(1)}, bf16[480,128]{1,0:T(8,128)(2,1)S(1)}, u32[]{:S(2)}, u32[]{:S(2)}) %collective-permute-start.16) | collective-permute-done | bytes 122912 | tf_op jit(solution)/shard_map/ppermute | solution.py:424
  85.0 1.7 %collective-permute-done.18 = bf16[480,128]{1,0:T(8,128)(2,1)S(1)} collective-permute-done((bf16[480,128]{1,0:T(8,128)(2,1)S(1)}, bf16[480,128]{1,0:T(8,128)(2,1)S(1)}, u32[]{:S(2)}, u32[]{:S(2)}) %collective-permute-start.18) | collective-permute-done | bytes 122912 | tf_op jit(solution)/shard_map/ppermute | solution.py:424
  86.9 1.8 %collective-permute-done.19.other = bf16[1920,128]{1,0:T(8,128)(2,1)S(1)} collective-permute-done((bf16[1920,128]{1,0:T(8,128)(2,1)S(1)}, bf16[1920,128]{1,0:T(8,128)(2,1)S(1)}, u32[]{:S(2)}, u32[]{:S(2)}) %collective-permute-start.19) | collective-permute-done | bytes 491552 | tf_op jit(solution)/shard_map/ppermute | solution.py:424
  88.7 2.0 %finish.1 = (f32[3,3,256,128]{3,2,1,0:T(8,128)}, f32[3,3,128,128]{3,2,1,0:T(8,128)}, f32[162,128]{1,0:T(8,128)}, f32[7,7,2,128]{3,2,1,0:T(2,128)}, f32[128]{0:T(...) custom-call(s32[4]{0:T(128)S(1)} %pad_add_fusion.bits, ...), custom_call_target="tpu_custom_call" | custom-call | flops 100000000 | bytes 333333 | tf_op jit(solution)/shard_map/finish/pallas_call | solution.py:545
  (75 shorter events, 16.9 us)
Async XLA Ops:
  0.6 19.1 %copy-start = (bf16[128,2]{0,1:T(2,128)(2,1)S(1)}, bf16[128,2]{0,1:T(2,128)(2,1)}, u32[]{:S(2)}) copy-start(bf16[128,2]{0,1:T(2,128)(2,1)} %param.26) | copy-start | bytes 1540
  0.7 11.2 %collective-permute-start.3 = (bf16[1024,256]{1,0:T(8,128)(2,1)}, bf16[1024,256]{1,0:T(8,128)(2,1)S(1)}, u32[]{:S(2)}, u32[]{:S(2)}) collective-permute-start(bf16[1024,256]{1,0:T(8,128)(2,1)} %bitcast.15), channel_id=1, source_target_pairs={{4,8},{5,9},{6,10},{7,11},{8,4},{9,5},{10,6},{11,7},{20,24},{21,25... | collective-permute-start | bytes 1572872 | tf_op jit(solution)/shard_map/ppermute | solution.py:587
  1.4 18.4 %collective-permute-start = (bf16[1024,256]{1,0:T(8,128)(2,1)}, bf16[1024,256]{1,0:T(8,128)(2,1)S(1)}, u32[]{:S(2)}, u32[]{:S(2)}) collective-permute-start(bf16[1024,256]{1,0:T(8,128)(2,1)} %bitcast.16), channel_id=1, source_target_pairs={{0,4},{1,5},{2,6},{3,7},{4,0},{5,1},{6,2},{7,3},{8,12},{9,13},{10,... | collective-permute-start | bytes 1572872 | tf_op jit(solution)/shard_map/ppermute | solution.py:586
  6.8 9.6 %collective-permute-start.1 = (bf16[512,256]{1,0:T(8,128)(2,1)S(1)}, bf16[512,256]{1,0:T(8,128)(2,1)S(1)}, u32[]{:S(2)}, u32[]{:S(2)}) collective-permute-start(bf16[512,256]{1,0:T(8,128)(2,1)S(1)} %bitcast.19), channel_id=1, source_target_pairs={{0,5},{1,6},{2,7},{4,1},{5,2},{6,3},{8,13},{9,14},{10,15},{12,9},{... | collective-permute-start | bytes 786440 | tf_op jit(solution)/shard_map/ppermute | solution.py:588
  9.9 9.9 %collective-permute-start.2 = (bf16[512,256]{1,0:T(8,128)(2,1)S(1)}, bf16[512,256]{1,0:T(8,128)(2,1)S(1)}, u32[]{:S(2)}, u32[]{:S(2)}) collective-permute-start(bf16[512,256]{1,0:T(8,128)(2,1)S(1)} %bitcast.18), channel_id=1, source_target_pairs={{1,4},{2,5},{3,6},{5,0},{6,1},{7,2},{9,12},{10,13},{11,14},{13,8},... | collective-permute-start | bytes 786440 | tf_op jit(solution)/shard_map/ppermute | solution.py:589
  11.9 11.8 %collective-permute-start.4 = (bf16[512,256]{1,0:T(8,128)(2,1)S(1)}, bf16[512,256]{1,0:T(8,128)(2,1)S(1)}, u32[]{:S(2)}, u32[]{:S(2)}) collective-permute-start(bf16[512,256]{1,0:T(8,128)(2,1)S(1)} %get-tuple-element.101), channel_id=1, source_target_pairs={{4,5},{5,6},{6,7},{8,9},{9,10},{10,11},{20,21},{21,22},{22,23},{24... | collective-permute-start | bytes 786440 | tf_op jit(solution)/shard_map/ppermute | solution.py:594
  12.6 11.1 %collective-permute-start.5 = (bf16[512,256]{1,0:T(8,128)(2,1)S(1)}, bf16[512,256]{1,0:T(8,128)(2,1)S(1)}, u32[]{:S(2)}, u32[]{:S(2)}) collective-permute-start(bf16[512,256]{1,0:T(8,128)(2,1)S(1)} %get-tuple-element.100), channel_id=1, source_target_pairs={{5,4},{6,5},{7,6},{9,8},{10,9},{11,10},{21,20},{22,21},{23,22},{25... | collective-permute-start | bytes 786440 | tf_op jit(solution)/shard_map/ppermute | solution.py:595
  26.7 6.9 %collective-permute-start.6 = (bf16[528,128]{1,0:T(8,128)(2,1)S(1)}, bf16[528,128]{1,0:T(8,128)(2,1)S(1)}, u32[]{:S(2)}, u32[]{:S(2)}) collective-permute-start(bf16[528,128]{1,0:T(8,128)(2,1)S(1)} %get-tuple-element.59), channel_id=1, source_target_pairs={{0,1},{1,2},{2,3},{4,5},{5,6},{6,7},{8,9},{9,10},{10,11},{12,13},{... | collective-permute-start | bytes 405512 | tf_op jit(solution)/shard_map/ppermute | solution.py:637
  30.2 7.6 %collective-permute-start.7 = (bf16[528,128]{1,0:T(8,128)(2,1)S(1)}, bf16[528,128]{1,0:T(8,128)(2,1)S(1)}, u32[]{:S(2)}, u32[]{:S(2)}) collective-permute-start(bf16[528,128]{1,0:T(8,128)(2,1)S(1)} %get-tuple-element.60), channel_id=1, source_target_pairs={{1,0},{2,1},{3,2},{5,4},{6,5},{7,6},{9,8},{10,9},{11,10},{13,12},{... | collective-permute-start | bytes 405512 | tf_op jit(solution)/shard_map/ppermute | solution.py:638
  37.8 1.1 %copy-start.1 = (f32[2]{0:T(128)S(1)}, f32[2]{0:T(128)}, u32[]{:S(2)}) copy-start(f32[2]{0:T(128)} %b_head.1) | copy-start | bytes 28
  49.5 2.6 %collective-permute-start.8 = (f32[1920,128]{1,0:T(8,128)S(1)}, f32[1920,128]{1,0:T(8,128)S(1)}, u32[]{:S(2)}, u32[]{:S(2)}) collective-permute-start(f32[1920,128]{1,0:T(8,128)S(1)} %get-tuple-element.79), channel_id=1, source_target_pairs={{0,4},{4,0},{8,12},{12,8},{1,5},{5,1},{9,13},{13,9},{2,6},{6,2},{1... | collective-permute-start | bytes 2949128 | tf_op jit(solution)/shard_map/ppermute | solution.py:424
  52.4 5.4 %collective-permute-start.9 = (bf16[480,128]{1,0:T(8,128)(2,1)S(1)}, bf16[480,128]{1,0:T(8,128)(2,1)S(1)}, u32[]{:S(2)}, u32[]{:S(2)}) collective-permute-start(bf16[480,128]{1,0:T(8,128)(2,1)S(1)} %fusion), channel_id=1, source_target_pairs={{0,1},{1,0},{2,3},{3,2},{4,5},{5,4},{6,7},{7,6},{8,9},{9,8},{10,11... | collective-permute-start | bytes 368648 | tf_op jit(solution)/shard_map/ppermute | solution.py:424
  54.1 5.9 %collective-permute-start.11 = (bf16[480,128]{1,0:T(8,128)(2,1)S(1)}, bf16[480,128]{1,0:T(8,128)(2,1)S(1)}, u32[]{:S(2)}, u32[]{:S(2)}) collective-permute-start(bf16[480,128]{1,0:T(8,128)(2,1)S(1)} %dynamic-slice_convert_fusion), channel_id=1, source_target_pairs={{0,8},{4,12},{8,0},{12,4},{1,9},{5,13},{9,1},{13,5},{2,10},{6,14},... | collective-permute-start | bytes 368648 | tf_op jit(solution)/shard_map/ppermute | solution.py:424
  58.1 4.3 %collective-permute-start.10 = (bf16[240,128]{1,0:T(8,128)(2,1)S(1)}, bf16[240,128]{1,0:T(8,128)(2,1)S(1)}, u32[]{:S(2)}, u32[]{:S(2)}) collective-permute-start(bf16[240,128]{1,0:T(8,128)(2,1)S(1)} %fusion.5), channel_id=1, source_target_pairs={{0,8},{4,12},{8,0},{12,4},{1,9},{5,13},{9,1},{13,5},{2,10},{6,14},... | collective-permute-start | bytes 184328 | tf_op jit(solution)/shard_map/ppermute | solution.py:424
  60.0 4.3 %collective-permute-start.12 = (bf16[240,128]{1,0:T(8,128)(2,1)S(1)}, bf16[240,128]{1,0:T(8,128)(2,1)S(1)}, u32[]{:S(2)}, u32[]{:S(2)}) collective-permute-start(bf16[240,128]{1,0:T(8,128)(2,1)S(1)} %dynamic-slice_convert_fusion.1), channel_id=1, source_target_pairs={{0,1},{1,0},{2,3},{3,2},{4,5},{5,4},{6,7},{7,6},{8,9},{9,8},{10,11... | collective-permute-start | bytes 184328 | tf_op jit(solution)/shard_map/ppermute | solution.py:424
  64.4 5.2 %collective-permute-start.13 = (bf16[240,128]{1,0:T(8,128)(2,1)S(1)}, bf16[240,128]{1,0:T(8,128)(2,1)S(1)}, u32[]{:S(2)}, u32[]{:S(2)}) collective-permute-start(bf16[240,128]{1,0:T(8,128)(2,1)S(1)} %fusion.6), channel_id=1, source_target_pairs={{0,2},{1,3},{2,0},{3,1},{4,6},{5,7},{6,4},{7,5},{8,10},{9,11},{10,... | collective-permute-start | bytes 184328 | tf_op jit(solution)/shard_map/ppermute | solution.py:424
  69.7 5.3 %collective-permute-start.14 = (bf16[240,128]{1,0:T(8,128)(2,1)S(1)}, bf16[240,128]{1,0:T(8,128)(2,1)S(1)}, u32[]{:S(2)}, u32[]{:S(2)}) collective-permute-start(bf16[240,128]{1,0:T(8,128)(2,1)S(1)} %fusion.4), channel_id=1, source_target_pairs={{0,2},{1,3},{2,0},{3,1},{4,6},{5,7},{6,4},{7,5},{8,10},{9,11},{10,... | collective-permute-start | bytes 184328 | tf_op jit(solution)/shard_map/ppermute | solution.py:424
  75.0 4.9 %collective-permute-start.15 = (bf16[240,128]{1,0:T(8,128)(2,1)S(1)}, bf16[240,128]{1,0:T(8,128)(2,1)S(1)}, u32[]{:S(2)}, u32[]{:S(2)}) collective-permute-start(bf16[240,128]{1,0:T(8,128)(2,1)S(1)} %get-tuple-element.104), channel_id=1, source_target_pairs={{0,1},{1,0},{2,3},{3,2},{4,5},{5,4},{6,7},{7,6},{8,9},{9,8},{10,11... | collective-permute-start | bytes 184328 | tf_op jit(solution)/shard_map/ppermute | solution.py:424
  76.6 5.1 %collective-permute-start.17 = (bf16[240,128]{1,0:T(8,128)(2,1)S(1)}, bf16[240,128]{1,0:T(8,128)(2,1)S(1)}, u32[]{:S(2)}, u32[]{:S(2)}) collective-permute-start(bf16[240,128]{1,0:T(8,128)(2,1)S(1)} %get-tuple-element.105), channel_id=1, source_target_pairs={{0,8},{4,12},{8,0},{12,4},{1,9},{5,13},{9,1},{13,5},{2,10},{6,14},... | collective-permute-start | bytes 184328 | tf_op jit(solution)/shard_map/ppermute | solution.py:424
  79.9 4.9 %collective-permute-start.16 = (bf16[480,128]{1,0:T(8,128)(2,1)S(1)}, bf16[480,128]{1,0:T(8,128)(2,1)S(1)}, u32[]{:S(2)}, u32[]{:S(2)}) collective-permute-start(bf16[480,128]{1,0:T(8,128)(2,1)S(1)} %maximum_select_fusion.5), channel_id=1, source_target_pairs={{0,8},{4,12},{8,0},{12,4},{1,9},{5,13},{9,1},{13,5},{2,10},{6,14},... | collective-permute-start | bytes 368648 | tf_op jit(solution)/shard_map/ppermute | solution.py:424
  81.7 4.9 %collective-permute-start.18 = (bf16[480,128]{1,0:T(8,128)(2,1)S(1)}, bf16[480,128]{1,0:T(8,128)(2,1)S(1)}, u32[]{:S(2)}, u32[]{:S(2)}) collective-permute-start(bf16[480,128]{1,0:T(8,128)(2,1)S(1)} %maximum_select_fusion.6), channel_id=1, source_target_pairs={{0,1},{1,0},{2,3},{3,2},{4,5},{5,4},{6,7},{7,6},{8,9},{9,8},{10,11... | collective-permute-start | bytes 368648 | tf_op jit(solution)/shard_map/ppermute | solution.py:424
  86.8 1.9 %collective-permute-start.19 = (bf16[1920,128]{1,0:T(8,128)(2,1)S(1)}, bf16[1920,128]{1,0:T(8,128)(2,1)S(1)}, u32[]{:S(2)}, u32[]{:S(2)}) collective-permute-start(bf16[1920,128]{1,0:T(8,128)(2,1)S(1)} %pad_maximum_fusion.mine), channel_id=1, source_target_pairs={{0,4},{4,0},{8,12},{12,8},{1,5},{5,1},{9,13},{13,9},{2,6},{6,2},{1... | collective-permute-start | bytes 1474568 | tf_op jit(solution)/shard_map/ppermute | solution.py:424
